TPU v7x, 32 devices: a whole 2x2x4 slice. The times are simulated.
32 devices in a mesh: groups: 2 (over x), ctx: 16 (over z, y, core).
Axes of the slice: x: 2, y: 2, z: 4, core: 2. Of those that a mesh axis runs over, the one named last changes fastest.
Arguments:
- projected: bfloat16 [3, 16384, 4096], P(None, ('groups', 'ctx')), parts along dimension 1, may hold values from -6 to 6
- conv_weight: float32 [3, 4, 4096], replicated, may hold values from -3 to 3
- level_codes: int32 [14, 32, 16384], P(None, None, ('groups', 'ctx')), parts along dimension 2, may hold values from 1 to 16
- out_gain: float32 [4096], replicated, may hold values from 0.25 to 1.75
Outputs:
- mixed: bfloat16 [16384, 4096], P(('groups', 'ctx')), parts along dimension 0
There are 2 independent parts, one for each index of `groups`. A program takes and returns all parts, laid end to end along the dimension named above; an argument that names none is the same for every part. Nothing has to cross between parts.
Inputs may be any that keep to these rules, and one draw needn't show every extreme that they name: `level_codes`: numerators of the level coefficients, which are the values divided by 8.
All inputs are finite; a program needn't handle non-finite values.
Results may differ from a plain program's by a relative error of at most 0.007.
Values may be sent and summed in bfloat16 or wider, within the bound.
A program may use at most 192 MiB of HBM per device.

v0:
```python
import jax
import jax.numpy as jnp
from jax import lax
from jax.sharding import PartitionSpec as P


def shifted(value, axis, steps):
    count = lax.axis_size(axis)
    leading, last = (max(0, -steps), min(count, count - steps))
    return lax.ppermute(value, axis, [(source, source + steps) for source in range(leading, last)])


def intra_levels(length, bit_count):
    position = lax.iota(jnp.int32, length)
    differ = jnp.bitwise_xor(position[:, None], position[None, :])
    level = jnp.zeros((length, length), jnp.int32)
    for exponent in range(bit_count):
        level = level + (differ >= 2**exponent).astype(jnp.int32)
    causal = position[None, :] <= position[:, None]
    return jnp.stack(
        [(causal & (level == number)).astype(jnp.float32) for number in range(bit_count + 1)]
    )


def on_device(projected, conv_weight, level_codes, out_gain):
    tap_count = conv_weight.shape[1]
    row_count = projected.shape[1]
    model_width = projected.shape[2]
    head_count = level_codes.shape[1]
    head_dim = model_width // head_count
    tok_bits = row_count.bit_length() - 1
    ctx_count = lax.axis_size("ctx")
    ctx_bits = ctx_count.bit_length() - 1
    highest = lax.Precision.HIGHEST
    rim_rows = shifted(projected[:, row_count - tap_count + 1 :, :], "ctx", 1)
    padded = jnp.concatenate([rim_rows, projected], 1).astype(jnp.float32)
    running = jnp.zeros((3, row_count, model_width), jnp.float32)
    for offset in range(tap_count):
        running = (
            running + conv_weight[:, offset, None, :] * padded[:, offset : offset + row_count, :]
        )
    mixed_in = running.astype(jnp.bfloat16)
    query_rows = mixed_in[0].reshape(row_count, head_count, head_dim)
    key_rows = mixed_in[1].reshape(row_count, head_count, head_dim)
    value_rows = mixed_in[2].reshape(row_count, head_count, head_dim)
    level_weight = level_codes.astype(jnp.float32) / 8.0
    states = jnp.einsum("shd,she->hde", key_rows, value_rows, preferred_element_type=jnp.float32)
    outgoing = states.reshape(1, head_count, head_dim, head_dim)
    spread = lax.all_to_all(outgoing, "ctx", split_axis=1, concat_axis=0, tiled=True)
    span_ids = lax.iota(jnp.int32, ctx_count)
    differ = jnp.bitwise_xor(span_ids[:, None], span_ids[None, :])
    earlier = span_ids[None, :] < span_ids[:, None]
    bucket_masks = jnp.stack(
        [
            (earlier & (differ >= 2**bit_index) & (differ < 2 ** (bit_index + 1))).astype(
                jnp.float32
            )
            for bit_index in range(ctx_bits)
        ]
    )
    buckets = jnp.einsum("bcs,spde->bcpde", bucket_masks, spread, precision=highest).astype(
        jnp.bfloat16
    )
    returned = lax.all_to_all(buckets, "ctx", split_axis=1, concat_axis=2, tiled=True)
    fenwick_bf = returned[:, 0]
    onehot = intra_levels(row_count, tok_bits)
    group_size = min(8, head_count)

    def group_block(group_index):
        head_start = group_index * group_size
        query_part = lax.dynamic_slice_in_dim(query_rows, head_start, group_size, 1)
        key_part = lax.dynamic_slice_in_dim(key_rows, head_start, group_size, 1)
        value_part = lax.dynamic_slice_in_dim(value_rows, head_start, group_size, 1)
        level_part = lax.dynamic_slice_in_dim(level_weight, head_start, group_size, 1)[
            : tok_bits + 1
        ]
        scores = jnp.einsum(
            "thd,shd->hts", query_part, key_part, preferred_element_type=jnp.float32
        )
        weight = jnp.einsum("lts,lht->hts", onehot, level_part, precision=highest)
        weights = (scores * weight).astype(jnp.bfloat16)
        return jnp.einsum("hts,shd->thd", weights, value_part, preferred_element_type=jnp.float32)

    blocks = lax.map(group_block, jnp.arange(head_count // group_size, dtype=jnp.int32))
    inside = blocks.transpose(1, 0, 2, 3).reshape(row_count, head_count, head_dim)
    across = jnp.zeros((row_count, head_count, head_dim), jnp.float32)
    for bit_index in range(ctx_bits):
        product = jnp.einsum(
            "thd,hde->the", query_rows, fenwick_bf[bit_index], preferred_element_type=jnp.float32
        )
        across = across + level_weight[tok_bits + 1 + bit_index].T[:, :, None] * product
    combined = inside + across
    inverse = lax.rsqrt(jnp.mean(combined * combined, -1, keepdims=True) + 1e-06)
    normed = combined * inverse * out_gain.reshape(head_count, head_dim)
    return normed.astype(jnp.bfloat16).reshape(row_count, model_width)


def solution(mesh):
    placed = (P(None, ("groups", "ctx"), None), P(), P(None, None, ("groups", "ctx")), P())
    return jax.shard_map(
        on_device, mesh=mesh, in_specs=placed, out_specs=P(("groups", "ctx"), None), check_vma=False
    )
```

profile of v0, /device:TPU:15, one launch (start us, length us, event | category | flops | bytes accessed | tf_op | source)
XLA Modules:
  0.0 414.6 jit_solution(12851691643838151552)
XLA Ops:
  4.7 11.9 %compare_and_fusion = (pred[1,512,512]{2,0,1:T(4,128)(4,1)}, pred[1,512,512]{2,0,1:T(4,128)(4,1)}) fusion(), kind=kLoop, calls=%fused_computation.29 | loop fusion | flops 8388608 | bytes 524288 | tf_op jit(solution)/shard_map/and | solution.py:21
  18.3 16.6 %copy.58 = bf16[3,512,4096]{1,2,0:T(8,128)(2,1)} copy(bf16[3,512,4096]{2,1,0:T(8,128)(2,1)} %param.6) | data formatting | bytes 25165824 | tf_op args[0]
  36.5 16.9 %maximum_convert_fusion = f32[3,515,4096]{1,2,0:T(8,128)} fusion(bf16[3,512,4096]{1,2,0:T(8,128)(2,1)} %copy.58, bf16[3,3,4096]{1,2,0:T(8,128)(2,1)S(1)} %copy.57), kind=kLoop, calls=%fused_computation.18 | loop fusion | flops 25313280 | bytes 37969920 | tf_op jit(solution)/shard_map/convert_element_type | solution.py:36
  53.5 58.4 %fusion.15 = bf16[3,512,4096]{1,2,0:T(8,128)(2,1)} fusion(f32[3,515,4096]{1,2,0:T(8,128)} %maximum_convert_fusion, f32[3,4096]{1,0:T(4,128)S(1)} %get-tuple-element.113, f32[3,4096]{1,0:T(4,128)S(1)} %get-tuple-element.114, f32[3,4096]{1,0:T(4,128)S(1)} %get-tuple-element.115, f32[3,4096]{1,0:T(4,128)S(1)} %get-tuple-element.116), kind=kLoop, calls=%fused_computation.12 | loop fusion | flops 50331648 | bytes 113442816 | tf_op jit(solution)/shard_map/convert_element_type | solution.py:42
  111.9 6.9 %fusion.54 = (bf16[1,512,4096]{1,2,0:T(8,128)(2,1)S(1)}, bf16[1,512,4096]{1,2,0:T(8,128)(2,1)}, bf16[1,512,4096]{1,2,0:T(8,128)(2,1)S(1)}) fusion(bf16[3,512,4096]{1,2,0:T(8,128)(2,1)} %fusion.15), kind=kLoop, calls=%fused_computation.97 | loop fusion | bytes 25165824 | tf_op jit(solution)/shard_map/slice | solution.py:44
  130.1 11.8 %compare_and_fusion.2 = (pred[1,512,512]{2,0,1:T(4,128)(4,1)S(1)}, pred[1,512,512]{2,0,1:T(4,128)(4,1)}) fusion(), kind=kLoop, calls=%fused_computation.31 | loop fusion | flops 8388608 | bytes 524288 | tf_op jit(solution)/shard_map/and | solution.py:21
  141.9 11.9 %compare_and_fusion.4 = (pred[1,512,512]{2,0,1:T(4,128)(4,1)}, pred[1,512,512]{2,0,1:T(4,128)(4,1)}) fusion(), kind=kLoop, calls=%fused_computation.33 | loop fusion | flops 8388608 | bytes 524288 | tf_op jit(solution)/shard_map/and | solution.py:21
  153.8 11.9 %compare_and_fusion.6 = (pred[1,512,512]{2,0,1:T(4,128)(4,1)}, pred[1,512,512]{2,0,1:T(4,128)(4,1)}) fusion(), kind=kLoop, calls=%fused_computation.35 | loop fusion | flops 8388608 | bytes 524288 | tf_op jit(solution)/shard_map/and | solution.py:21
  165.6 11.8 %all-to-all-done = f32[1,32,128,128]{3,2,0,1:T(8,128)S(1)} async-done(((f32[1,32,128,128]{3,2,0,1:T(8,128)}), f32[1,32,128,128]{3,2,0,1:T(8,128)S(1)}, u32[]{:S(2)}, u32[]{:S(2)}) %all-to-all-start) | async-done | bytes 2097184 | tf_op jit(solution)/shard_map/all_to_all | solution.py:49
  184.3 15.2 %all-to-all-start.1 = ((bf16[4,16,2,128,128]{4,3,2,0,1:T(8,128)(2,1)}), bf16[4,16,2,128,128]{4,3,2,0,1:T(8,128)(2,1)}, u32[]{:S(2)}, u32[]{:S(2)}) async-start(bf16[4,16,2,128,128]{4,3,2,0,1:T(8,128)(2,1)} %copy.65), calls=%async_computation.1 | async-start | bytes 8388608 | tf_op jit(solution)/shard_map/all_to_all | solution.py:64
  199.5 11.9 %compare_and_fusion.8 = (pred[1,512,512]{2,0,1:T(4,128)(4,1)}, pred[1,512,512]{2,0,1:T(4,128)(4,1)}) fusion(), kind=kLoop, calls=%fused_computation.37 | loop fusion | flops 8388608 | bytes 524288 | tf_op jit(solution)/shard_map/and | solution.py:21
  211.4 33.7 %stack.10 = pred[10,512,512]{2,0,1:T(8,128)(4,1)} concatenate(pred[1,512,512]{2,0,1:T(4,128)(4,1)} %get-tuple-element.130, pred[1,512,512]{2,0,1:T(4,128)(4,1)} %get-tuple-element.129, pred[1,512,512]{2,0,1:T(4,128)(4,1)} %get-tuple-element.128, pred[1,512,512]{2,0,1:T(4,128)(4,1)} %get-tuple-element.127, pred[1,512,512]{2,0,1:T(4,128)(4,1)} %get-tuple-element.126, ...), dimensions={0} | concatenate | bytes 5242880 | tf_op jit(solution)/shard_map/stack | solution.py:20
  245.1 10.4 %stack.11 = f32[10,512,512]{2,0,1:T(8,128)} convert(pred[10,512,512]{2,0,1:T(8,128)(4,1)} %stack.10) | non-fusion elementwise | flops 2621440 | bytes 13107200 | tf_op jit(solution)/shard_map/stack | solution.py:20
  255.6 112.7 %while.10 = (s32[]{:T(128)}, f32[4,512,8,128]{1,3,2,0:T(8,128)}, s32[4]{0:T(128)S(1)}, bf16[512,32,128]{0,2,1:T(8,128)(2,1)}, bf16[512,32,128]{0,2,1:T(8,128)(2,...) while((s32[]{:T(128)}, f32[4,512,8,128]{1,3,2,0:T(8,128)}, ...), condition=%wide.region_1.2_spmd, body=%wide.region_0.1_spmd.sunk | while | flops 1329594368 | bytes 33327284 | solution.py:84
  257.7 13.8 %fusion.86 = f32[512,8,512]{2,1,0:T(8,128)} fusion(f32[10,8,512]{0,1,2:T(8,128)S(1)} %copy.116, f32[10,512,512]{2,0,1:T(8,128)} %get-tuple-element.211), kind=kOutput, calls=%fused_computation.100.clone.1 | convolution fusion | flops 251658240 | bytes 19038208 | tf_op jit(solution)/shard_map/while/body/eval_jaxpr/lts,lht->hts/dot_general | solution.py:80
  271.5 12.2 %bitcast_dynamic-update-slice_fusion.2 = f32[4,512,8,128]{1,3,2,0:T(8,128)} fusion(f32[4,512,8,128]{1,3,2,0:T(8,128)} %get-tuple-element.193, s32[]{:T(128)} %get-tuple-element.192, f32[512,8,512]{2,1,0:T(8,128)} %fusion.86, bf16[512,32,128]{0,2,1:T(8,128)(2,1)} %get-tuple-element.209, s32[]{:T(128)S(6)} %select_n.3, ...), kind=kOutput, calls=%fused_computation.4.clone.1 | convolution fusion | flops 1077936128 | bytes 13633536 | tf_op jit(solution)/shard_map/while/body/eval_jaxpr/hts,shd->thd/dot_general | solution.py:82
  285.8 13.8 %fusion.86 = f32[512,8,512]{2,1,0:T(8,128)} fusion(f32[10,8,512]{0,1,2:T(8,128)S(1)} %copy.116, f32[10,512,512]{2,0,1:T(8,128)} %get-tuple-element.211), kind=kOutput, calls=%fused_computation.100.clone.1 | convolution fusion | flops 251658240 | bytes 19038208 | tf_op jit(solution)/shard_map/while/body/eval_jaxpr/lts,lht->hts/dot_general | solution.py:80
  299.6 12.2 %bitcast_dynamic-update-slice_fusion.2 = f32[4,512,8,128]{1,3,2,0:T(8,128)} fusion(f32[4,512,8,128]{1,3,2,0:T(8,128)} %get-tuple-element.193, s32[]{:T(128)} %get-tuple-element.192, f32[512,8,512]{2,1,0:T(8,128)} %fusion.86, bf16[512,32,128]{0,2,1:T(8,128)(2,1)} %get-tuple-element.209, s32[]{:T(128)S(6)} %select_n.3, ...), kind=kOutput, calls=%fused_computation.4.clone.1 | convolution fusion | flops 1077936128 | bytes 13633536 | tf_op jit(solution)/shard_map/while/body/eval_jaxpr/hts,shd->thd/dot_general | solution.py:82
  313.9 13.8 %fusion.86 = f32[512,8,512]{2,1,0:T(8,128)} fusion(f32[10,8,512]{0,1,2:T(8,128)S(1)} %copy.116, f32[10,512,512]{2,0,1:T(8,128)} %get-tuple-element.211), kind=kOutput, calls=%fused_computation.100.clone.1 | convolution fusion | flops 251658240 | bytes 19038208 | tf_op jit(solution)/shard_map/while/body/eval_jaxpr/lts,lht->hts/dot_general | solution.py:80
  327.7 12.2 %bitcast_dynamic-update-slice_fusion.2 = f32[4,512,8,128]{1,3,2,0:T(8,128)} fusion(f32[4,512,8,128]{1,3,2,0:T(8,128)} %get-tuple-element.193, s32[]{:T(128)} %get-tuple-element.192, f32[512,8,512]{2,1,0:T(8,128)} %fusion.86, bf16[512,32,128]{0,2,1:T(8,128)(2,1)} %get-tuple-element.209, s32[]{:T(128)S(6)} %select_n.3, ...), kind=kOutput, calls=%fused_computation.4.clone.1 | convolution fusion | flops 1077936128 | bytes 13633536 | tf_op jit(solution)/shard_map/while/body/eval_jaxpr/hts,shd->thd/dot_general | solution.py:82
  342.0 13.8 %fusion.86 = f32[512,8,512]{2,1,0:T(8,128)} fusion(f32[10,8,512]{0,1,2:T(8,128)S(1)} %copy.116, f32[10,512,512]{2,0,1:T(8,128)} %get-tuple-element.211), kind=kOutput, calls=%fused_computation.100.clone.1 | convolution fusion | flops 251658240 | bytes 19038208 | tf_op jit(solution)/shard_map/while/body/eval_jaxpr/lts,lht->hts/dot_general | solution.py:80
  355.8 12.3 %bitcast_dynamic-update-slice_fusion.2 = f32[4,512,8,128]{1,3,2,0:T(8,128)} fusion(f32[4,512,8,128]{1,3,2,0:T(8,128)} %get-tuple-element.193, s32[]{:T(128)} %get-tuple-element.192, f32[512,8,512]{2,1,0:T(8,128)} %fusion.86, bf16[512,32,128]{0,2,1:T(8,128)(2,1)} %get-tuple-element.209, s32[]{:T(128)S(6)} %select_n.3, ...), kind=kOutput, calls=%fused_computation.4.clone.1 | convolution fusion | flops 1077936128 | bytes 13633536 | tf_op jit(solution)/shard_map/while/body/eval_jaxpr/hts,shd->thd/dot_general | solution.py:82
  385.4 17.4 %multiply_reduce_fusion = (f32[512,32]{0,1:T(8,128)S(1)}, f32[512,32,128]{0,2,1:T(8,128)}) fusion(bf16[32,128,128]{2,1,0:T(8,128)(2,1)S(1)} %bitcast.121, bf16[512,32,128]{0,2,1:T(8,128)(2,1)} %get-tuple-element.216, f32[512,32]{0,1:T(8,128)S(1)} %get-tuple-element.104, f32[32,128,512]{2,1,0:T(8,128)} %fusion.60, f32[512,32]{0,1:T(8,128)S(1)} %get-tuple-element.105, ...), kind=kOutput, calls=%fused_computation.28 | convolution fusion | flops 557826048 | bytes 47513600 | tf_op jit(solution)/shard_map/thd,hde->the/dot_general | solution.py:88
  408.1 6.3 %copy.78 = bf16[512,4096]{1,0:T(8,128)(2,1)} copy(bf16[512,4096]{0,1:T(8,128)(2,1)} %bitcast.119) | data formatting | bytes 8388608 | tf_op jit(solution)/shard_map/reshape | solution.py:95
  (50 shorter events, 54.5 us)
Async XLA Ops:
  1.0 34.0 %collective-permute-start = (bf16[3,3,4096]{2,1,0:T(4,128)(2,1)S(1)}, bf16[3,3,4096]{2,1,0:T(4,128)(2,1)S(1)}, u32[]{:S(2)}, u32[]{:S(2)}) collective-permute-start(bf16[3,3,4096]{2,1,0:T(4,128)(2,1)S(1)} %slice.69), channel_id=1, source_target_pairs={{0,1},{1,2},{2,3},{3,4},{4,5},{5,6},{6,7},{7,8},{8,9},{9,10},{10,1... | collective-permute-start | bytes 221192 | tf_op jit(solution)/shard_map/ppermute | solution.py:10
  118.8 2.0 copy-start.1
  118.8 3.3 copy-start.2
  124.8 52.7 %all-to-all-start = ((f32[1,32,128,128]{3,2,0,1:T(8,128)}), f32[1,32,128,128]{3,2,0,1:T(8,128)S(1)}, u32[]{:S(2)}, u32[]{:S(2)}) async-start(f32[1,32,128,128]{3,2,0,1:T(8,128)} %convolution_bitcast_fusion), calls=%async_computation | async-start | bytes 4194304 | tf_op jit(solution)/shard_map/all_to_all | solution.py:49
  181.2 30.2 %copy-start.3 = (pred[1,512,512]{2,0,1:T(4,128)(4,1)S(1)}, pred[1,512,512]{2,0,1:T(4,128)(4,1)}, u32[]{:S(2)}) copy-start(pred[1,512,512]{2,0,1:T(4,128)(4,1)} %get-tuple-element.121) | copy-start | bytes 786436
  181.2 30.2 %copy-start.4 = (pred[1,512,512]{2,0,1:T(4,128)(4,1)S(1)}, pred[1,512,512]{2,0,1:T(4,128)(4,1)}, u32[]{:S(2)}) copy-start(pred[1,512,512]{2,0,1:T(4,128)(4,1)} %get-tuple-element.122) | copy-start | bytes 786436
  184.3 184.0 %all-to-all-start.1 = ((bf16[4,16,2,128,128]{4,3,2,0,1:T(8,128)(2,1)}), bf16[4,16,2,128,128]{4,3,2,0,1:T(8,128)(2,1)}, u32[]{:S(2)}, u32[]{:S(2)}) async-start(bf16[4,16,2,128,128]{4,3,2,0,1:T(8,128)(2,1)} %copy.65), calls=%async_computation.1 | async-start | bytes 8388608 | tf_op jit(solution)/shard_map/all_to_all | solution.py:64
  245.1 10.4 %copy-start.5 = (s32[14,32,512]{2,1,0:T(8,128)S(1)}, s32[14,32,512]{2,1,0:T(8,128)}, u32[]{:S(2)}) copy-start(s32[14,32,512]{2,1,0:T(8,128)} %param.8) | copy-start | bytes 2752516
  368.3 3.5 copy-start
  385.4 17.4 %copy-start.6 = (f32[4096]{0:T(1024)S(1)}, f32[4096]{0:T(1024)}, u32[]{:S(2)}) copy-start(f32[4096]{0:T(1024)} %param.9) | copy-start | bytes 49156
where the time goes:
time: 422 us; the launch traced here: 415 us
  other arithmetic  150 us (36%)
  matrix products  141 us (33%)
  local copies, waits for them, and re-layouts  83.5 us (20%)
  starting transfers between devices  24.3 us (6%)
  waiting for transfers between devices  11.8 us (3%)
    and x5, other arithmetic, intra_levels(): causal & (level == number)  59.2 us
    convert_element_type x1, other arithmetic, on_device(): mixed_in = running.astype(jnp.bfloat16)  58.4 us
    dot_general x4, matrix products, group_block(): weight = jnp.einsum('lts,lht->hts', onehot, level_part, precision=highest)  55.2 us
    dot_general x4, matrix products, group_block(): jnp.einsum('hts,shd->thd', weights, value_part, preferred_element_type=jn...  48.9 us
    another operation x1, local copies, waits for them, and re-layouts, intra_levels(): jnp.stack([(causal & (level == number)).astype(jnp.float32) for number in...  33.7 us
    dot_general x4, matrix products, on_device(): jnp.einsum('thd,hde->the', query_rows, fenwick_bf[bit_index], preferred_e...  31 us
    unnamed x17, local copies, waits for them, and re-layouts  20.7 us
    convert_element_type x1, other arithmetic, on_device(): padded = jnp.concatenate([rim_rows, projected], 1).astype(jnp.float32)  16.9 us
  transfers between devices with their start and end apart: 3, of which 1 were waited for; matrix products, arithmetic and copies ran while one was open for 56% of the time, Pallas kernels for 0%

commit v1 on v0

v1 whole, which is shorter than its diff:
```python
import functools

import jax
import jax.numpy as jnp
from jax import lax
from jax.experimental import pallas as pl
from jax.experimental.pallas import tpu as pltpu
from jax.sharding import PartitionSpec as P

PAD = 8
TILE = 128
NT = (((1,), (1,)), ((), ()))


def convolve(data_ref, rim_ref, taps_ref, held):
    rows = data_ref.shape[1]
    taps = taps_ref.shape[1]
    held[0:PAD, :] = rim_ref[0]
    held[PAD : PAD + rows, :] = data_ref[0].astype(jnp.float32)
    total = taps_ref[0, 0:1, :] * held[PAD - taps + 1 : PAD - taps + 1 + rows, :]
    for tap in range(1, taps):
        first = PAD - taps + 1 + tap
        total = total + taps_ref[0, tap : tap + 1, :] * held[first : first + rows, :]
    return total.astype(jnp.bfloat16)


def state_kernel(dim, k_in, v_in, k_rim, v_rim, k_taps, v_taps, k_out, vt_out, state_out, held):
    k_out[...] = convolve(k_in, k_rim, k_taps, held)
    values = convolve(v_in, v_rim, v_taps, held)
    for head in range(k_out.shape[1] // dim):
        lanes = slice(head * dim, (head + 1) * dim)
        flipped = values[:, lanes].T
        vt_out[lanes, :] = flipped
        state_out[head] = jnp.dot(
            flipped, k_out[:, lanes], preferred_element_type=jnp.float32
        ).astype(jnp.bfloat16)


def tile_weights(lam, rows):
    strip = PAD.bit_length() - 1
    query = lax.rem(lax.broadcasted_iota(jnp.int32, (TILE // PAD, rows), 1), TILE)
    block = lax.broadcasted_iota(jnp.int32, (TILE // PAD, rows), 0)
    differ = lax.bitwise_xor(lax.shift_right_logical(query, strip), block)
    top = TILE.bit_length() - 1
    outer = jnp.broadcast_to(lam[top : top + 1], differ.shape)
    for level in range(top - 1, strip, -1):
        outer = jnp.where(differ < 2 ** (level - strip), lam[level : level + 1], outer)
    outer = jnp.where(block <= lax.shift_right_logical(query, strip), outer, 0.0)
    query8 = lax.rem(lax.broadcasted_iota(jnp.int32, (PAD, rows), 1), PAD)
    key8 = lax.broadcasted_iota(jnp.int32, (PAD, rows), 0)
    differ8 = lax.bitwise_xor(query8, key8)
    inner = jnp.broadcast_to(lam[strip : strip + 1], differ8.shape)
    for level in range(strip - 1, -1, -1):
        inner = jnp.where(differ8 < 2**level, lam[level : level + 1], inner)
    inner = jnp.where(key8 <= query8, inner, 0.0)
    own = lax.shift_right_logical(
        lax.rem(lax.broadcasted_iota(jnp.int32, (PAD, rows), 1), TILE), strip
    )
    return jnp.concatenate(
        [
            jnp.where(own == number, inner, outer[number : number + 1])
            for number in range(TILE // PAD)
        ],
        0,
    )


def inside_kernel(dim, q_in, q_rim, q_taps, k_in, vt_in, lam_in, q_old, in_old, q_out, in_out, held, weights):
    rows = k_in.shape[0]
    tiles = rows // TILE
    q_out[...] = convolve(q_in, q_rim, q_taps, held)
    top = TILE.bit_length() - 1
    pair = min(2, tiles)
    for tile in range(tiles):
        start = tile // pair * pair * TILE
        if start < tile * TILE:
            weights[tile * TILE : (tile + 1) * TILE, start : tile * TILE] = jnp.zeros(
                (TILE, tile * TILE - start), jnp.bfloat16
            )
    for head in range(k_in.shape[1] // dim):
        lanes = slice(head * dim, (head + 1) * dim)
        lam = lam_in[head]
        diagonal = tile_weights(lam, rows)
        for tile in range(tiles):
            keys = slice(tile * TILE, (tile + 1) * TILE)
            scores = lax.dot_general(
                k_in[keys, lanes],
                q_out[tile * TILE :, lanes],
                NT,
                preferred_element_type=jnp.float32,
            )
            for other in range(tile, tiles):
                queries = slice(other * TILE, (other + 1) * TILE)
                part = scores[:, (other - tile) * TILE : (other - tile + 1) * TILE]
                if other == tile:
                    factor = diagonal[:, queries]
                else:
                    level = top + (other ^ tile).bit_length()
                    factor = lam[level : level + 1, queries]
                weights[keys, queries] = (part * factor).astype(jnp.bfloat16)
        for first in range(0, tiles, pair):
            queries = slice(first * TILE, (first + pair) * TILE)
            depth = (first + pair) * TILE
            in_out[lanes, queries] = jnp.dot(
                vt_in[lanes, :depth], weights[:depth, queries], preferred_element_type=jnp.float32
            )


def mix_kernel(dim, base, bits, q_in, in_in, lam_in, gain_in, *rest):
    levels, out = rest[:bits], rest[bits]
    for head in range(q_in.shape[1] // dim):
        lanes = slice(head * dim, (head + 1) * dim)
        total = in_in[lanes, :]
        for bit in range(bits):
            product = lax.dot_general(
                levels[bit][head], q_in[:, lanes], NT, preferred_element_type=jnp.float32
            )
            total = total + lam_in[head, base + bit : base + bit + 1, :] * product
        inverse = lax.rsqrt(jnp.mean(total * total, 0, keepdims=True) + 1e-06)
        normed = (total * inverse).T * gain_in[0:1, lanes]
        out[:, lanes] = normed.astype(jnp.bfloat16)


def fenwick_levels(state):
    count = lax.axis_size("ctx")
    bits = count.bit_length() - 1
    me = lax.axis_index("ctx")
    heads = state.shape[0]
    found = []
    for bit in range(bits):
        depth = (bit + 1) // 2
        last = bit == bits - 1
        size = heads // 2**depth
        piece = state
        if depth:
            piece = lax.dynamic_slice_in_dim(state, (me & (2**depth - 1)) * size, size, 0)
        takers = [to for to in range(count) if not last or to >> bit & 1]
        got = lax.ppermute(piece, "ctx", [(to ^ 2**bit, to) for to in takers])
        for step in range(depth):
            other = lax.ppermute(got, "ctx", [(to ^ 2**step, to) for to in takers])
            got = jnp.where(
                (me >> step) & 1 == 1,
                jnp.concatenate([other, got], 0),
                jnp.concatenate([got, other], 0),
            )
        found.append(got)
        if not last:
            state = (state.astype(jnp.float32) + got.astype(jnp.float32)).astype(jnp.bfloat16)
    return found


def on_device(projected, conv_weight, level_codes, out_gain):
    taps = conv_weight.shape[1]
    rows, width = projected.shape[1:]
    level_count, heads = level_codes.shape[:2]
    dim = width // heads
    tok_bits = rows.bit_length() - 1
    count = lax.axis_size("ctx")
    bits = count.bit_length() - 1
    me = lax.axis_index("ctx")
    group = 4 if heads % 4 == 0 else 1
    lanes = group * dim
    steps = heads // group

    rim = lax.ppermute(
        projected[:, rows - taps + 1 :, :], "ctx", [(c, c + 1) for c in range(count - 1)]
    )
    rim = jnp.pad(rim.astype(jnp.float32), ((0, 0), (PAD - taps + 1, 0), (0, 0)))
    on_bit = (me >> jnp.arange(bits)) & 1
    scale = jnp.concatenate([jnp.ones((tok_bits + 1,), jnp.int32), on_bit])
    lam = (level_codes * scale[:, None, None]).transpose(1, 0, 2).astype(jnp.float32) / 8.0

    def data(kind, base=0):
        return [
            pl.BlockSpec((1, rows, lanes), lambda g: (kind, 0, g + base)),
            pl.BlockSpec((1, PAD, lanes), lambda g: (kind, 0, g + base)),
            pl.BlockSpec((1, taps, lanes), lambda g: (kind, 0, g + base)),
        ]

    def wide(base=0):
        return pl.BlockSpec((rows, lanes), lambda g: (0, g + base))

    def tall(base=0):
        return pl.BlockSpec((lanes, rows), lambda g: (g + base, 0))

    def per_head(size, base=0):
        return pl.BlockSpec((group,) + size, lambda g: (g + base, 0, 0))

    k_specs, v_specs = data(1), data(2)
    held = pltpu.VMEM((PAD + rows, lanes), jnp.float32)
    limit = pltpu.CompilerParams(vmem_limit_bytes=48 * 2**20)
    keys, values_t, state = pl.pallas_call(
        functools.partial(state_kernel, dim),
        grid=(steps,),
        in_specs=[s for both in zip(k_specs, v_specs) for s in both],
        out_specs=[wide(), tall(), per_head((dim, dim))],
        out_shape=[
            jax.ShapeDtypeStruct((rows, width), jnp.bfloat16),
            jax.ShapeDtypeStruct((width, rows), jnp.bfloat16),
            jax.ShapeDtypeStruct((heads, dim, dim), jnp.bfloat16),
        ],
        scratch_shapes=[held],
        compiler_params=limit,
        name="states",
    )(projected, projected, rim, rim, conv_weight, conv_weight)

    levels = fenwick_levels(state)

    parts = 4 if steps % 4 == 0 else 1
    own = steps // parts
    shapes = [
        jax.ShapeDtypeStruct((rows, width), jnp.bfloat16),
        jax.ShapeDtypeStruct((width, rows), jnp.float32),
    ]
    done = []
    for part in range(parts):
        base = part * own
        share = rows * rows * width // parts
        call = pl.pallas_call(
            functools.partial(inside_kernel, dim)
            if done
            else lambda *refs: inside_kernel(dim, *refs[:6], None, None, *refs[6:]),
            grid=(own,),
            in_specs=data(0, base)
            + [wide(base), tall(base), per_head((level_count, rows), base)]
            + [pl.BlockSpec(memory_space=pl.ANY)] * len(done),
            out_specs=[wide(base), tall(base)],
            out_shape=shapes,
            scratch_shapes=[held, pltpu.VMEM((rows, rows), jnp.bfloat16)],
            input_output_aliases={6: 0, 7: 1} if done else {},
            compiler_params=limit,
            cost_estimate=pl.CostEstimate(
                flops=8 * share, bytes_accessed=10 * rows * width // parts, transcendentals=0
            ),
            name="inside",
        )
        done = list(call(projected, rim, conv_weight, keys, values_t, lam, *done))
    queries, inside = done

    return pl.pallas_call(
        functools.partial(mix_kernel, dim, tok_bits + 1, bits),
        grid=(steps,),
        in_specs=[
            wide(),
            tall(),
            per_head((level_count, rows)),
            pl.BlockSpec((1, lanes), lambda g: (0, g)),
        ]
        + [per_head((dim, dim))] * bits,
        out_specs=wide(),
        out_shape=jax.ShapeDtypeStruct((rows, width), jnp.bfloat16),
        compiler_params=limit,
        name="mix",
    )(queries, inside, lam, out_gain.reshape(1, width), *levels)


def solution(mesh):
    placed = (P(None, ("groups", "ctx"), None), P(), P(None, None, ("groups", "ctx")), P())
    return jax.shard_map(
        on_device, mesh=mesh, in_specs=placed, out_specs=P(("groups", "ctx"), None), check_vma=False
    )
```

time: 422 us -> 131 us (0.31)
  the two profiles are of different devices: /device:TPU:15 before, /device:TPU:25 now
where the time goes in v1:
time: 131 us
  Pallas kernels  53.5 us (41%)
  waiting for transfers between devices  48 us (37%)
  starting transfers between devices  15.1 us (12%)
  local copies, waits for them, and re-layouts  7.07 us (5%)
  other arithmetic  6.91 us (5%)
    ppermute x4, waiting for transfers between devices, fenwick_levels(): got = lax.ppermute(piece, 'ctx', [(to ^ 2 ** bit, to) for to in takers])  43.1 us
    pallas_call x4, Pallas kernels, on_device(): done = list(call(projected, rim, conv_weight, keys, values_t, lam, *done))  25.7 us
    pallas_call x1, Pallas kernels, on_device(): pl.pallas_call(functools.partial(state_kernel, dim), grid=(steps,), in_sp...  16 us
    pallas_call x1, Pallas kernels, on_device(): pl.pallas_call(functools.partial(mix_kernel, dim, tok_bits + 1, bits), gr...  11.8 us
    ppermute x4, starting transfers between devices, fenwick_levels(): other = lax.ppermute(got, 'ctx', [(to ^ 2 ** step, to) for to in takers])  7.27 us
    unnamed x16, local copies, waits for them, and re-layouts  4.89 us
    convert_element_type x3, other arithmetic, fenwick_levels(): (state.astype(jnp.float32) + got.astype(jnp.float32)).astype(jnp.bfloat16)  4.66 us
    ppermute x4, starting transfers between devices, fenwick_levels(): got = lax.ppermute(piece, 'ctx', [(to ^ 2 ** bit, to) for to in takers])  4.11 us
  transfers between devices with their start and end apart: 9, of which 7 were waited for; matrix products, arithmetic and copies ran while one was open for 1% of the time, Pallas kernels for 20%

profile of v1, /device:TPU:25, one launch (start us, length us, event | category | flops | bytes accessed | tf_op | source)
XLA Modules:
  0.0 130.7 jit_solution(13118521669476422156)
XLA Ops:
  1.0 3.7 %collective-permute-start = (bf16[3,3,4096]{2,1,0:T(4,128)(2,1)S(1)}, bf16[3,3,4096]{2,1,0:T(4,128)(2,1)S(1)}, u32[]{:S(2)}, u32[]{:S(2)}) collective-permute-start(bf16[3,3,4096]{2,1,0:T(4,128)(2,1)S(1)} %slice.3), channel_id=1, source_target_pairs={{0,1},{1,2},{2,3},{3,4},{4,5},{5,6},{6,7},{7,8},{8,9},{9,10},{10,1... | collective-permute-start | bytes 221192 | tf_op jit(solution)/shard_map/ppermute | solution.py:165
  4.7 1.6 %collective-permute-done = bf16[3,3,4096]{2,1,0:T(4,128)(2,1)S(1)} collective-permute-done((bf16[3,3,4096]{2,1,0:T(4,128)(2,1)S(1)}, bf16[3,3,4096]{2,1,0:T(4,128)(2,1)S(1)}, u32[]{:S(2)}, u32[]{:S(2)}) %collective-permute-start) | collective-permute-done | bytes 73760 | tf_op jit(solution)/shard_map/ppermute | solution.py:165
  7.3 16.0 %states.1 = (bf16[512,4096]{1,0:T(8,128)(2,1)S(1)}, bf16[4096,512]{1,0:T(8,128)(2,1)}, bf16[32,128,128]{2,1,0:T(8,128)(2,1)S(1)}) custom-call(bf16[3,512,4096]{2,1,0:T(8,128)(2,1)} %q_in.5, bf16[3,512,4096]{2,1,0:T(8,128)(2,1)} %q_in.5, f32[3,8,4096]{2,1,0:T(8,128)S(1)} %pad_convert_fusion.k_rim.v_rim.refs_1_.q_rim, ...), custom_call_target="tpu_custom_call" | custom-call | tf_op jit(solution)/shard_map/states/pallas_call | solution.py:192
  23.3 2.0 %copy-done = bf16[512,4096]{1,0:T(8,128)(2,1)} copy-done((bf16[512,4096]{1,0:T(8,128)(2,1)}, bf16[512,4096]{1,0:T(8,128)(2,1)S(1)}, u32[]{:S(2)}) %copy-start) | copy-done | bytes 4194328
  25.3 2.2 %collective-permute-start.1 = (bf16[32,128,128]{2,1,0:T(8,128)(2,1)S(1)}, bf16[32,128,128]{2,1,0:T(8,128)(2,1)S(1)}, u32[]{:S(2)}, u32[]{:S(2)}) collective-permute-start(bf16[32,128,128]{2,1,0:T(8,128)(2,1)S(1)} %get-tuple-element.26), channel_id=1, source_target_pairs={{1,0},{0,1},{3,2},{2,3},{5,4},{4,5},{7,6},{6,7},{9,8},{8,9},{11,10... | collective-permute-start | bytes 3145736 | tf_op jit(solution)/shard_map/ppermute | solution.py:138
  27.5 2.3 %collective-permute-done.1.rest_0_ = bf16[32,128,128]{2,1,0:T(8,128)(2,1)S(1)} collective-permute-done((bf16[32,128,128]{2,1,0:T(8,128)(2,1)S(1)}, bf16[32,128,128]{2,1,0:T(8,128)(2,1)S(1)}, u32[]{:S(2)}, u32[]{:S(2)}) %collective-permute-start.1) | collective-permute-done | bytes 1048608 | tf_op jit(solution)/shard_map/ppermute | solution.py:138
  30.7 12.8 %collective-permute-done.2 = bf16[16,128,128]{2,1,0:T(8,128)(2,1)S(1)} collective-permute-done((bf16[16,128,128]{2,1,0:T(8,128)(2,1)S(1)}, bf16[16,128,128]{2,1,0:T(8,128)(2,1)S(1)}, u32[]{:S(2)}, u32[]{:S(2)}) %collective-permute-start.2) | collective-permute-done | bytes 524320 | tf_op jit(solution)/shard_map/ppermute | solution.py:138
  43.5 1.2 collective-permute-start.3
  44.7 1.7 %collective-permute-done.3 = bf16[16,128,128]{2,1,0:T(8,128)(2,1)} collective-permute-done((bf16[16,128,128]{2,1,0:T(8,128)(2,1)S(1)}, bf16[16,128,128]{2,1,0:T(8,128)(2,1)}, u32[]{:S(2)}, u32[]{:S(2)}) %collective-permute-start.3) | collective-permute-done | bytes 524320 | tf_op jit(solution)/shard_map/ppermute | solution.py:140
  46.4 3.2 %add_convert_fusion = (bf16[32,128,128]{2,1,0:T(8,128)(2,1)}, bf16[32,128,128]{2,1,0:T(8,128)(2,1)}) fusion(bf16[32,128,128]{2,1,0:T(8,128)(2,1)S(1)} %add_convert_fusion.1, bf16[16,128,128]{2,1,0:T(8,128)(2,1)} %collective-permute-done.3, bf16[16,128,128]{2,1,0:T(8,128)(2,1)S(1)} %collective-permute-done.2, pred[]{:T(512)S(6)} %eq.8), kind=kLoop, calls=%fused_computation | loop fusion | flops 3670016 | bytes 4194305 | tf_op jit(solution)/shard_map/convert_element_type | solution.py:148
  50.9 12.9 %collective-permute-done.4 = bf16[16,128,128]{2,1,0:T(8,128)(2,1)S(1)} collective-permute-done((bf16[16,128,128]{2,1,0:T(8,128)(2,1)S(1)}, bf16[16,128,128]{2,1,0:T(8,128)(2,1)S(1)}, u32[]{:S(2)}, u32[]{:S(2)}) %collective-permute-start.4) | collective-permute-done | bytes 524320 | tf_op jit(solution)/shard_map/ppermute | solution.py:138
  63.8 1.2 collective-permute-start.5
  65.0 1.5 %collective-permute-done.5 = bf16[16,128,128]{2,1,0:T(8,128)(2,1)S(1)} collective-permute-done((bf16[16,128,128]{2,1,0:T(8,128)(2,1)S(1)}, bf16[16,128,128]{2,1,0:T(8,128)(2,1)S(1)}, u32[]{:S(2)}, u32[]{:S(2)}) %collective-permute-start.5) | collective-permute-done | bytes 524320 | tf_op jit(solution)/shard_map/ppermute | solution.py:140
  67.8 1.3 collective-permute-start.6
  69.2 15.2 %collective-permute-done.6 = bf16[8,128,128]{2,1,0:T(8,128)(2,1)S(1)} collective-permute-done((bf16[8,128,128]{2,1,0:T(8,128)(2,1)S(1)}, bf16[8,128,128]{2,1,0:T(8,128)(2,1)S(1)}, u32[]{:S(2)}, u32[]{:S(2)}) %collective-permute-start.6) | collective-permute-done | bytes 262176 | tf_op jit(solution)/shard_map/ppermute | solution.py:138
  84.3 2.4 %collective-permute-start.7 = (bf16[8,128,128]{2,1,0:T(8,128)(2,1)S(1)}, bf16[8,128,128]{2,1,0:T(8,128)(2,1)S(1)}, u32[]{:S(2)}, u32[]{:S(2)}) collective-permute-start(bf16[8,128,128]{2,1,0:T(8,128)(2,1)S(1)} %collective-permute-done.6), channel_id=1, source_target_pairs={{9,8},{8,9},{11,10},{10,11},{13,12},{12,13},{15,14},{14,15},{25,24... | collective-permute-start | bytes 786440 | tf_op jit(solution)/shard_map/ppermute | solution.py:140
  86.7 1.8 %fusion.2.refs_5_.lam_in = f32[32,14,512]{2,1,0:T(8,128)S(1)} fusion(s32[14,32,512]{2,1,0:T(8,128)} %param.6, s32[14]{0:T(128)S(1)} %concatenate.27), kind=kLoop, calls=%fused_computation.8 | loop fusion | flops 688128 | bytes 1835064 | tf_op jit(solution)/shard_map/div | solution.py:171
  88.5 6.4 %inside.4 = (bf16[512,4096]{1,0:T(8,128)(2,1)S(1)}, f32[4096,512]{1,0:T(8,128)}) custom-call(bf16[3,512,4096]{2,1,0:T(8,128)(2,1)} %q_in.5, f32[3,8,4096]{2,1,0:T(8,128)S(1)} %pad_convert_fusion.k_rim.v_rim.refs_1_.q_rim, f32[3,4,4096]{2,1,0:T(4,128)S(1)} %copy-done.3, bf16[512,4096]{1,0:T(8,128)(2,1)} %copy-done, ...), custom_call_target="tpu_custom_call" | custom-call | flops 2147483648 | bytes 5242880 | tf_op jit(solution)/shard_map/inside/pallas_call | solution.py:237
  94.9 2.4 %collective-permute-start.8 = (bf16[16,128,128]{2,1,0:T(8,128)(2,1)S(1)}, bf16[16,128,128]{2,1,0:T(8,128)(2,1)S(1)}, u32[]{:S(2)}, u32[]{:S(2)}) collective-permute-start(bf16[16,128,128]{2,1,0:T(8,128)(2,1)S(1)} %maximum_select_fusion.3), channel_id=1, source_target_pairs={{10,8},{11,9},{8,10},{9,11},{14,12},{15,13},{12,14},{13,15},{26,24... | collective-permute-start | bytes 1572872 | tf_op jit(solution)/shard_map/ppermute | solution.py:140
  97.4 6.4 %inside.5 = (bf16[512,4096]{1,0:T(8,128)(2,1)S(1)}, f32[4096,512]{1,0:T(8,128)}) custom-call(bf16[3,512,4096]{2,1,0:T(8,128)(2,1)} %q_in.5, f32[3,8,4096]{2,1,0:T(8,128)S(1)} %pad_convert_fusion.k_rim.v_rim.refs_1_.q_rim, f32[3,4,4096]{2,1,0:T(4,128)S(1)} %copy-done.3, bf16[512,4096]{1,0:T(8,128)(2,1)} %copy-done, ...), custom_call_target="tpu_custom_call", output_to_operand_aliasing={{0}: (6, {}), {1}: (7, {})} | custom-call | flops 2147483648 | bytes 5242880 | tf_op jit(solution)/shard_map/inside/pallas_call | solution.py:237
  103.8 6.4 %inside.6 = (bf16[512,4096]{1,0:T(8,128)(2,1)S(1)}, f32[4096,512]{1,0:T(8,128)}) custom-call(bf16[3,512,4096]{2,1,0:T(8,128)(2,1)} %q_in.5, f32[3,8,4096]{2,1,0:T(8,128)S(1)} %pad_convert_fusion.k_rim.v_rim.refs_1_.q_rim, f32[3,4,4096]{2,1,0:T(4,128)S(1)} %copy-done.3, bf16[512,4096]{1,0:T(8,128)(2,1)} %copy-done, ...), custom_call_target="tpu_custom_call", output_to_operand_aliasing={{0}: (6, {}), {1}: (7, {})} | custom-call | flops 2147483648 | bytes 5242880 | tf_op jit(solution)/shard_map/inside/pallas_call | solution.py:237
  110.1 6.6 %inside.7 = (bf16[512,4096]{1,0:T(8,128)(2,1)S(1)}, f32[4096,512]{1,0:T(8,128)}) custom-call(bf16[3,512,4096]{2,1,0:T(8,128)(2,1)} %q_in.5, f32[3,8,4096]{2,1,0:T(8,128)S(1)} %pad_convert_fusion.k_rim.v_rim.refs_1_.q_rim, f32[3,4,4096]{2,1,0:T(4,128)S(1)} %copy-done.3, bf16[512,4096]{1,0:T(8,128)(2,1)} %copy-done, ...), custom_call_target="tpu_custom_call", output_to_operand_aliasing={{0}: (6, {}), {1}: (7, {})} | custom-call | flops 2147483648 | bytes 5242880 | tf_op jit(solution)/shard_map/inside/pallas_call | solution.py:237
  116.7 2.0 %copy-done.1 = bf16[512,4096]{1,0:T(8,128)(2,1)} copy-done((bf16[512,4096]{1,0:T(8,128)(2,1)}, bf16[512,4096]{1,0:T(8,128)(2,1)S(1)}, u32[]{:S(2)}) %copy-start.1) | copy-done | bytes 4194328
  118.9 11.8 %mix.1 = bf16[512,4096]{1,0:T(8,128)(2,1)} custom-call(bf16[512,4096]{1,0:T(8,128)(2,1)} %copy-done.1, f32[4096,512]{1,0:T(8,128)} %get-tuple-element.25.in_in, f32[32,14,512]{2,1,0:T(8,128)S(1)} %fusion.2.refs_5_.lam_in, f32[1,4096]{1,0:T(1,128)S(1)} %bitcast.3, bf16[32,128,128]{2,1,0:T(8,128)(2,1)S(1)} %copy-done.5, bf16[32,128,128]{2,1,0:T(8,128)(2,1)S(1)} %copy-done.6, ...), custom_call_target="tpu_custom_call" | custom-call | tf_op jit(solution)/shard_map/mix/pallas_call | solution.py:240
  (29 shorter events, 5.7 us)
Async XLA Ops:
  1.0 5.3 %collective-permute-start = (bf16[3,3,4096]{2,1,0:T(4,128)(2,1)S(1)}, bf16[3,3,4096]{2,1,0:T(4,128)(2,1)S(1)}, u32[]{:S(2)}, u32[]{:S(2)}) collective-permute-start(bf16[3,3,4096]{2,1,0:T(4,128)(2,1)S(1)} %slice.3), channel_id=1, source_target_pairs={{0,1},{1,2},{2,3},{3,4},{4,5},{5,6},{6,7},{7,8},{8,9},{9,10},{10,1... | collective-permute-start | bytes 221192 | tf_op jit(solution)/shard_map/ppermute | solution.py:165
  6.4 0.9 copy-start.2
  23.3 2.0 %copy-start = (bf16[512,4096]{1,0:T(8,128)(2,1)}, bf16[512,4096]{1,0:T(8,128)(2,1)S(1)}, u32[]{:S(2)}) copy-start(bf16[512,4096]{1,0:T(8,128)(2,1)S(1)} %get-tuple-element.16.refs_3_.k_in) | copy-start | bytes 12582916
  25.3 4.5 %collective-permute-start.1 = (bf16[32,128,128]{2,1,0:T(8,128)(2,1)S(1)}, bf16[32,128,128]{2,1,0:T(8,128)(2,1)S(1)}, u32[]{:S(2)}, u32[]{:S(2)}) collective-permute-start(bf16[32,128,128]{2,1,0:T(8,128)(2,1)S(1)} %get-tuple-element.26), channel_id=1, source_target_pairs={{1,0},{0,1},{3,2},{2,3},{5,4},{4,5},{7,6},{6,7},{9,8},{8,9},{11,10... | collective-permute-start | bytes 3145736 | tf_op jit(solution)/shard_map/ppermute | solution.py:138
  29.8 19.8 %copy-start.4 = (bf16[32,128,128]{2,1,0:T(8,128)(2,1)}, bf16[32,128,128]{2,1,0:T(8,128)(2,1)S(1)}, u32[]{:S(2)}) copy-start(bf16[32,128,128]{2,1,0:T(8,128)(2,1)S(1)} %collective-permute-done.1.rest_0_) | copy-start | bytes 3145732
  30.3 13.2 %collective-permute-start.2 = (bf16[16,128,128]{2,1,0:T(8,128)(2,1)S(1)}, bf16[16,128,128]{2,1,0:T(8,128)(2,1)S(1)}, u32[]{:S(2)}, u32[]{:S(2)}) collective-permute-start(bf16[16,128,128]{2,1,0:T(8,128)(2,1)S(1)} %constant_dynamic-slice_fusion.1), channel_id=1, source_target_pairs={{2,0},{3,1},{0,2},{1,3},{6,4},{7,5},{4,6},{5,7},{10,8},{11,9},{8,1... | collective-permute-start | bytes 1572872 | tf_op jit(solution)/shard_map/ppermute | solution.py:138
  43.5 2.9 %collective-permute-start.3 = (bf16[16,128,128]{2,1,0:T(8,128)(2,1)S(1)}, bf16[16,128,128]{2,1,0:T(8,128)(2,1)}, u32[]{:S(2)}, u32[]{:S(2)}) collective-permute-start(bf16[16,128,128]{2,1,0:T(8,128)(2,1)S(1)} %collective-permute-done.2), channel_id=1, source_target_pairs={{1,0},{0,1},{3,2},{2,3},{5,4},{4,5},{7,6},{6,7},{9,8},{8,9},{11,10... | collective-permute-start | bytes 1572872 | tf_op jit(solution)/shard_map/ppermute | solution.py:140
  44.7 43.8 %copy-start.3 = (f32[3,4,4096]{2,1,0:T(4,128)S(1)}, f32[3,4,4096]{2,1,0:T(4,128)}, u32[]{:S(2)}) copy-start(f32[3,4,4096]{2,1,0:T(4,128)} %q_taps.5) | copy-start | bytes 589828
  50.6 13.2 %collective-permute-start.4 = (bf16[16,128,128]{2,1,0:T(8,128)(2,1)S(1)}, bf16[16,128,128]{2,1,0:T(8,128)(2,1)S(1)}, u32[]{:S(2)}, u32[]{:S(2)}) collective-permute-start(bf16[16,128,128]{2,1,0:T(8,128)(2,1)S(1)} %constant_dynamic-slice_fusion), channel_id=1, source_target_pairs={{4,0},{5,1},{6,2},{7,3},{0,4},{1,5},{2,6},{3,7},{12,8},{13,9},{14,... | collective-permute-start | bytes 1572872 | tf_op jit(solution)/shard_map/ppermute | solution.py:138
  63.8 2.8 %collective-permute-start.5 = (bf16[16,128,128]{2,1,0:T(8,128)(2,1)S(1)}, bf16[16,128,128]{2,1,0:T(8,128)(2,1)S(1)}, u32[]{:S(2)}, u32[]{:S(2)}) collective-permute-start(bf16[16,128,128]{2,1,0:T(8,128)(2,1)S(1)} %collective-permute-done.4), channel_id=1, source_target_pairs={{1,0},{0,1},{3,2},{2,3},{5,4},{4,5},{7,6},{6,7},{9,8},{8,9},{11,10... | collective-permute-start | bytes 1572872 | tf_op jit(solution)/shard_map/ppermute | solution.py:140
  67.8 16.5 %collective-permute-start.6 = (bf16[8,128,128]{2,1,0:T(8,128)(2,1)S(1)}, bf16[8,128,128]{2,1,0:T(8,128)(2,1)S(1)}, u32[]{:S(2)}, u32[]{:S(2)}) collective-permute-start(bf16[8,128,128]{2,1,0:T(8,128)(2,1)S(1)} %add_convert_fusion.2), channel_id=1, source_target_pairs={{0,8},{1,9},{2,10},{3,11},{4,12},{5,13},{6,14},{7,15},{16,24},{17,... | collective-permute-start | bytes 786440 | tf_op jit(solution)/shard_map/ppermute | solution.py:138
  84.3 10.6 %collective-permute-start.7 = (bf16[8,128,128]{2,1,0:T(8,128)(2,1)S(1)}, bf16[8,128,128]{2,1,0:T(8,128)(2,1)S(1)}, u32[]{:S(2)}, u32[]{:S(2)}) collective-permute-start(bf16[8,128,128]{2,1,0:T(8,128)(2,1)S(1)} %collective-permute-done.6), channel_id=1, source_target_pairs={{9,8},{8,9},{11,10},{10,11},{13,12},{12,13},{15,14},{14,15},{25,24... | collective-permute-start | bytes 786440 | tf_op jit(solution)/shard_map/ppermute | solution.py:140
  94.9 23.8 %collective-permute-start.8 = (bf16[16,128,128]{2,1,0:T(8,128)(2,1)S(1)}, bf16[16,128,128]{2,1,0:T(8,128)(2,1)S(1)}, u32[]{:S(2)}, u32[]{:S(2)}) collective-permute-start(bf16[16,128,128]{2,1,0:T(8,128)(2,1)S(1)} %maximum_select_fusion.3), channel_id=1, source_target_pairs={{10,8},{11,9},{8,10},{9,11},{14,12},{15,13},{12,14},{13,15},{26,24... | collective-permute-start | bytes 1572872 | tf_op jit(solution)/shard_map/ppermute | solution.py:140
  110.1 8.7 %copy-start.5 = (bf16[32,128,128]{2,1,0:T(8,128)(2,1)S(1)}, bf16[32,128,128]{2,1,0:T(8,128)(2,1)}, u32[]{:S(2)}) copy-start(bf16[32,128,128]{2,1,0:T(8,128)(2,1)} %copy-done.4) | copy-start | bytes 3145732
  110.1 8.8 %copy-start.6 = (bf16[32,128,128]{2,1,0:T(8,128)(2,1)S(1)}, bf16[32,128,128]{2,1,0:T(8,128)(2,1)}, u32[]{:S(2)}) copy-start(bf16[32,128,128]{2,1,0:T(8,128)(2,1)} %get-tuple-element.28.rest_1_) | copy-start | bytes 3145732
  110.1 8.8 %copy-start.7 = (f32[4096]{0:T(1024)S(1)}, f32[4096]{0:T(1024)}, u32[]{:S(2)}) copy-start(f32[4096]{0:T(1024)} %param.7) | copy-start | bytes 49156
  116.7 2.0 %copy-start.1 = (bf16[512,4096]{1,0:T(8,128)(2,1)}, bf16[512,4096]{1,0:T(8,128)(2,1)S(1)}, u32[]{:S(2)}) copy-start(bf16[512,4096]{1,0:T(8,128)(2,1)S(1)} %get-tuple-element.24.q_in) | copy-start | bytes 12582916

commit v2 on v1

--- a/solution.py
+++ b/solution.py
@@ -121,32 +121,67 @@
         out[:, lanes] = normed.astype(jnp.bfloat16)
 
 
-def fenwick_levels(state):
-    count = lax.axis_size("ctx")
-    bits = count.bit_length() - 1
-    me = lax.axis_index("ctx")
-    heads = state.shape[0]
-    found = []
-    for bit in range(bits):
+class Chain:
+    def __init__(self):
+        self.count = lax.axis_size("ctx")
+        self.bits = self.count.bit_length() - 1
+        self.me = lax.axis_index("ctx")
+        self.state, self.got, self.found = None, None, []
+
+    def piece(self, bit):
         depth = (bit + 1) // 2
-        last = bit == bits - 1
-        size = heads // 2**depth
-        piece = state
-        if depth:
-            piece = lax.dynamic_slice_in_dim(state, (me & (2**depth - 1)) * size, size, 0)
-        takers = [to for to in range(count) if not last or to >> bit & 1]
-        got = lax.ppermute(piece, "ctx", [(to ^ 2**bit, to) for to in takers])
+        if not depth:
+            return self.state
+        size = self.state.shape[0] // 2**depth
+        index = 0
         for step in range(depth):
-            other = lax.ppermute(got, "ctx", [(to ^ 2**step, to) for to in takers])
-            got = jnp.where(
-                (me >> step) & 1 == 1,
-                jnp.concatenate([other, got], 0),
-                jnp.concatenate([got, other], 0),
-            )
-        found.append(got)
-        if not last:
-            state = (state.astype(jnp.float32) + got.astype(jnp.float32)).astype(jnp.bfloat16)
-    return found
+            index = index + (((self.me >> step) & 1) << (depth - 1 - step))
+        return lax.dynamic_slice_in_dim(self.state, index * size, size, 0)
+
+    def operations(self, bit):
+        return [(bit, None)] + [(bit, step) for step in reversed(range((bit + 1) // 2))]
+
+    def takers(self, bit):
+        return [to for to in range(self.count) if bit < self.bits - 1 or to >> bit & 1]
+
+    def outgoing(self, operation):
+        bit, step = operation
+        return self.piece(bit) if step is None else self.got
+
+    def exchange(self, operation, value):
+        bit, step = operation
+        away = 2**bit if step is None else 2**step
+        return lax.ppermute(value, "ctx", [(to ^ away, to) for to in self.takers(bit)])
+
+    def land(self, operation, value, came):
+        bit, step = operation
+        if step is None:
+            self.got = came
+        else:
+            self.got = jnp.where(
+                (self.me >> step) & 1 == 1,
+                jnp.concatenate([came, value], 0),
+                jnp.concatenate([value, came], 0),
+            )
+        if operation == self.operations(bit)[-1]:
+            self.found.append(self.got)
+            if bit < self.bits - 1:
+                total = self.state.astype(jnp.float32) + self.got.astype(jnp.float32)
+                self.state = total.astype(jnp.bfloat16)
+
+
+def tie(values):
+    return lax.optimization_barrier(values)
+
+
+def stage(moves, compute, inputs):
+    values, inputs = tie(([chain.outgoing(op) for chain, op in moves], inputs))
+    came = [chain.exchange(op, value) for (chain, op), value in zip(moves, values)]
+    results = compute(inputs) if compute else inputs
+    came, values, results = tie((came, values, results))
+    for (chain, op), value, new in zip(moves, values, came):
+        chain.land(op, value, new)
+    return results
 
 
 def on_device(projected, conv_weight, level_codes, out_gain):
@@ -158,19 +193,21 @@
     count = lax.axis_size("ctx")
     bits = count.bit_length() - 1
     me = lax.axis_index("ctx")
-    group = 4 if heads % 4 == 0 else 1
+    group = 4
     lanes = group * dim
-    steps = heads // group
+    halves, parts = 2, 4
+    steps = heads // group // halves
 
     rim = lax.ppermute(
         projected[:, rows - taps + 1 :, :], "ctx", [(c, c + 1) for c in range(count - 1)]
     )
-    rim = jnp.pad(rim.astype(jnp.float32), ((0, 0), (PAD - taps + 1, 0), (0, 0)))
     on_bit = (me >> jnp.arange(bits)) & 1
     scale = jnp.concatenate([jnp.ones((tok_bits + 1,), jnp.int32), on_bit])
     lam = (level_codes * scale[:, None, None]).transpose(1, 0, 2).astype(jnp.float32) / 8.0
-
-    def data(kind, base=0):
+    rim, lam = tie((rim, lam))
+    rim = jnp.pad(rim.astype(jnp.float32), ((0, 0), (PAD - taps + 1, 0), (0, 0)))
+
+    def data(kind, base):
         return [
             pl.BlockSpec((1, rows, lanes), lambda g: (kind, 0, g + base)),
             pl.BlockSpec((1, PAD, lanes), lambda g: (kind, 0, g + base)),
@@ -186,46 +223,49 @@
     def per_head(size, base=0):
         return pl.BlockSpec((group,) + size, lambda g: (g + base, 0, 0))
 
-    k_specs, v_specs = data(1), data(2)
     held = pltpu.VMEM((PAD + rows, lanes), jnp.float32)
-    limit = pltpu.CompilerParams(vmem_limit_bytes=48 * 2**20)
-    keys, values_t, state = pl.pallas_call(
-        functools.partial(state_kernel, dim),
-        grid=(steps,),
-        in_specs=[s for both in zip(k_specs, v_specs) for s in both],
-        out_specs=[wide(), tall(), per_head((dim, dim))],
-        out_shape=[
-            jax.ShapeDtypeStruct((rows, width), jnp.bfloat16),
-            jax.ShapeDtypeStruct((width, rows), jnp.bfloat16),
-            jax.ShapeDtypeStruct((heads, dim, dim), jnp.bfloat16),
-        ],
-        scratch_shapes=[held],
-        compiler_params=limit,
-        name="states",
-    )(projected, projected, rim, rim, conv_weight, conv_weight)
-
-    levels = fenwick_levels(state)
-
-    parts = 4 if steps % 4 == 0 else 1
-    own = steps // parts
-    shapes = [
-        jax.ShapeDtypeStruct((rows, width), jnp.bfloat16),
-        jax.ShapeDtypeStruct((width, rows), jnp.float32),
-    ]
-    done = []
-    for part in range(parts):
-        base = part * own
+    limit = pltpu.CompilerParams(vmem_limit_bytes=56 * 2**20)
+    half_width = width // halves
+
+    def states(half, rim):
+        base = half * steps
+        return pl.pallas_call(
+            functools.partial(state_kernel, dim),
+            grid=(steps,),
+            in_specs=[s for both in zip(data(1, base), data(2, base)) for s in both],
+            out_specs=[wide(), tall(), per_head((dim, dim))],
+            out_shape=[
+                jax.ShapeDtypeStruct((rows, half_width), jnp.bfloat16),
+                jax.ShapeDtypeStruct((half_width, rows), jnp.bfloat16),
+                jax.ShapeDtypeStruct((heads // halves, dim, dim), jnp.bfloat16),
+            ],
+            scratch_shapes=[held],
+            compiler_params=limit,
+            cost_estimate=pl.CostEstimate(
+                flops=2 * rows * half_width * dim,
+                bytes_accessed=8 * rows * half_width,
+                transcendentals=0,
+            ),
+            name="states",
+        )(projected, projected, rim, rim, conv_weight, conv_weight)
+
+    def inside(part, rim, keys, values_t, lam, done):
+        own = steps * halves // parts
+        within = part % (parts // halves) * own
         share = rows * rows * width // parts
         call = pl.pallas_call(
             functools.partial(inside_kernel, dim)
             if done
             else lambda *refs: inside_kernel(dim, *refs[:6], None, None, *refs[6:]),
             grid=(own,),
-            in_specs=data(0, base)
-            + [wide(base), tall(base), per_head((level_count, rows), base)]
+            in_specs=data(0, part * own)
+            + [wide(within), tall(within), per_head((level_count, rows), part * own)]
             + [pl.BlockSpec(memory_space=pl.ANY)] * len(done),
-            out_specs=[wide(base), tall(base)],
-            out_shape=shapes,
+            out_specs=[wide(within), tall(within)],
+            out_shape=[
+                jax.ShapeDtypeStruct((rows, half_width), jnp.bfloat16),
+                jax.ShapeDtypeStruct((half_width, rows), jnp.float32),
+            ],
             scratch_shapes=[held, pltpu.VMEM((rows, rows), jnp.bfloat16)],
             input_output_aliases={6: 0, 7: 1} if done else {},
             compiler_params=limit,
@@ -234,24 +274,76 @@
             ),
             name="inside",
         )
-        done = list(call(projected, rim, conv_weight, keys, values_t, lam, *done))
-    queries, inside = done
-
-    return pl.pallas_call(
-        functools.partial(mix_kernel, dim, tok_bits + 1, bits),
-        grid=(steps,),
-        in_specs=[
-            wide(),
-            tall(),
-            per_head((level_count, rows)),
-            pl.BlockSpec((1, lanes), lambda g: (0, g)),
-        ]
-        + [per_head((dim, dim))] * bits,
-        out_specs=wide(),
-        out_shape=jax.ShapeDtypeStruct((rows, width), jnp.bfloat16),
-        compiler_params=limit,
-        name="mix",
-    )(queries, inside, lam, out_gain.reshape(1, width), *levels)
+        return list(call(projected, rim, conv_weight, keys, values_t, lam, *done))
+
+    def mix(half, queries, within, lam, levels, done):
+        base = half * steps
+        kernel = functools.partial(mix_kernel, dim, tok_bits + 1, bits)
+        if done:
+            kernel = lambda *refs: mix_kernel(
+                dim, tok_bits + 1, bits, *refs[: 4 + bits], refs[-1]
+            )
+        return pl.pallas_call(
+            kernel,
+            grid=(steps,),
+            in_specs=[
+                wide(),
+                tall(),
+                per_head((level_count, rows), base),
+                pl.BlockSpec((1, lanes), lambda g: (0, g + base)),
+            ]
+            + [per_head((dim, dim))] * bits
+            + [pl.BlockSpec(memory_space=pl.ANY)] * len(done),
+            out_specs=wide(base),
+            out_shape=jax.ShapeDtypeStruct((rows, width), jnp.bfloat16),
+            input_output_aliases={4 + bits: 0} if done else {},
+            compiler_params=limit,
+            cost_estimate=pl.CostEstimate(
+                flops=2 * bits * rows * half_width * dim,
+                bytes_accessed=8 * rows * half_width,
+                transcendentals=0,
+            ),
+            name="mix",
+        )(queries, within, lam, out_gain.reshape(1, width), *levels, *done)
+
+    first, second = Chain(), Chain()
+    keys, values_t = [None] * halves, [None] * halves
+    keys[0], values_t[0], first.state = states(0, rim)
+    keys[1], values_t[1], second.state = stage(
+        [(first, op) for op in first.operations(0)], lambda r: states(1, r), rim
+    )
+    done = [[], []]
+    waiting = list(range(parts))
+    for turn in range(1, bits + 1):
+        early = first.operations(turn) if turn < bits else []
+        late = second.operations(turn - 1)
+        todo = [waiting.pop(0)] if waiting else []
+        if turn == bits:
+            todo, waiting = todo + waiting, []
+        for index in range(max(len(early), len(late))):
+            moves = [(first, op) for op in early[index : index + 1]]
+            moves += [(second, op) for op in late[index : index + 1]]
+            if index == 0 and todo:
+
+                def run(inputs):
+                    lam, done = inputs
+                    done = list(done)
+                    for part in todo:
+                        half = part * halves // parts
+                        done[half] = inside(part, rim, keys[half], values_t[half], lam, done[half])
+                    return lam, done
+
+                lam, done = stage(moves, run, (lam, done))
+            elif turn == bits and index == 1:
+
+                def run(inputs):
+                    lam, (queries, within), levels = inputs
+                    return mix(0, queries, within, lam, levels, [])
+
+                out = stage(moves, run, (lam, done[0], first.found))
+            else:
+                lam, done = stage(moves, None, (lam, done))
+    return mix(1, *done[1], lam, second.found, [out])
 
 
 def solution(mesh):

time: 131 us -> 107 us (0.82)
  waiting for transfers between devices: 48 us -> 13.3 us
  starting transfers between devices: 15.1 us -> 24.4 us
  local copies, waits for them, and re-layouts: 7.07 us -> 2.17 us
  Pallas kernels: 53.5 us -> 57.9 us
  other arithmetic: 6.91 us -> 8.26 us
    ppermute x8 -> x16, waiting for transfers between devices: 46.4 us -> 13.3 us  [exchange(): lax.ppermute(value, 'ctx', [(to ^ away, to) for to in self.takers(bit)])]
    ppermute x8 -> x16, starting transfers between devices: 11.4 us -> 20.7 us  [exchange(): lax.ppermute(value, 'ctx', [(to ^ away, to) for to in self.takers(bit)])]
    pallas_call x6 -> x8, Pallas kernels: 53.5 us -> 57.9 us  [the longest x4 25.8 us: inside(): return list(call(projected, rim, conv_weight, keys, values_t, lam, *done))]
    unnamed x16 -> x12, local copies, waits for them, and re-layouts: 4.89 us -> 1.04 us
    convert_element_type x3 -> x6, other arithmetic: 4.66 us -> 2.61 us  [land(): self.state = total.astype(jnp.bfloat16)]
    select_n x3 -> x6, other arithmetic: 0.41 us -> 2.05 us  [land(): jnp.where(self.me >> step & 1 == 1, jnp.concatenate([came, value], 0), jn...]
    ppermute x1, waiting for transfers between devices: 1.62 us -> 0.01 us  [on_device(): lax.ppermute(projected[:, rows - taps + 1:, :], 'ctx', [(c, c + 1) for c...]
  transfers between devices with their start and end apart: 9 -> 17, of which waited for: 7 -> 10; matrix products, arithmetic and copies ran while one was open for 1% -> 4% of each run, Pallas kernels for 20% -> 39%
where the time goes in v2:
time: 107 us; the launch traced here: 106 us
  Pallas kernels  57.9 us (54%)
  starting transfers between devices  24.4 us (23%)
  waiting for transfers between devices  13.3 us (12%)
  other arithmetic  8.26 us (8%)
  local copies, waits for them, and re-layouts  2.17 us (2%)
    pallas_call x4, Pallas kernels, inside(): return list(call(projected, rim, conv_weight, keys, values_t, lam, *done))  25.8 us
    ppermute x16, starting transfers between devices, exchange(): lax.ppermute(value, 'ctx', [(to ^ away, to) for to in self.takers(bit)])  20.7 us
    pallas_call x2, Pallas kernels, states(): pl.pallas_call(functools.partial(state_kernel, dim), grid=(steps,), in_sp...  18.1 us
    pallas_call x2, Pallas kernels, mix(): pl.pallas_call(kernel, grid=(steps,), in_specs=[wide(), tall(), per_head(...  14 us
    ppermute x16, waiting for transfers between devices, exchange(): lax.ppermute(value, 'ctx', [(to ^ away, to) for to in self.takers(bit)])  13.3 us
    ppermute x1, starting transfers between devices, on_device(): lax.ppermute(projected[:, rows - taps + 1:, :], 'ctx', [(c, c + 1) for c...  3.71 us
    div x1, other arithmetic, on_device(): (level_codes * scale[:, None, None]).transpose(1, 0, 2).astype(jnp.float32)  2.79 us
    convert_element_type x6, other arithmetic, land(): self.state = total.astype(jnp.bfloat16)  2.61 us
  transfers between devices with their start and end apart: 17, of which 10 were waited for; matrix products, arithmetic and copies ran while one was open for 4% of the time, Pallas kernels for 39%

profile of v2, /device:TPU:25, one launch (start us, length us, event | category | flops | bytes accessed | tf_op | source)
XLA Modules:
  0.0 106.3 jit_solution(1502723040758004381)
XLA Ops:
  1.0 3.7 %collective-permute-start = (bf16[3,3,4096]{2,1,0:T(4,128)(2,1)S(1)}, bf16[3,3,4096]{2,1,0:T(4,128)(2,1)S(1)}, u32[]{:S(2)}, u32[]{:S(2)}) collective-permute-start(bf16[3,3,4096]{2,1,0:T(4,128)(2,1)S(1)} %slice.3), channel_id=1, source_target_pairs={{0,1},{1,2},{2,3},{3,4},{4,5},{5,6},{6,7},{7,8},{8,9},{9,10},{10,1... | collective-permute-start | bytes 221192 | tf_op jit(solution)/shard_map/ppermute | solution.py:201
  4.8 2.8 %fusion.2.refs_5_.lam_in.refs_2_ = f32[32,14,512]{2,1,0:T(8,128)} fusion(s32[14,32,512]{2,1,0:T(8,128)} %param.6, s32[14]{0:T(128)S(1)} %concatenate.51), kind=kLoop, calls=%fused_computation.3 | loop fusion | flops 688128 | bytes 1835064 | tf_op jit(solution)/shard_map/div | solution.py:206
  8.4 9.1 %states.2 = (bf16[512,2048]{1,0:T(8,128)(2,1)}, bf16[2048,512]{1,0:T(8,128)(2,1)}, bf16[16,128,128]{2,1,0:T(8,128)(2,1)}) custom-call(bf16[3,512,4096]{2,1,0:T(8,128)(2,1)} %q_in.3, bf16[3,512,4096]{2,1,0:T(8,128)(2,1)} %q_in.3, f32[3,8,4096]{2,1,0:T(8,128)} %pad_convert_fusion.k_rim.v_rim.refs_1_.q_rim, ...), custom_call_target="tpu_custom_call" | custom-call | flops 268435456 | bytes 8388608 | tf_op jit(solution)/shard_map/states/pallas_call | solution.py:232
  18.4 9.1 %states.3 = (bf16[512,2048]{1,0:T(8,128)(2,1)}, bf16[2048,512]{1,0:T(8,128)(2,1)}, bf16[16,128,128]{2,1,0:T(8,128)(2,1)}) custom-call(bf16[3,512,4096]{2,1,0:T(8,128)(2,1)} %q_in.3, bf16[3,512,4096]{2,1,0:T(8,128)(2,1)} %q_in.3, f32[3,8,4096]{2,1,0:T(8,128)} %pad_convert_fusion.k_rim.v_rim.refs_1_.q_rim, ...), custom_call_target="tpu_custom_call" | custom-call | flops 268435456 | bytes 8388608 | tf_op jit(solution)/shard_map/states/pallas_call | solution.py:232
  29.0 6.4 %inside.4 = (bf16[512,2048]{1,0:T(8,128)(2,1)}, f32[2048,512]{1,0:T(8,128)}) custom-call(bf16[3,512,4096]{2,1,0:T(8,128)(2,1)} %q_in.3, f32[3,8,4096]{2,1,0:T(8,128)} %pad_convert_fusion.k_rim.v_rim.refs_1_.q_rim, f32[3,4,4096]{2,1,0:T(4,128)} %q_taps.3, bf16[512,2048]{1,0:T(8,128)(2,1)} %get-tuple-element.152.refs_3_.k_in, ...), custom_call_target="tpu_custom_call" | custom-call | flops 2147483648 | bytes 5242880 | tf_op jit(solution)/shard_map/inside/pallas_call | solution.py:277
  36.1 1.3 %collective-permute-start.4 = (bf16[8,128,128]{2,1,0:T(8,128)(2,1)S(1)}, bf16[8,128,128]{2,1,0:T(8,128)(2,1)S(1)}, u32[]{:S(2)}, u32[]{:S(2)}) collective-permute-start(bf16[8,128,128]{2,1,0:T(8,128)(2,1)S(1)} %collective-permute-done.2), channel_id=1, source_target_pairs={{1,0},{0,1},{3,2},{2,3},{5,4},{4,5},{7,6},{6,7},{9,8},{8,9},{11,10... | collective-permute-start | bytes 786440 | tf_op jit(solution)/shard_map/ppermute | solution.py:154
  40.8 6.4 %inside.5 = (bf16[512,2048]{1,0:T(8,128)(2,1)}, f32[2048,512]{1,0:T(8,128)}) custom-call(bf16[3,512,4096]{2,1,0:T(8,128)(2,1)} %q_in.3, f32[3,8,4096]{2,1,0:T(8,128)} %pad_convert_fusion.k_rim.v_rim.refs_1_.q_rim, f32[3,4,4096]{2,1,0:T(4,128)} %q_taps.3, ...), custom_call_target="tpu_custom_call", output_to_operand_aliasing={{0}: (6, {}), {1}: (7, {})} | custom-call | flops 2147483648 | bytes 5242880 | tf_op jit(solution)/shard_map/inside/pallas_call | solution.py:277
  47.3 1.4 %collective-permute-start.7 = (bf16[8,128,128]{2,1,0:T(8,128)(2,1)S(1)}, bf16[8,128,128]{2,1,0:T(8,128)(2,1)S(1)}, u32[]{:S(2)}, u32[]{:S(2)}) collective-permute-start(bf16[8,128,128]{2,1,0:T(8,128)(2,1)S(1)} %collective-permute-done.5), channel_id=1, source_target_pairs={{1,0},{0,1},{3,2},{2,3},{5,4},{4,5},{7,6},{6,7},{9,8},{8,9},{11,10... | collective-permute-start | bytes 786440 | tf_op jit(solution)/shard_map/ppermute | solution.py:154
  48.7 1.2 %collective-permute-done.7 = bf16[8,128,128]{2,1,0:T(8,128)(2,1)S(1)} collective-permute-done((bf16[8,128,128]{2,1,0:T(8,128)(2,1)S(1)}, bf16[8,128,128]{2,1,0:T(8,128)(2,1)S(1)}, u32[]{:S(2)}, u32[]{:S(2)}) %collective-permute-start.7) | collective-permute-done | bytes 262176 | tf_op jit(solution)/shard_map/ppermute | solution.py:154
  51.6 1.4 %collective-permute-start.10 = (bf16[8,128,128]{2,1,0:T(8,128)(2,1)S(1)}, bf16[8,128,128]{2,1,0:T(8,128)(2,1)S(1)}, u32[]{:S(2)}, u32[]{:S(2)}) collective-permute-start(bf16[8,128,128]{2,1,0:T(8,128)(2,1)S(1)} %constant_dynamic-slice_fusion), channel_id=1, source_target_pairs={{4,0},{5,1},{6,2},{7,3},{0,4},{1,5},{2,6},{3,7},{12,8},{13,9},{14,... | collective-permute-start | bytes 786440 | tf_op jit(solution)/shard_map/ppermute | solution.py:154
  52.9 1.3 %collective-permute-start.9 = (bf16[4,128,128]{2,1,0:T(8,128)(2,1)S(1)}, bf16[4,128,128]{2,1,0:T(8,128)(2,1)S(1)}, u32[]{:S(2)}, u32[]{:S(2)}) collective-permute-start(bf16[4,128,128]{2,1,0:T(8,128)(2,1)S(1)} %add_convert_fusion.5), channel_id=1, source_target_pairs={{0,8},{1,9},{2,10},{3,11},{4,12},{5,13},{6,14},{7,15},{16,24},{17,... | collective-permute-start | bytes 393224 | tf_op jit(solution)/shard_map/ppermute | solution.py:154
  54.2 6.5 %inside.6 = (bf16[512,2048]{1,0:T(8,128)(2,1)}, f32[2048,512]{1,0:T(8,128)}) custom-call(bf16[3,512,4096]{2,1,0:T(8,128)(2,1)} %q_in.3, f32[3,8,4096]{2,1,0:T(8,128)} %pad_convert_fusion.k_rim.v_rim.refs_1_.q_rim, f32[3,4,4096]{2,1,0:T(4,128)} %q_taps.3, bf16[512,2048]{1,0:T(8,128)(2,1)} %get-tuple-element.199.refs_3_.k_in, ...), custom_call_target="tpu_custom_call" | custom-call | flops 2147483648 | bytes 5242880 | tf_op jit(solution)/shard_map/inside/pallas_call | solution.py:277
  60.7 2.6 %collective-permute-done.9 = bf16[4,128,128]{2,1,0:T(8,128)(2,1)S(1)} collective-permute-done((bf16[4,128,128]{2,1,0:T(8,128)(2,1)S(1)}, bf16[4,128,128]{2,1,0:T(8,128)(2,1)S(1)}, u32[]{:S(2)}, u32[]{:S(2)}) %collective-permute-start.9) | collective-permute-done | bytes 131104 | tf_op jit(solution)/shard_map/ppermute | solution.py:154
  63.3 1.2 %collective-permute-start.12 = (bf16[8,128,128]{2,1,0:T(8,128)(2,1)S(1)}, bf16[8,128,128]{2,1,0:T(8,128)(2,1)S(1)}, u32[]{:S(2)}, u32[]{:S(2)}) collective-permute-start(bf16[8,128,128]{2,1,0:T(8,128)(2,1)S(1)} %collective-permute-done.10), channel_id=1, source_target_pairs={{1,0},{0,1},{3,2},{2,3},{5,4},{4,5},{7,6},{6,7},{9,8},{8,9},{11,10... | collective-permute-start | bytes 786440 | tf_op jit(solution)/shard_map/ppermute | solution.py:154
  64.4 2.3 %collective-permute-start.11 = (bf16[4,128,128]{2,1,0:T(8,128)(2,1)S(1)}, bf16[4,128,128]{2,1,0:T(8,128)(2,1)S(1)}, u32[]{:S(2)}, u32[]{:S(2)}) collective-permute-start(bf16[4,128,128]{2,1,0:T(8,128)(2,1)S(1)} %collective-permute-done.9), channel_id=1, source_target_pairs={{10,8},{11,9},{8,10},{9,11},{14,12},{15,13},{12,14},{13,15},{26,24... | collective-permute-start | bytes 393224 | tf_op jit(solution)/shard_map/ppermute | solution.py:154
  66.7 4.7 %collective-permute-done.11 = bf16[4,128,128]{2,1,0:T(8,128)(2,1)S(1)} collective-permute-done((bf16[4,128,128]{2,1,0:T(8,128)(2,1)S(1)}, bf16[4,128,128]{2,1,0:T(8,128)(2,1)S(1)}, u32[]{:S(2)}, u32[]{:S(2)}) %collective-permute-start.11) | collective-permute-done | bytes 131104 | tf_op jit(solution)/shard_map/ppermute | solution.py:154
  71.4 2.8 %collective-permute-start.13 = (bf16[8,128,128]{2,1,0:T(8,128)(2,1)S(1)}, bf16[8,128,128]{2,1,0:T(8,128)(2,1)S(1)}, u32[]{:S(2)}, u32[]{:S(2)}) collective-permute-start(bf16[8,128,128]{2,1,0:T(8,128)(2,1)S(1)} %maximum_select_fusion.6), channel_id=1, source_target_pairs={{9,8},{8,9},{11,10},{10,11},{13,12},{12,13},{15,14},{14,15},{25,24... | collective-permute-start | bytes 786440 | tf_op jit(solution)/shard_map/ppermute | solution.py:154
  75.3 1.5 %collective-permute-start.14 = (bf16[4,128,128]{2,1,0:T(8,128)(2,1)S(1)}, bf16[4,128,128]{2,1,0:T(8,128)(2,1)S(1)}, u32[]{:S(2)}, u32[]{:S(2)}) collective-permute-start(bf16[4,128,128]{2,1,0:T(8,128)(2,1)S(1)} %add_convert_fusion.4), channel_id=1, source_target_pairs={{0,8},{1,9},{2,10},{3,11},{4,12},{5,13},{6,14},{7,15},{16,24},{17,... | collective-permute-start | bytes 393224 | tf_op jit(solution)/shard_map/ppermute | solution.py:154
  76.8 6.5 %inside.7 = (bf16[512,2048]{1,0:T(8,128)(2,1)}, f32[2048,512]{1,0:T(8,128)}) custom-call(bf16[3,512,4096]{2,1,0:T(8,128)(2,1)} %q_in.3, f32[3,8,4096]{2,1,0:T(8,128)} %pad_convert_fusion.k_rim.v_rim.refs_1_.q_rim, f32[3,4,4096]{2,1,0:T(4,128)} %q_taps.3, ...), custom_call_target="tpu_custom_call", output_to_operand_aliasing={{0}: (6, {}), {1}: (7, {})} | custom-call | flops 2147483648 | bytes 5242880 | tf_op jit(solution)/shard_map/inside/pallas_call | solution.py:277
  84.9 2.7 %collective-permute-start.15 = (bf16[4,128,128]{2,1,0:T(8,128)(2,1)S(1)}, bf16[4,128,128]{2,1,0:T(8,128)(2,1)S(1)}, u32[]{:S(2)}, u32[]{:S(2)}) collective-permute-start(bf16[4,128,128]{2,1,0:T(8,128)(2,1)S(1)} %collective-permute-done.14), channel_id=1, source_target_pairs={{10,8},{11,9},{8,10},{9,11},{14,12},{15,13},{12,14},{13,15},{26,24... | collective-permute-start | bytes 393224 | tf_op jit(solution)/shard_map/ppermute | solution.py:154
  87.6 7.0 %mix.2.refs_8_ = bf16[512,4096]{1,0:T(8,128)(2,1)} custom-call(bf16[512,2048]{1,0:T(8,128)(2,1)} %get-tuple-element.252.q_in, f32[2048,512]{1,0:T(8,128)} %get-tuple-element.253.in_in, f32[32,14,512]{2,1,0:T(8,128)} %fusion.2.refs_5_.lam_in.refs_2_, f32[1,4096]{1,0:T(1,128)} %bitcast.3, bf16[16,128,128]{2,1,0:T(8,128)(2,1)} %copy-done.3, ...), custom_call_target="tpu_custom_call" | custom-call | flops 1073741824 | bytes 8388608 | tf_op jit(solution)/shard_map/mix/pallas_call | solution.py:286
  94.6 2.7 %collective-permute-start.16 = (bf16[8,128,128]{2,1,0:T(8,128)(2,1)S(1)}, bf16[8,128,128]{2,1,0:T(8,128)(2,1)S(1)}, u32[]{:S(2)}, u32[]{:S(2)}) collective-permute-start(bf16[8,128,128]{2,1,0:T(8,128)(2,1)S(1)} %maximum_select_fusion.7), channel_id=1, source_target_pairs={{9,8},{8,9},{11,10},{10,11},{13,12},{12,13},{15,14},{14,15},{25,24... | collective-permute-start | bytes 786440 | tf_op jit(solution)/shard_map/ppermute | solution.py:154
  97.3 1.1 %collective-permute-done.16 = bf16[8,128,128]{2,1,0:T(8,128)(2,1)S(1)} collective-permute-done((bf16[8,128,128]{2,1,0:T(8,128)(2,1)S(1)}, bf16[8,128,128]{2,1,0:T(8,128)(2,1)S(1)}, u32[]{:S(2)}, u32[]{:S(2)}) %collective-permute-start.16) | collective-permute-done | bytes 262176 | tf_op jit(solution)/shard_map/ppermute | solution.py:154
  99.3 7.0 %mix.3 = bf16[512,4096]{1,0:T(8,128)(2,1)} custom-call(bf16[512,2048]{1,0:T(8,128)(2,1)} %get-tuple-element.267.refs_0_, f32[2048,512]{1,0:T(8,128)} %get-tuple-element.268.refs_1_, f32[32,14,512]{2,1,0:T(8,128)} %fusion.2.refs_5_.lam_in.refs_2_, f32[1,4096]{1,0:T(1,128)} %bitcast.4, ...), custom_call_target="tpu_custom_call", output_to_operand_aliasing={{}: (8, {})} | custom-call | flops 1073741824 | bytes 8388608 | tf_op jit(solution)/shard_map/mix/pallas_call | solution.py:286
  (50 shorter events, 13.7 us)
Async XLA Ops:
  1.0 6.6 %collective-permute-start = (bf16[3,3,4096]{2,1,0:T(4,128)(2,1)S(1)}, bf16[3,3,4096]{2,1,0:T(4,128)(2,1)S(1)}, u32[]{:S(2)}, u32[]{:S(2)}) collective-permute-start(bf16[3,3,4096]{2,1,0:T(4,128)(2,1)S(1)} %slice.3), channel_id=1, source_target_pairs={{0,1},{1,2},{2,3},{3,4},{4,5},{5,6},{6,7},{7,8},{8,9},{9,10},{10,1... | collective-permute-start | bytes 221192 | tf_op jit(solution)/shard_map/ppermute | solution.py:201
  17.5 10.0 %collective-permute-start.1 = (bf16[16,128,128]{2,1,0:T(8,128)(2,1)}, bf16[16,128,128]{2,1,0:T(8,128)(2,1)S(1)}, u32[]{:S(2)}, u32[]{:S(2)}) collective-permute-start(bf16[16,128,128]{2,1,0:T(8,128)(2,1)} %get-tuple-element.141), channel_id=1, source_target_pairs={{1,0},{0,1},{3,2},{2,3},{5,4},{4,5},{7,6},{6,7},{9,8},{8,9},{11,10... | collective-permute-start | bytes 1572872 | tf_op jit(solution)/shard_map/ppermute | solution.py:154
  18.4 9.1 %copy-start.5 = (bf16[16,128,128]{2,1,0:T(8,128)(2,1)S(1)}, bf16[16,128,128]{2,1,0:T(8,128)(2,1)}, u32[]{:S(2)}) copy-start(bf16[16,128,128]{2,1,0:T(8,128)(2,1)} %get-tuple-element.141) | copy-start | bytes 1572868
  27.4 1.2 %copy-start.4 = (bf16[16,128,128]{2,1,0:T(8,128)(2,1)S(1)}, bf16[16,128,128]{2,1,0:T(8,128)(2,1)}, u32[]{:S(2)}) copy-start(bf16[16,128,128]{2,1,0:T(8,128)(2,1)} %get-tuple-element.150) | copy-start | bytes 1572868
  27.5 8.0 %copy-start.3 = (bf16[16,128,128]{2,1,0:T(8,128)(2,1)}, bf16[16,128,128]{2,1,0:T(8,128)(2,1)S(1)}, u32[]{:S(2)}) copy-start(bf16[16,128,128]{2,1,0:T(8,128)(2,1)S(1)} %collective-permute-done.1.rest_0_) | copy-start | bytes 1572868
  28.7 7.4 %collective-permute-start.3 = (bf16[16,128,128]{2,1,0:T(8,128)(2,1)S(1)}, bf16[16,128,128]{2,1,0:T(8,128)(2,1)S(1)}, u32[]{:S(2)}, u32[]{:S(2)}) collective-permute-start(bf16[16,128,128]{2,1,0:T(8,128)(2,1)S(1)} %copy-done.4), channel_id=1, source_target_pairs={{1,0},{0,1},{3,2},{2,3},{5,4},{4,5},{7,6},{6,7},{9,8},{8,9},{11,10... | collective-permute-start | bytes 1572872 | tf_op jit(solution)/shard_map/ppermute | solution.py:154
  28.7 7.4 %collective-permute-start.2 = (bf16[8,128,128]{2,1,0:T(8,128)(2,1)S(1)}, bf16[8,128,128]{2,1,0:T(8,128)(2,1)S(1)}, u32[]{:S(2)}, u32[]{:S(2)}) collective-permute-start(bf16[8,128,128]{2,1,0:T(8,128)(2,1)S(1)} %constant_dynamic-slice_fusion.3), channel_id=1, source_target_pairs={{2,0},{3,1},{0,2},{1,3},{6,4},{7,5},{4,6},{5,7},{10,8},{11,9},{8,1... | collective-permute-start | bytes 786440 | tf_op jit(solution)/shard_map/ppermute | solution.py:154
  36.1 3.7 %copy-start.2 = (bf16[16,128,128]{2,1,0:T(8,128)(2,1)}, bf16[16,128,128]{2,1,0:T(8,128)(2,1)S(1)}, u32[]{:S(2)}) copy-start(bf16[16,128,128]{2,1,0:T(8,128)(2,1)S(1)} %collective-permute-done.3.refs_4_) | copy-start | bytes 1572868
  36.1 2.5 %collective-permute-start.4 = (bf16[8,128,128]{2,1,0:T(8,128)(2,1)S(1)}, bf16[8,128,128]{2,1,0:T(8,128)(2,1)S(1)}, u32[]{:S(2)}, u32[]{:S(2)}) collective-permute-start(bf16[8,128,128]{2,1,0:T(8,128)(2,1)S(1)} %collective-permute-done.2), channel_id=1, source_target_pairs={{1,0},{0,1},{3,2},{2,3},{5,4},{4,5},{7,6},{6,7},{9,8},{8,9},{11,10... | collective-permute-start | bytes 786440 | tf_op jit(solution)/shard_map/ppermute | solution.py:154
  39.8 7.6 %collective-permute-start.5 = (bf16[8,128,128]{2,1,0:T(8,128)(2,1)S(1)}, bf16[8,128,128]{2,1,0:T(8,128)(2,1)S(1)}, u32[]{:S(2)}, u32[]{:S(2)}) collective-permute-start(bf16[8,128,128]{2,1,0:T(8,128)(2,1)S(1)} %get-tuple-element.170), channel_id=1, source_target_pairs={{4,0},{5,1},{6,2},{7,3},{0,4},{1,5},{2,6},{3,7},{12,8},{13,9},{14,... | collective-permute-start | bytes 786440 | tf_op jit(solution)/shard_map/ppermute | solution.py:154
  40.0 7.3 %collective-permute-start.6 = (bf16[8,128,128]{2,1,0:T(8,128)(2,1)S(1)}, bf16[8,128,128]{2,1,0:T(8,128)(2,1)S(1)}, u32[]{:S(2)}, u32[]{:S(2)}) collective-permute-start(bf16[8,128,128]{2,1,0:T(8,128)(2,1)S(1)} %get-tuple-element.171), channel_id=1, source_target_pairs={{2,0},{3,1},{0,2},{1,3},{6,4},{7,5},{4,6},{5,7},{10,8},{11,9},{8,1... | collective-permute-start | bytes 786440 | tf_op jit(solution)/shard_map/ppermute | solution.py:154
  47.3 2.6 %collective-permute-start.7 = (bf16[8,128,128]{2,1,0:T(8,128)(2,1)S(1)}, bf16[8,128,128]{2,1,0:T(8,128)(2,1)S(1)}, u32[]{:S(2)}, u32[]{:S(2)}) collective-permute-start(bf16[8,128,128]{2,1,0:T(8,128)(2,1)S(1)} %collective-permute-done.5), channel_id=1, source_target_pairs={{1,0},{0,1},{3,2},{2,3},{5,4},{4,5},{7,6},{6,7},{9,8},{8,9},{11,10... | collective-permute-start | bytes 786440 | tf_op jit(solution)/shard_map/ppermute | solution.py:154
  48.7 1.5 %collective-permute-start.8 = (bf16[8,128,128]{2,1,0:T(8,128)(2,1)S(1)}, bf16[8,128,128]{2,1,0:T(8,128)(2,1)S(1)}, u32[]{:S(2)}, u32[]{:S(2)}) collective-permute-start(bf16[8,128,128]{2,1,0:T(8,128)(2,1)S(1)} %collective-permute-done.6), channel_id=1, source_target_pairs={{1,0},{0,1},{3,2},{2,3},{5,4},{4,5},{7,6},{6,7},{9,8},{8,9},{11,10... | collective-permute-start | bytes 786440 | tf_op jit(solution)/shard_map/ppermute | solution.py:154
  51.5 9.2 %copy-start.1 = (bf16[16,128,128]{2,1,0:T(8,128)(2,1)}, bf16[16,128,128]{2,1,0:T(8,128)(2,1)S(1)}, u32[]{:S(2)}) copy-start(bf16[16,128,128]{2,1,0:T(8,128)(2,1)S(1)} %maximum_select_fusion.2.rest_2_) | copy-start | bytes 1572868
  51.6 11.7 %collective-permute-start.10 = (bf16[8,128,128]{2,1,0:T(8,128)(2,1)S(1)}, bf16[8,128,128]{2,1,0:T(8,128)(2,1)S(1)}, u32[]{:S(2)}, u32[]{:S(2)}) collective-permute-start(bf16[8,128,128]{2,1,0:T(8,128)(2,1)S(1)} %constant_dynamic-slice_fusion), channel_id=1, source_target_pairs={{4,0},{5,1},{6,2},{7,3},{0,4},{1,5},{2,6},{3,7},{12,8},{13,9},{14,... | collective-permute-start | bytes 786440 | tf_op jit(solution)/shard_map/ppermute | solution.py:154
  52.9 10.3 %collective-permute-start.9 = (bf16[4,128,128]{2,1,0:T(8,128)(2,1)S(1)}, bf16[4,128,128]{2,1,0:T(8,128)(2,1)S(1)}, u32[]{:S(2)}, u32[]{:S(2)}) collective-permute-start(bf16[4,128,128]{2,1,0:T(8,128)(2,1)S(1)} %add_convert_fusion.5), channel_id=1, source_target_pairs={{0,8},{1,9},{2,10},{3,11},{4,12},{5,13},{6,14},{7,15},{16,24},{17,... | collective-permute-start | bytes 393224 | tf_op jit(solution)/shard_map/ppermute | solution.py:154
  63.3 8.1 %collective-permute-start.12 = (bf16[8,128,128]{2,1,0:T(8,128)(2,1)S(1)}, bf16[8,128,128]{2,1,0:T(8,128)(2,1)S(1)}, u32[]{:S(2)}, u32[]{:S(2)}) collective-permute-start(bf16[8,128,128]{2,1,0:T(8,128)(2,1)S(1)} %collective-permute-done.10), channel_id=1, source_target_pairs={{1,0},{0,1},{3,2},{2,3},{5,4},{4,5},{7,6},{6,7},{9,8},{8,9},{11,10... | collective-permute-start | bytes 786440 | tf_op jit(solution)/shard_map/ppermute | solution.py:154
  64.4 6.9 %collective-permute-start.11 = (bf16[4,128,128]{2,1,0:T(8,128)(2,1)S(1)}, bf16[4,128,128]{2,1,0:T(8,128)(2,1)S(1)}, u32[]{:S(2)}, u32[]{:S(2)}) collective-permute-start(bf16[4,128,128]{2,1,0:T(8,128)(2,1)S(1)} %collective-permute-done.9), channel_id=1, source_target_pairs={{10,8},{11,9},{8,10},{9,11},{14,12},{15,13},{12,14},{13,15},{26,24... | collective-permute-start | bytes 393224 | tf_op jit(solution)/shard_map/ppermute | solution.py:154
  71.4 3.9 %collective-permute-start.13 = (bf16[8,128,128]{2,1,0:T(8,128)(2,1)S(1)}, bf16[8,128,128]{2,1,0:T(8,128)(2,1)S(1)}, u32[]{:S(2)}, u32[]{:S(2)}) collective-permute-start(bf16[8,128,128]{2,1,0:T(8,128)(2,1)S(1)} %maximum_select_fusion.6), channel_id=1, source_target_pairs={{9,8},{8,9},{11,10},{10,11},{13,12},{12,13},{15,14},{14,15},{25,24... | collective-permute-start | bytes 786440 | tf_op jit(solution)/shard_map/ppermute | solution.py:154
  74.3 9.1 %copy-start = (bf16[16,128,128]{2,1,0:T(8,128)(2,1)}, bf16[16,128,128]{2,1,0:T(8,128)(2,1)S(1)}, u32[]{:S(2)}) copy-start(bf16[16,128,128]{2,1,0:T(8,128)(2,1)S(1)} %maximum_select_fusion.3.refs_6_) | copy-start | bytes 1572868
  75.3 9.5 %collective-permute-start.14 = (bf16[4,128,128]{2,1,0:T(8,128)(2,1)S(1)}, bf16[4,128,128]{2,1,0:T(8,128)(2,1)S(1)}, u32[]{:S(2)}, u32[]{:S(2)}) collective-permute-start(bf16[4,128,128]{2,1,0:T(8,128)(2,1)S(1)} %add_convert_fusion.4), channel_id=1, source_target_pairs={{0,8},{1,9},{2,10},{3,11},{4,12},{5,13},{6,14},{7,15},{16,24},{17,... | collective-permute-start | bytes 393224 | tf_op jit(solution)/shard_map/ppermute | solution.py:154
  84.9 9.7 %collective-permute-start.15 = (bf16[4,128,128]{2,1,0:T(8,128)(2,1)S(1)}, bf16[4,128,128]{2,1,0:T(8,128)(2,1)S(1)}, u32[]{:S(2)}, u32[]{:S(2)}) collective-permute-start(bf16[4,128,128]{2,1,0:T(8,128)(2,1)S(1)} %collective-permute-done.14), channel_id=1, source_target_pairs={{10,8},{11,9},{8,10},{9,11},{14,12},{15,13},{12,14},{13,15},{26,24... | collective-permute-start | bytes 393224 | tf_op jit(solution)/shard_map/ppermute | solution.py:154
  94.6 3.8 %collective-permute-start.16 = (bf16[8,128,128]{2,1,0:T(8,128)(2,1)S(1)}, bf16[8,128,128]{2,1,0:T(8,128)(2,1)S(1)}, u32[]{:S(2)}, u32[]{:S(2)}) collective-permute-start(bf16[8,128,128]{2,1,0:T(8,128)(2,1)S(1)} %maximum_select_fusion.7), channel_id=1, source_target_pairs={{9,8},{8,9},{11,10},{10,11},{13,12},{12,13},{15,14},{14,15},{25,24... | collective-permute-start | bytes 786440 | tf_op jit(solution)/shard_map/ppermute | solution.py:154

commit v3 on v2

--- a/solution.py
+++ b/solution.py
@@ -111,10 +111,12 @@
     for head in range(q_in.shape[1] // dim):
         lanes = slice(head * dim, (head + 1) * dim)
         total = in_in[lanes, :]
+        stacked = jnp.concatenate([level[head] for level in levels], 0)
+        products = lax.dot_general(
+            stacked, q_in[:, lanes], NT, preferred_element_type=jnp.float32
+        )
         for bit in range(bits):
-            product = lax.dot_general(
-                levels[bit][head], q_in[:, lanes], NT, preferred_element_type=jnp.float32
-            )
+            product = products[bit * dim : (bit + 1) * dim]
             total = total + lam_in[head, base + bit : base + bit + 1, :] * product
         inverse = lax.rsqrt(jnp.mean(total * total, 0, keepdims=True) + 1e-06)
         normed = (total * inverse).T * gain_in[0:1, lanes]
@@ -126,17 +128,7 @@
         self.count = lax.axis_size("ctx")
         self.bits = self.count.bit_length() - 1
         self.me = lax.axis_index("ctx")
-        self.state, self.got, self.found = None, None, []
-
-    def piece(self, bit):
-        depth = (bit + 1) // 2
-        if not depth:
-            return self.state
-        size = self.state.shape[0] // 2**depth
-        index = 0
-        for step in range(depth):
-            index = index + (((self.me >> step) & 1) << (depth - 1 - step))
-        return lax.dynamic_slice_in_dim(self.state, index * size, size, 0)
+        self.state, self.depth, self.got = None, 0, {}
 
     def operations(self, bit):
         return [(bit, None)] + [(bit, step) for step in reversed(range((bit + 1) // 2))]
@@ -146,7 +138,14 @@
 
     def outgoing(self, operation):
         bit, step = operation
-        return self.piece(bit) if step is None else self.got
+        if step is not None:
+            return self.got[bit]
+        while self.depth < (bit + 1) // 2:
+            size = self.state.shape[0] // 2
+            start = ((self.me >> self.depth) & 1) * size
+            self.state = lax.dynamic_slice_in_dim(self.state, start, size, 0)
+            self.depth += 1
+        return self.state
 
     def exchange(self, operation, value):
         bit, step = operation
@@ -156,18 +155,19 @@
     def land(self, operation, value, came):
         bit, step = operation
         if step is None:
-            self.got = came
+            self.got[bit] = came
+            if bit < self.bits - 1:
+                total = value.astype(jnp.float32) + came.astype(jnp.float32)
+                self.state = total.astype(jnp.bfloat16)
         else:
-            self.got = jnp.where(
+            self.got[bit] = jnp.where(
                 (self.me >> step) & 1 == 1,
                 jnp.concatenate([came, value], 0),
                 jnp.concatenate([value, came], 0),
             )
-        if operation == self.operations(bit)[-1]:
-            self.found.append(self.got)
-            if bit < self.bits - 1:
-                total = self.state.astype(jnp.float32) + self.got.astype(jnp.float32)
-                self.state = total.astype(jnp.bfloat16)
+
+    def levels(self):
+        return [self.got[bit] for bit in range(self.bits)]
 
 
 def tie(values):
@@ -182,6 +182,18 @@
     for (chain, op), value, new in zip(moves, values, came):
         chain.land(op, value, new)
     return results
+
+
+def spread(groups, rounds):
+    half = len(groups) // 2
+    early = rounds // 2
+    calls = []
+    for base, count in ((0, early), (half, rounds - early)):
+        for index in range(count):
+            start = -(-half * index // count)
+            stop = -(-half * (index + 1) // count)
+            calls.append([(base + start, stop - start)] if stop > start else [])
+    return calls
 
 
 def on_device(projected, conv_weight, level_codes, out_gain):
@@ -195,7 +207,7 @@
     me = lax.axis_index("ctx")
     group = 4
     lanes = group * dim
-    halves, parts = 2, 4
+    halves = 2
     steps = heads // group // halves
 
     rim = lax.ppermute(
@@ -249,17 +261,16 @@
             name="states",
         )(projected, projected, rim, rim, conv_weight, conv_weight)
 
-    def inside(part, rim, keys, values_t, lam, done):
-        own = steps * halves // parts
-        within = part % (parts // halves) * own
-        share = rows * rows * width // parts
+    def inside(first_group, own, rim, keys, values_t, lam, done):
+        within = first_group % steps
+        share = rows * rows * lanes * own
         call = pl.pallas_call(
             functools.partial(inside_kernel, dim)
             if done
             else lambda *refs: inside_kernel(dim, *refs[:6], None, None, *refs[6:]),
             grid=(own,),
-            in_specs=data(0, part * own)
-            + [wide(within), tall(within), per_head((level_count, rows), part * own)]
+            in_specs=data(0, first_group)
+            + [wide(within), tall(within), per_head((level_count, rows), first_group)]
             + [pl.BlockSpec(memory_space=pl.ANY)] * len(done),
             out_specs=[wide(within), tall(within)],
             out_shape=[
@@ -270,7 +281,7 @@
             input_output_aliases={6: 0, 7: 1} if done else {},
             compiler_params=limit,
             cost_estimate=pl.CostEstimate(
-                flops=8 * share, bytes_accessed=10 * rows * width // parts, transcendentals=0
+                flops=8 * share, bytes_accessed=10 * rows * lanes * own, transcendentals=0
             ),
             name="inside",
         )
@@ -312,38 +323,42 @@
     keys[1], values_t[1], second.state = stage(
         [(first, op) for op in first.operations(0)], lambda r: states(1, r), rim
     )
+    plan = {}
+    for chain, lag in ((first, 0), (second, 1)):
+        for bit in range(bits):
+            for late, op in enumerate(chain.operations(bit)):
+                plan.setdefault(bit + lag + late, []).append((chain, op))
+    rounds = max(plan)
+    ready = max(turn for turn in plan for chain, _ in plan[turn] if chain is first)
+    left = list(range(steps * halves))
+    sizes = spread(left, ready)
     done = [[], []]
-    waiting = list(range(parts))
-    for turn in range(1, bits + 1):
-        early = first.operations(turn) if turn < bits else []
-        late = second.operations(turn - 1)
-        todo = [waiting.pop(0)] if waiting else []
-        if turn == bits:
-            todo, waiting = todo + waiting, []
-        for index in range(max(len(early), len(late))):
-            moves = [(first, op) for op in early[index : index + 1]]
-            moves += [(second, op) for op in late[index : index + 1]]
-            if index == 0 and todo:
-
-                def run(inputs):
-                    lam, done = inputs
-                    done = list(done)
-                    for part in todo:
-                        half = part * halves // parts
-                        done[half] = inside(part, rim, keys[half], values_t[half], lam, done[half])
-                    return lam, done
-
-                lam, done = stage(moves, run, (lam, done))
-            elif turn == bits and index == 1:
-
-                def run(inputs):
-                    lam, (queries, within), levels = inputs
-                    return mix(0, queries, within, lam, levels, [])
-
-                out = stage(moves, run, (lam, done[0], first.found))
-            else:
-                lam, done = stage(moves, None, (lam, done))
-    return mix(1, *done[1], lam, second.found, [out])
+    for turn in range(1, rounds + 1):
+        moves = plan[turn]
+        if turn <= ready:
+            todo = sizes[turn - 1]
+
+            def run(inputs):
+                lam, done = inputs
+                done = list(done)
+                for start, own in todo:
+                    half = start // steps
+                    done[half] = inside(
+                        start, own, rim, keys[half], values_t[half], lam, done[half]
+                    )
+                return lam, done
+
+            lam, done = stage(moves, run, (lam, done))
+        elif turn == ready + 1:
+
+            def run(inputs):
+                lam, (queries, within), levels = inputs
+                return mix(0, queries, within, lam, levels, [])
+
+            out = stage(moves, run, (lam, done[0], first.levels()))
+        else:
+            out = stage(moves, None, out)
+    return mix(1, *done[1], lam, second.levels(), [out])
 
 
 def solution(mesh):

time: 107 us -> 102 us (0.953)
  waiting for transfers between devices: 13.3 us -> 6.89 us
  Pallas kernels: 57.9 us -> 60.2 us
  starting transfers between devices: 24.4 us -> 23.2 us
  other arithmetic: 8.26 us -> 9.42 us
  local copies, waits for them, and re-layouts: 2.17 us -> 1.07 us
    ppermute x16, waiting for transfers between devices: 13.3 us -> 6.89 us  [exchange(): lax.ppermute(value, 'ctx', [(to ^ away, to) for to in self.takers(bit)])]
    select_n x6 -> x8, other arithmetic: 2.05 us -> 5.43 us  [land(): jnp.where(self.me >> step & 1 == 1, jnp.concatenate([came, value], 0), jn...]
    pallas_call x4 -> x5, Pallas kernels: 25.8 us -> 28.2 us  [inside(): return list(call(projected, rim, conv_weight, keys, values_t, lam, *done))]
    convert_element_type x6 -> x5, other arithmetic: 2.61 us -> 0.39 us  [land(): self.state = total.astype(jnp.bfloat16)]
    ppermute x16, starting transfers between devices: 20.7 us -> 19.5 us  [exchange(): lax.ppermute(value, 'ctx', [(to ^ away, to) for to in self.takers(bit)])]
  transfers between devices with their start and end apart: 17 -> 17, of which waited for: 10 -> 4; matrix products, arithmetic and copies ran while one was open for 4% -> 6% of each run, Pallas kernels for 39% -> 44%
where the time goes in v3:
time: 102 us; the launch traced here: 101 us
  Pallas kernels  60.2 us (59%)
  starting transfers between devices  23.2 us (23%)
  other arithmetic  9.42 us (9%)
  waiting for transfers between devices  6.89 us (7%)
  local copies, waits for them, and re-layouts  1.07 us (1%)
    pallas_call x5, Pallas kernels, inside(): return list(call(projected, rim, conv_weight, keys, values_t, lam, *done))  28.2 us
    ppermute x16, starting transfers between devices, exchange(): lax.ppermute(value, 'ctx', [(to ^ away, to) for to in self.takers(bit)])  19.5 us
    pallas_call x2, Pallas kernels, states(): pl.pallas_call(functools.partial(state_kernel, dim), grid=(steps,), in_sp...  18.1 us
    pallas_call x2, Pallas kernels, mix(): pl.pallas_call(kernel, grid=(steps,), in_specs=[wide(), tall(), per_head(...  13.9 us
    ppermute x16, waiting for transfers between devices, exchange(): lax.ppermute(value, 'ctx', [(to ^ away, to) for to in self.takers(bit)])  6.89 us
    select_n x8, other arithmetic, land(): jnp.where(self.me >> step & 1 == 1, jnp.concatenate([came, value], 0), jn...  5.43 us
    ppermute x1, starting transfers between devices, on_device(): lax.ppermute(projected[:, rows - taps + 1:, :], 'ctx', [(c, c + 1) for c...  3.71 us
    div x1, other arithmetic, on_device(): (level_codes * scale[:, None, None]).transpose(1, 0, 2).astype(jnp.float32)  2.79 us
  transfers between devices with their start and end apart: 17, of which 4 were waited for; matrix products, arithmetic and copies ran while one was open for 6% of the time, Pallas kernels for 44%

profile of v3, /device:TPU:25, one launch (start us, length us, event | category | flops | bytes accessed | tf_op | source)
XLA Modules:
  0.0 101.0 jit_solution(6216814584484996635)
XLA Ops:
  0.0 1.0 slice.3
  1.0 3.7 %collective-permute-start = (bf16[3,3,4096]{2,1,0:T(4,128)(2,1)S(1)}, bf16[3,3,4096]{2,1,0:T(4,128)(2,1)S(1)}, u32[]{:S(2)}, u32[]{:S(2)}) collective-permute-start(bf16[3,3,4096]{2,1,0:T(4,128)(2,1)S(1)} %slice.3), channel_id=1, source_target_pairs={{0,1},{1,2},{2,3},{3,4},{4,5},{5,6},{6,7},{7,8},{8,9},{9,10},{10,1... | collective-permute-start | bytes 221192 | tf_op jit(solution)/shard_map/ppermute | solution.py:213
  4.8 2.8 %fusion.2.refs_5_.lam_in.refs_2_ = f32[32,14,512]{2,1,0:T(8,128)} fusion(s32[14,32,512]{2,1,0:T(8,128)} %param.6, s32[14]{0:T(128)S(1)} %concatenate.51), kind=kLoop, calls=%fused_computation.3 | loop fusion | flops 688128 | bytes 1835064 | tf_op jit(solution)/shard_map/div | solution.py:218
  8.4 9.1 %states.2 = (bf16[512,2048]{1,0:T(8,128)(2,1)}, bf16[2048,512]{1,0:T(8,128)(2,1)}, bf16[16,128,128]{2,1,0:T(8,128)(2,1)}) custom-call(bf16[3,512,4096]{2,1,0:T(8,128)(2,1)} %q_in.5, bf16[3,512,4096]{2,1,0:T(8,128)(2,1)} %q_in.5, f32[3,8,4096]{2,1,0:T(8,128)} %pad_convert_fusion.k_rim.v_rim.refs_1_.q_rim, ...), custom_call_target="tpu_custom_call" | custom-call | flops 268435456 | bytes 8388608 | tf_op jit(solution)/shard_map/states/pallas_call | solution.py:244
  18.4 9.0 %states.3 = (bf16[512,2048]{1,0:T(8,128)(2,1)}, bf16[2048,512]{1,0:T(8,128)(2,1)}, bf16[16,128,128]{2,1,0:T(8,128)(2,1)}) custom-call(bf16[3,512,4096]{2,1,0:T(8,128)(2,1)} %q_in.5, bf16[3,512,4096]{2,1,0:T(8,128)(2,1)} %q_in.5, f32[3,8,4096]{2,1,0:T(8,128)} %pad_convert_fusion.k_rim.v_rim.refs_1_.q_rim, ...), custom_call_target="tpu_custom_call" | custom-call | flops 268435456 | bytes 8388608 | tf_op jit(solution)/shard_map/states/pallas_call | solution.py:244
  28.0 6.5 %inside.5 = (bf16[512,2048]{1,0:T(8,128)(2,1)}, f32[2048,512]{1,0:T(8,128)}) custom-call(bf16[3,512,4096]{2,1,0:T(8,128)(2,1)} %q_in.5, f32[3,8,4096]{2,1,0:T(8,128)} %pad_convert_fusion.k_rim.v_rim.refs_1_.q_rim, f32[3,4,4096]{2,1,0:T(4,128)} %q_taps.5, bf16[512,2048]{1,0:T(8,128)(2,1)} %get-tuple-element.133.refs_3_.k_in, ...), custom_call_target="tpu_custom_call" | custom-call | flops 2147483648 | bytes 5242880 | tf_op jit(solution)/shard_map/inside/pallas_call | solution.py:288
  35.3 1.4 %collective-permute-start.4 = (bf16[8,128,128]{2,1,0:T(8,128)(2,1)S(1)}, bf16[8,128,128]{2,1,0:T(8,128)(2,1)S(1)}, u32[]{:S(2)}, u32[]{:S(2)}) collective-permute-start(bf16[8,128,128]{2,1,0:T(8,128)(2,1)S(1)} %collective-permute-done.2), channel_id=1, source_target_pairs={{1,0},{0,1},{3,2},{2,3},{5,4},{4,5},{7,6},{6,7},{9,8},{8,9},{11,10... | collective-permute-start | bytes 786440 | tf_op jit(solution)/shard_map/ppermute | solution.py:153
  37.6 6.4 %inside.6 = (bf16[512,2048]{1,0:T(8,128)(2,1)}, f32[2048,512]{1,0:T(8,128)}) custom-call(bf16[3,512,4096]{2,1,0:T(8,128)(2,1)} %q_in.5, f32[3,8,4096]{2,1,0:T(8,128)} %pad_convert_fusion.k_rim.v_rim.refs_1_.q_rim, f32[3,4,4096]{2,1,0:T(4,128)} %q_taps.5, ...), custom_call_target="tpu_custom_call", output_to_operand_aliasing={{0}: (6, {}), {1}: (7, {})} | custom-call | flops 2147483648 | bytes 5242880 | tf_op jit(solution)/shard_map/inside/pallas_call | solution.py:288
  44.6 1.2 %collective-permute-start.10 = (bf16[8,128,128]{2,1,0:T(8,128)(2,1)S(1)}, bf16[8,128,128]{2,1,0:T(8,128)(2,1)S(1)}, u32[]{:S(2)}, u32[]{:S(2)}) collective-permute-start(bf16[8,128,128]{2,1,0:T(8,128)(2,1)S(1)} %add_convert_fusion), channel_id=1, source_target_pairs={{4,0},{5,1},{6,2},{7,3},{0,4},{1,5},{2,6},{3,7},{12,8},{13,9},{14,... | collective-permute-start | bytes 786440 | tf_op jit(solution)/shard_map/ppermute | solution.py:153
  45.8 1.5 %collective-permute-start.7 = (bf16[8,128,128]{2,1,0:T(8,128)(2,1)S(1)}, bf16[8,128,128]{2,1,0:T(8,128)(2,1)S(1)}, u32[]{:S(2)}, u32[]{:S(2)}) collective-permute-start(bf16[8,128,128]{2,1,0:T(8,128)(2,1)S(1)} %collective-permute-done.5), channel_id=1, source_target_pairs={{1,0},{0,1},{3,2},{2,3},{5,4},{4,5},{7,6},{6,7},{9,8},{8,9},{11,10... | collective-permute-start | bytes 786440 | tf_op jit(solution)/shard_map/ppermute | solution.py:153
  47.3 1.3 %collective-permute-start.8 = (bf16[4,128,128]{2,1,0:T(8,128)(2,1)S(1)}, bf16[4,128,128]{2,1,0:T(8,128)(2,1)S(1)}, u32[]{:S(2)}, u32[]{:S(2)}) collective-permute-start(bf16[4,128,128]{2,1,0:T(8,128)(2,1)S(1)} %add_convert_fusion.5), channel_id=1, source_target_pairs={{0,8},{1,9},{2,10},{3,11},{4,12},{5,13},{6,14},{7,15},{16,24},{17,... | collective-permute-start | bytes 393224 | tf_op jit(solution)/shard_map/ppermute | solution.py:153
  48.6 6.4 %inside.7 = (bf16[512,2048]{1,0:T(8,128)(2,1)}, f32[2048,512]{1,0:T(8,128)}) custom-call(bf16[3,512,4096]{2,1,0:T(8,128)(2,1)} %q_in.5, f32[3,8,4096]{2,1,0:T(8,128)} %pad_convert_fusion.k_rim.v_rim.refs_1_.q_rim, f32[3,4,4096]{2,1,0:T(4,128)} %q_taps.5, bf16[512,2048]{1,0:T(8,128)(2,1)} %get-tuple-element.166.refs_3_.k_in, ...), custom_call_target="tpu_custom_call" | custom-call | flops 2147483648 | bytes 5242880 | tf_op jit(solution)/shard_map/inside/pallas_call | solution.py:288
  55.0 3.2 %collective-permute-done.8 = bf16[4,128,128]{2,1,0:T(8,128)(2,1)S(1)} collective-permute-done((bf16[4,128,128]{2,1,0:T(8,128)(2,1)S(1)}, bf16[4,128,128]{2,1,0:T(8,128)(2,1)S(1)}, u32[]{:S(2)}, u32[]{:S(2)}) %collective-permute-start.8) | collective-permute-done | bytes 131104 | tf_op jit(solution)/shard_map/ppermute | solution.py:153
  58.9 2.3 %collective-permute-start.11 = (bf16[4,128,128]{2,1,0:T(8,128)(2,1)S(1)}, bf16[4,128,128]{2,1,0:T(8,128)(2,1)S(1)}, u32[]{:S(2)}, u32[]{:S(2)}) collective-permute-start(bf16[4,128,128]{2,1,0:T(8,128)(2,1)S(1)} %collective-permute-done.8), channel_id=1, source_target_pairs={{10,8},{11,9},{8,10},{9,11},{14,12},{15,13},{12,14},{13,15},{26,24... | collective-permute-start | bytes 393224 | tf_op jit(solution)/shard_map/ppermute | solution.py:153
  61.2 1.5 %collective-permute-start.13 = (bf16[4,128,128]{2,1,0:T(8,128)(2,1)S(1)}, bf16[4,128,128]{2,1,0:T(8,128)(2,1)S(1)}, u32[]{:S(2)}, u32[]{:S(2)}) collective-permute-start(bf16[4,128,128]{2,1,0:T(8,128)(2,1)S(1)} %add_convert_fusion.4), channel_id=1, source_target_pairs={{0,8},{1,9},{2,10},{3,11},{4,12},{5,13},{6,14},{7,15},{16,24},{17,... | collective-permute-start | bytes 393224 | tf_op jit(solution)/shard_map/ppermute | solution.py:153
  62.7 4.4 %inside.8 = (bf16[512,2048]{1,0:T(8,128)(2,1)}, f32[2048,512]{1,0:T(8,128)}) custom-call(bf16[3,512,4096]{2,1,0:T(8,128)(2,1)} %q_in.5, f32[3,8,4096]{2,1,0:T(8,128)} %pad_convert_fusion.k_rim.v_rim.refs_1_.q_rim, f32[3,4,4096]{2,1,0:T(4,128)} %q_taps.5, ...), custom_call_target="tpu_custom_call", output_to_operand_aliasing={{0}: (6, {}), {1}: (7, {})} | custom-call | flops 1073741824 | bytes 2621440 | tf_op jit(solution)/shard_map/inside/pallas_call | solution.py:288
  67.0 2.6 %collective-permute-done.13 = bf16[4,128,128]{2,1,0:T(8,128)(2,1)S(1)} collective-permute-done((bf16[4,128,128]{2,1,0:T(8,128)(2,1)S(1)}, bf16[4,128,128]{2,1,0:T(8,128)(2,1)S(1)}, u32[]{:S(2)}, u32[]{:S(2)}) %collective-permute-start.13) | collective-permute-done | bytes 131104 | tf_op jit(solution)/shard_map/ppermute | solution.py:153
  69.7 2.6 %collective-permute-start.14 = (bf16[8,128,128]{2,1,0:T(8,128)(2,1)S(1)}, bf16[8,128,128]{2,1,0:T(8,128)(2,1)S(1)}, u32[]{:S(2)}, u32[]{:S(2)}) collective-permute-start(bf16[8,128,128]{2,1,0:T(8,128)(2,1)S(1)} %maximum_select_fusion.6), channel_id=1, source_target_pairs={{9,8},{8,9},{11,10},{10,11},{13,12},{12,13},{15,14},{14,15},{25,24... | collective-permute-start | bytes 786440 | tf_op jit(solution)/shard_map/ppermute | solution.py:153
  73.2 2.6 %collective-permute-start.15 = (bf16[4,128,128]{2,1,0:T(8,128)(2,1)S(1)}, bf16[4,128,128]{2,1,0:T(8,128)(2,1)S(1)}, u32[]{:S(2)}, u32[]{:S(2)}) collective-permute-start(bf16[4,128,128]{2,1,0:T(8,128)(2,1)S(1)} %collective-permute-done.13), channel_id=1, source_target_pairs={{10,8},{11,9},{8,10},{9,11},{14,12},{15,13},{12,14},{13,15},{26,24... | collective-permute-start | bytes 393224 | tf_op jit(solution)/shard_map/ppermute | solution.py:153
  76.7 4.5 %inside.9 = (bf16[512,2048]{1,0:T(8,128)(2,1)}, f32[2048,512]{1,0:T(8,128)}) custom-call(bf16[3,512,4096]{2,1,0:T(8,128)(2,1)} %q_in.5, f32[3,8,4096]{2,1,0:T(8,128)} %pad_convert_fusion.k_rim.v_rim.refs_1_.q_rim, f32[3,4,4096]{2,1,0:T(4,128)} %q_taps.5, ...), custom_call_target="tpu_custom_call", output_to_operand_aliasing={{0}: (6, {}), {1}: (7, {})} | custom-call | flops 1073741824 | bytes 2621440 | tf_op jit(solution)/shard_map/inside/pallas_call | solution.py:288
  82.1 2.2 %collective-permute-start.16 = (bf16[8,128,128]{2,1,0:T(8,128)(2,1)S(1)}, bf16[8,128,128]{2,1,0:T(8,128)(2,1)S(1)}, u32[]{:S(2)}, u32[]{:S(2)}) collective-permute-start(bf16[8,128,128]{2,1,0:T(8,128)(2,1)S(1)} %maximum_select_fusion.7), channel_id=1, source_target_pairs={{9,8},{8,9},{11,10},{10,11},{13,12},{12,13},{15,14},{14,15},{25,24... | collective-permute-start | bytes 786440 | tf_op jit(solution)/shard_map/ppermute | solution.py:153
  84.3 1.0 maximum_select_fusion.refs_5_
  86.1 7.0 %mix.2.refs_8_ = bf16[512,4096]{1,0:T(8,128)(2,1)} custom-call(bf16[512,2048]{1,0:T(8,128)(2,1)} %get-tuple-element.223.q_in, f32[2048,512]{1,0:T(8,128)} %get-tuple-element.224.in_in, f32[32,14,512]{2,1,0:T(8,128)} %fusion.2.refs_5_.lam_in.refs_2_, f32[1,4096]{1,0:T(1,128)} %bitcast.3, bf16[16,128,128]{2,1,0:T(8,128)(2,1)} %copy-done.1, ...), custom_call_target="tpu_custom_call" | custom-call | flops 1073741824 | bytes 8388608 | tf_op jit(solution)/shard_map/mix/pallas_call | solution.py:297
  94.0 7.0 %mix.3 = bf16[512,4096]{1,0:T(8,128)(2,1)} custom-call(bf16[512,2048]{1,0:T(8,128)(2,1)} %get-tuple-element.205.refs_0_, f32[2048,512]{1,0:T(8,128)} %get-tuple-element.206.refs_1_, f32[32,14,512]{2,1,0:T(8,128)} %fusion.2.refs_5_.lam_in.refs_2_, f32[1,4096]{1,0:T(1,128)} %bitcast.4, bf16[16,128,128]{2,1,0:T(8,128)(2,1)} %copy-done, ...), custom_call_target="tpu_custom_call", output_to_operand_aliasing={{}: (8, {})} | custom-call | flops 1073741824 | bytes 8388608 | tf_op jit(solution)/shard_map/mix/pallas_call | solution.py:297
  (45 shorter events, 9.7 us)
Async XLA Ops:
  1.0 6.6 %collective-permute-start = (bf16[3,3,4096]{2,1,0:T(4,128)(2,1)S(1)}, bf16[3,3,4096]{2,1,0:T(4,128)(2,1)S(1)}, u32[]{:S(2)}, u32[]{:S(2)}) collective-permute-start(bf16[3,3,4096]{2,1,0:T(4,128)(2,1)S(1)} %slice.3), channel_id=1, source_target_pairs={{0,1},{1,2},{2,3},{3,4},{4,5},{5,6},{6,7},{7,8},{8,9},{9,10},{10,1... | collective-permute-start | bytes 221192 | tf_op jit(solution)/shard_map/ppermute | solution.py:213
  17.5 9.9 %collective-permute-start.1 = (bf16[16,128,128]{2,1,0:T(8,128)(2,1)}, bf16[16,128,128]{2,1,0:T(8,128)(2,1)S(1)}, u32[]{:S(2)}, u32[]{:S(2)}) collective-permute-start(bf16[16,128,128]{2,1,0:T(8,128)(2,1)} %get-tuple-element.126), channel_id=1, source_target_pairs={{1,0},{0,1},{3,2},{2,3},{5,4},{4,5},{7,6},{6,7},{9,8},{8,9},{11,10... | collective-permute-start | bytes 1572872 | tf_op jit(solution)/shard_map/ppermute | solution.py:153
  18.4 9.1 %copy-start.3 = (bf16[16,128,128]{2,1,0:T(8,128)(2,1)S(1)}, bf16[16,128,128]{2,1,0:T(8,128)(2,1)}, u32[]{:S(2)}) copy-start(bf16[16,128,128]{2,1,0:T(8,128)(2,1)} %get-tuple-element.126) | copy-start | bytes 1572868
  27.4 7.1 %copy-start.1 = (bf16[16,128,128]{2,1,0:T(8,128)(2,1)}, bf16[16,128,128]{2,1,0:T(8,128)(2,1)S(1)}, u32[]{:S(2)}) copy-start(bf16[16,128,128]{2,1,0:T(8,128)(2,1)S(1)} %collective-permute-done.1.rest_0_) | copy-start | bytes 1572868
  27.5 7.6 %collective-permute-start.3 = (bf16[16,128,128]{2,1,0:T(8,128)(2,1)}, bf16[16,128,128]{2,1,0:T(8,128)(2,1)S(1)}, u32[]{:S(2)}, u32[]{:S(2)}) collective-permute-start(bf16[16,128,128]{2,1,0:T(8,128)(2,1)} %get-tuple-element.139), channel_id=1, source_target_pairs={{1,0},{0,1},{3,2},{2,3},{5,4},{4,5},{7,6},{6,7},{9,8},{8,9},{11,10... | collective-permute-start | bytes 1572872 | tf_op jit(solution)/shard_map/ppermute | solution.py:153
  27.6 7.5 %collective-permute-start.2 = (bf16[8,128,128]{2,1,0:T(8,128)(2,1)S(1)}, bf16[8,128,128]{2,1,0:T(8,128)(2,1)S(1)}, u32[]{:S(2)}, u32[]{:S(2)}) collective-permute-start(bf16[8,128,128]{2,1,0:T(8,128)(2,1)S(1)} %add_convert_fusion.3), channel_id=1, source_target_pairs={{2,0},{3,1},{0,2},{1,3},{6,4},{7,5},{4,6},{5,7},{10,8},{11,9},{8,1... | collective-permute-start | bytes 786440 | tf_op jit(solution)/shard_map/ppermute | solution.py:153
  28.0 7.1 %copy-start.2 = (bf16[16,128,128]{2,1,0:T(8,128)(2,1)S(1)}, bf16[16,128,128]{2,1,0:T(8,128)(2,1)}, u32[]{:S(2)}) copy-start(bf16[16,128,128]{2,1,0:T(8,128)(2,1)} %get-tuple-element.139) | copy-start | bytes 1572868
  35.1 8.9 %copy-start = (bf16[16,128,128]{2,1,0:T(8,128)(2,1)}, bf16[16,128,128]{2,1,0:T(8,128)(2,1)S(1)}, u32[]{:S(2)}) copy-start(bf16[16,128,128]{2,1,0:T(8,128)(2,1)S(1)} %collective-permute-done.3.refs_4_) | copy-start | bytes 1572868
  35.3 8.7 %collective-permute-start.4 = (bf16[8,128,128]{2,1,0:T(8,128)(2,1)S(1)}, bf16[8,128,128]{2,1,0:T(8,128)(2,1)S(1)}, u32[]{:S(2)}, u32[]{:S(2)}) collective-permute-start(bf16[8,128,128]{2,1,0:T(8,128)(2,1)S(1)} %collective-permute-done.2), channel_id=1, source_target_pairs={{1,0},{0,1},{3,2},{2,3},{5,4},{4,5},{7,6},{6,7},{9,8},{8,9},{11,10... | collective-permute-start | bytes 786440 | tf_op jit(solution)/shard_map/ppermute | solution.py:153
  36.6 7.8 %collective-permute-start.5 = (bf16[8,128,128]{2,1,0:T(8,128)(2,1)S(1)}, bf16[8,128,128]{2,1,0:T(8,128)(2,1)S(1)}, u32[]{:S(2)}, u32[]{:S(2)}) collective-permute-start(bf16[8,128,128]{2,1,0:T(8,128)(2,1)S(1)} %get-tuple-element.153), channel_id=1, source_target_pairs={{4,0},{5,1},{6,2},{7,3},{0,4},{1,5},{2,6},{3,7},{12,8},{13,9},{14,... | collective-permute-start | bytes 786440 | tf_op jit(solution)/shard_map/ppermute | solution.py:153
  36.8 7.6 %collective-permute-start.6 = (bf16[8,128,128]{2,1,0:T(8,128)(2,1)S(1)}, bf16[8,128,128]{2,1,0:T(8,128)(2,1)S(1)}, u32[]{:S(2)}, u32[]{:S(2)}) collective-permute-start(bf16[8,128,128]{2,1,0:T(8,128)(2,1)S(1)} %get-tuple-element.155), channel_id=1, source_target_pairs={{2,0},{3,1},{0,2},{1,3},{6,4},{7,5},{4,6},{5,7},{10,8},{11,9},{8,1... | collective-permute-start | bytes 786440 | tf_op jit(solution)/shard_map/ppermute | solution.py:153
  44.6 13.7 %collective-permute-start.10 = (bf16[8,128,128]{2,1,0:T(8,128)(2,1)S(1)}, bf16[8,128,128]{2,1,0:T(8,128)(2,1)S(1)}, u32[]{:S(2)}, u32[]{:S(2)}) collective-permute-start(bf16[8,128,128]{2,1,0:T(8,128)(2,1)S(1)} %add_convert_fusion), channel_id=1, source_target_pairs={{4,0},{5,1},{6,2},{7,3},{0,4},{1,5},{2,6},{3,7},{12,8},{13,9},{14,... | collective-permute-start | bytes 786440 | tf_op jit(solution)/shard_map/ppermute | solution.py:153
  45.8 12.4 %collective-permute-start.7 = (bf16[8,128,128]{2,1,0:T(8,128)(2,1)S(1)}, bf16[8,128,128]{2,1,0:T(8,128)(2,1)S(1)}, u32[]{:S(2)}, u32[]{:S(2)}) collective-permute-start(bf16[8,128,128]{2,1,0:T(8,128)(2,1)S(1)} %collective-permute-done.5), channel_id=1, source_target_pairs={{1,0},{0,1},{3,2},{2,3},{5,4},{4,5},{7,6},{6,7},{9,8},{8,9},{11,10... | collective-permute-start | bytes 786440 | tf_op jit(solution)/shard_map/ppermute | solution.py:153
  47.3 11.0 %collective-permute-start.9 = (bf16[8,128,128]{2,1,0:T(8,128)(2,1)S(1)}, bf16[8,128,128]{2,1,0:T(8,128)(2,1)S(1)}, u32[]{:S(2)}, u32[]{:S(2)}) collective-permute-start(bf16[8,128,128]{2,1,0:T(8,128)(2,1)S(1)} %collective-permute-done.6), channel_id=1, source_target_pairs={{1,0},{0,1},{3,2},{2,3},{5,4},{4,5},{7,6},{6,7},{9,8},{8,9},{11,10... | collective-permute-start | bytes 786440 | tf_op jit(solution)/shard_map/ppermute | solution.py:153
  47.3 10.9 %collective-permute-start.8 = (bf16[4,128,128]{2,1,0:T(8,128)(2,1)S(1)}, bf16[4,128,128]{2,1,0:T(8,128)(2,1)S(1)}, u32[]{:S(2)}, u32[]{:S(2)}) collective-permute-start(bf16[4,128,128]{2,1,0:T(8,128)(2,1)S(1)} %add_convert_fusion.5), channel_id=1, source_target_pairs={{0,8},{1,9},{2,10},{3,11},{4,12},{5,13},{6,14},{7,15},{16,24},{17,... | collective-permute-start | bytes 393224 | tf_op jit(solution)/shard_map/ppermute | solution.py:153
  58.3 11.3 %collective-permute-start.12 = (bf16[8,128,128]{2,1,0:T(8,128)(2,1)S(1)}, bf16[8,128,128]{2,1,0:T(8,128)(2,1)S(1)}, u32[]{:S(2)}, u32[]{:S(2)}) collective-permute-start(bf16[8,128,128]{2,1,0:T(8,128)(2,1)S(1)} %collective-permute-done.10), channel_id=1, source_target_pairs={{1,0},{0,1},{3,2},{2,3},{5,4},{4,5},{7,6},{6,7},{9,8},{8,9},{11,10... | collective-permute-start | bytes 786440 | tf_op jit(solution)/shard_map/ppermute | solution.py:153
  58.9 8.2 %collective-permute-start.11 = (bf16[4,128,128]{2,1,0:T(8,128)(2,1)S(1)}, bf16[4,128,128]{2,1,0:T(8,128)(2,1)S(1)}, u32[]{:S(2)}, u32[]{:S(2)}) collective-permute-start(bf16[4,128,128]{2,1,0:T(8,128)(2,1)S(1)} %collective-permute-done.8), channel_id=1, source_target_pairs={{10,8},{11,9},{8,10},{9,11},{14,12},{15,13},{12,14},{13,15},{26,24... | collective-permute-start | bytes 393224 | tf_op jit(solution)/shard_map/ppermute | solution.py:153
  61.2 8.4 %collective-permute-start.13 = (bf16[4,128,128]{2,1,0:T(8,128)(2,1)S(1)}, bf16[4,128,128]{2,1,0:T(8,128)(2,1)S(1)}, u32[]{:S(2)}, u32[]{:S(2)}) collective-permute-start(bf16[4,128,128]{2,1,0:T(8,128)(2,1)S(1)} %add_convert_fusion.4), channel_id=1, source_target_pairs={{0,8},{1,9},{2,10},{3,11},{4,12},{5,13},{6,14},{7,15},{16,24},{17,... | collective-permute-start | bytes 393224 | tf_op jit(solution)/shard_map/ppermute | solution.py:153
  69.7 11.5 %collective-permute-start.14 = (bf16[8,128,128]{2,1,0:T(8,128)(2,1)S(1)}, bf16[8,128,128]{2,1,0:T(8,128)(2,1)S(1)}, u32[]{:S(2)}, u32[]{:S(2)}) collective-permute-start(bf16[8,128,128]{2,1,0:T(8,128)(2,1)S(1)} %maximum_select_fusion.6), channel_id=1, source_target_pairs={{9,8},{8,9},{11,10},{10,11},{13,12},{12,13},{15,14},{14,15},{25,24... | collective-permute-start | bytes 786440 | tf_op jit(solution)/shard_map/ppermute | solution.py:153
  73.2 8.0 %collective-permute-start.15 = (bf16[4,128,128]{2,1,0:T(8,128)(2,1)S(1)}, bf16[4,128,128]{2,1,0:T(8,128)(2,1)S(1)}, u32[]{:S(2)}, u32[]{:S(2)}) collective-permute-start(bf16[4,128,128]{2,1,0:T(8,128)(2,1)S(1)} %collective-permute-done.13), channel_id=1, source_target_pairs={{10,8},{11,9},{8,10},{9,11},{14,12},{15,13},{12,14},{13,15},{26,24... | collective-permute-start | bytes 393224 | tf_op jit(solution)/shard_map/ppermute | solution.py:153
  82.1 11.0 %collective-permute-start.16 = (bf16[8,128,128]{2,1,0:T(8,128)(2,1)S(1)}, bf16[8,128,128]{2,1,0:T(8,128)(2,1)S(1)}, u32[]{:S(2)}, u32[]{:S(2)}) collective-permute-start(bf16[8,128,128]{2,1,0:T(8,128)(2,1)S(1)} %maximum_select_fusion.7), channel_id=1, source_target_pairs={{9,8},{8,9},{11,10},{10,11},{13,12},{12,13},{15,14},{14,15},{25,24... | collective-permute-start | bytes 786440 | tf_op jit(solution)/shard_map/ppermute | solution.py:153

commit v4 on v3

--- a/solution.py
+++ b/solution.py
@@ -106,16 +106,21 @@
             )
 
 
-def mix_kernel(dim, base, bits, q_in, in_in, lam_in, gain_in, *rest):
-    levels, out = rest[:bits], rest[bits]
+def mix_kernel(dim, base, depths, q_in, in_in, lam_in, gain_in, pieces, out):
+    place = pl.program_id(0)
     for head in range(q_in.shape[1] // dim):
         lanes = slice(head * dim, (head + 1) * dim)
+        chosen = []
+        for shift, refs in zip(depths, pieces):
+            value = refs[0][head]
+            for index in range(1, len(refs)):
+                value = jnp.where((place >> shift) == index, refs[index][head], value)
+            chosen.append(value)
         total = in_in[lanes, :]
-        stacked = jnp.concatenate([level[head] for level in levels], 0)
         products = lax.dot_general(
-            stacked, q_in[:, lanes], NT, preferred_element_type=jnp.float32
+            jnp.concatenate(chosen, 0), q_in[:, lanes], NT, preferred_element_type=jnp.float32
         )
-        for bit in range(bits):
+        for bit in range(len(chosen)):
             product = products[bit * dim : (bit + 1) * dim]
             total = total + lam_in[head, base + bit : base + bit + 1, :] * product
         inverse = lax.rsqrt(jnp.mean(total * total, 0, keepdims=True) + 1e-06)
@@ -124,47 +129,50 @@
 
 
 class Chain:
-    def __init__(self):
+    def __init__(self, deepest):
         self.count = lax.axis_size("ctx")
         self.bits = self.count.bit_length() - 1
         self.me = lax.axis_index("ctx")
-        self.state, self.depth, self.got = None, 0, {}
+        self.deepest = deepest
+        self.state, self.cut, self.got = None, 0, {}
+
+    def depth(self, bit):
+        return min((bit + 1) // 2, self.deepest)
 
     def operations(self, bit):
-        return [(bit, None)] + [(bit, step) for step in reversed(range((bit + 1) // 2))]
+        return [(bit, offset) for offset in range(2 ** self.depth(bit))]
 
     def takers(self, bit):
         return [to for to in range(self.count) if bit < self.bits - 1 or to >> bit & 1]
 
     def outgoing(self, operation):
-        bit, step = operation
-        if step is not None:
-            return self.got[bit]
-        while self.depth < (bit + 1) // 2:
+        bit, offset = operation
+        if offset:
+            return self.got[bit][0]
+        while self.cut < self.depth(bit):
             size = self.state.shape[0] // 2
-            start = ((self.me >> self.depth) & 1) * size
+            start = ((self.me >> self.cut) & 1) * size
             self.state = lax.dynamic_slice_in_dim(self.state, start, size, 0)
-            self.depth += 1
+            self.cut += 1
         return self.state
 
     def exchange(self, operation, value):
-        bit, step = operation
-        away = 2**bit if step is None else 2**step
+        bit, offset = operation
+        depth = self.depth(bit)
+        away = sum(2 ** (depth - 1 - step) for step in range(depth) if offset >> step & 1)
+        if not offset:
+            away = 2**bit
         return lax.ppermute(value, "ctx", [(to ^ away, to) for to in self.takers(bit)])
 
     def land(self, operation, value, came):
-        bit, step = operation
-        if step is None:
-            self.got[bit] = came
-            if bit < self.bits - 1:
-                total = value.astype(jnp.float32) + came.astype(jnp.float32)
-                self.state = total.astype(jnp.bfloat16)
-        else:
-            self.got[bit] = jnp.where(
-                (self.me >> step) & 1 == 1,
-                jnp.concatenate([came, value], 0),
-                jnp.concatenate([value, came], 0),
-            )
+        bit, offset = operation
+        if offset:
+            self.got[bit].append(came)
+            return
+        self.got[bit] = [came]
+        if bit < self.bits - 1:
+            total = value.astype(jnp.float32) + came.astype(jnp.float32)
+            self.state = total.astype(jnp.bfloat16)
 
     def levels(self):
         return [self.got[bit] for bit in range(self.bits)]
@@ -209,6 +217,9 @@
     lanes = group * dim
     halves = 2
     steps = heads // group // halves
+    deepest = steps.bit_length() - 1
+    own_bits = sum(((me >> step) & 1) << (deepest - 1 - step) for step in range(deepest))
+    order = lax.iota(jnp.int32, steps) ^ own_bits
 
     rim = lax.ppermute(
         projected[:, rows - taps + 1 :, :], "ctx", [(c, c + 1) for c in range(count - 1)]
@@ -289,25 +300,40 @@
 
     def mix(half, queries, within, lam, levels, done):
         base = half * steps
-        kernel = functools.partial(mix_kernel, dim, tok_bits + 1, bits)
-        if done:
-            kernel = lambda *refs: mix_kernel(
-                dim, tok_bits + 1, bits, *refs[: 4 + bits], refs[-1]
-            )
+        shifts = [deepest - len(pieces).bit_length() + 1 for pieces in levels]
+        flat = [piece for pieces in levels for piece in pieces]
+
+        def kernel(order, q_in, in_in, lam_in, gain_in, *rest):
+            rest = list(rest)
+            refs = [[rest.pop(0) for _ in pieces] for pieces in levels]
+            mix_kernel(
+                dim, tok_bits + 1, shifts, q_in, in_in, lam_in, gain_in, refs, rest[-1]
+            )
+
+        def piece_spec(shift):
+            return pl.BlockSpec(
+                (group, dim, dim), lambda g, order: (order[g] & (2**shift - 1), 0, 0)
+            )
+
         return pl.pallas_call(
             kernel,
-            grid=(steps,),
-            in_specs=[
-                wide(),
-                tall(),
-                per_head((level_count, rows), base),
-                pl.BlockSpec((1, lanes), lambda g: (0, g + base)),
-            ]
-            + [per_head((dim, dim))] * bits
-            + [pl.BlockSpec(memory_space=pl.ANY)] * len(done),
-            out_specs=wide(base),
+            grid_spec=pltpu.PrefetchScalarGridSpec(
+                num_scalar_prefetch=1,
+                grid=(steps,),
+                in_specs=[
+                    pl.BlockSpec((rows, lanes), lambda g, order: (0, order[g])),
+                    pl.BlockSpec((lanes, rows), lambda g, order: (order[g], 0)),
+                    pl.BlockSpec(
+                        (group, level_count, rows), lambda g, order: (order[g] + base, 0, 0)
+                    ),
+                    pl.BlockSpec((1, lanes), lambda g, order: (0, order[g] + base)),
+                ]
+                + [piece_spec(shift) for shift, pieces in zip(shifts, levels) for _ in pieces]
+                + [pl.BlockSpec(memory_space=pl.ANY)] * len(done),
+                out_specs=pl.BlockSpec((rows, lanes), lambda g, order: (0, order[g] + base)),
+            ),
             out_shape=jax.ShapeDtypeStruct((rows, width), jnp.bfloat16),
-            input_output_aliases={4 + bits: 0} if done else {},
+            input_output_aliases={5 + len(flat): 0} if done else {},
             compiler_params=limit,
             cost_estimate=pl.CostEstimate(
                 flops=2 * bits * rows * half_width * dim,
@@ -315,9 +341,9 @@
                 transcendentals=0,
             ),
             name="mix",
-        )(queries, within, lam, out_gain.reshape(1, width), *levels, *done)
-
-    first, second = Chain(), Chain()
+        )(order, queries, within, lam, out_gain.reshape(1, width), *flat, *done)
+
+    first, second = Chain(deepest), Chain(deepest)
     keys, values_t = [None] * halves, [None] * halves
     keys[0], values_t[0], first.state = states(0, rim)
     keys[1], values_t[1], second.state = stage(
@@ -326,8 +352,8 @@
     plan = {}
     for chain, lag in ((first, 0), (second, 1)):
         for bit in range(bits):
-            for late, op in enumerate(chain.operations(bit)):
-                plan.setdefault(bit + lag + late, []).append((chain, op))
+            for op in chain.operations(bit):
+                plan.setdefault(bit + lag + (op[1] > 0), []).append((chain, op))
     rounds = max(plan)
     ready = max(turn for turn in plan for chain, _ in plan[turn] if chain is first)
     left = list(range(steps * halves))

time: 102 us -> 102 us (level)
  starting transfers between devices: 23.2 us -> 29.1 us
  other arithmetic: 9.42 us -> 4.51 us
  waiting for transfers between devices: 6.89 us -> 4.13 us
  local copies, waits for them, and re-layouts: 1.07 us -> 2.42 us
    ppermute x16 -> x18, starting transfers between devices: 19.5 us -> 25.4 us  [exchange(): lax.ppermute(value, 'ctx', [(to ^ away, to) for to in self.takers(bit)])]
    select_n x8 -> x0, other arithmetic: 5.43 us -> none  [land(): jnp.where(self.me >> step & 1 == 1, jnp.concatenate([came, value], 0), jn...]
    pallas_call x2, Pallas kernels: 13.9 us -> 16.9 us  [mix(): pl.pallas_call(kernel, grid_spec=pltpu.PrefetchScalarGridSpec(num_scalar_...]
    ppermute x16 -> x18, waiting for transfers between devices: 6.89 us -> 4.13 us  [exchange(): lax.ppermute(value, 'ctx', [(to ^ away, to) for to in self.takers(bit)])]
    pallas_call x5 -> x4, Pallas kernels: 28.2 us -> 25.9 us  [inside(): return list(call(projected, rim, conv_weight, keys, values_t, lam, *done))]
    unnamed x8 -> x40, local copies, waits for them, and re-layouts: 0.02 us -> 1.37 us
  transfers between devices with their start and end apart: 17 -> 19, of which waited for: 4 -> 3; matrix products, arithmetic and copies ran while one was open for 6% -> 3% of each run, Pallas kernels for 44% -> 43%
where the time goes in v4:
time: 102 us; the launch traced here: 101 us
  Pallas kernels  60.9 us (60%)
  starting transfers between devices  29.1 us (29%)
  other arithmetic  4.51 us (4%)
  waiting for transfers between devices  4.13 us (4%)
  local copies, waits for them, and re-layouts  2.42 us (2%)
    pallas_call x4, Pallas kernels, inside(): return list(call(projected, rim, conv_weight, keys, values_t, lam, *done))  25.9 us
    ppermute x18, starting transfers between devices, exchange(): lax.ppermute(value, 'ctx', [(to ^ away, to) for to in self.takers(bit)])  25.4 us
    pallas_call x2, Pallas kernels, states(): pl.pallas_call(functools.partial(state_kernel, dim), grid=(steps,), in_sp...  18.1 us
    pallas_call x2, Pallas kernels, mix(): pl.pallas_call(kernel, grid_spec=pltpu.PrefetchScalarGridSpec(num_scalar_...  16.9 us
    ppermute x18, waiting for transfers between devices, exchange(): lax.ppermute(value, 'ctx', [(to ^ away, to) for to in self.takers(bit)])  4.13 us
    ppermute x1, starting transfers between devices, on_device(): lax.ppermute(projected[:, rows - taps + 1:, :], 'ctx', [(c, c + 1) for c...  3.71 us
    div x1, other arithmetic, on_device(): (level_codes * scale[:, None, None]).transpose(1, 0, 2).astype(jnp.float32)  2.8 us
  transfers between devices with their start and end apart: 19, of which 3 were waited for; matrix products, arithmetic and copies ran while one was open for 3% of the time, Pallas kernels for 43%

profile of v4, /device:TPU:25, one launch (start us, length us, event | category | flops | bytes accessed | tf_op | source)
XLA Modules:
  0.0 101.5 jit_solution(6393844862895845707)
XLA Ops:
  0.0 1.0 slice.3
  1.0 3.7 %collective-permute-start = (bf16[3,3,4096]{2,1,0:T(4,128)(2,1)S(1)}, bf16[3,3,4096]{2,1,0:T(4,128)(2,1)S(1)}, u32[]{:S(2)}, u32[]{:S(2)}) collective-permute-start(bf16[3,3,4096]{2,1,0:T(4,128)(2,1)S(1)} %slice.3), channel_id=1, source_target_pairs={{0,1},{1,2},{2,3},{3,4},{4,5},{5,6},{6,7},{7,8},{8,9},{9,10},{10,1... | collective-permute-start | bytes 221192 | tf_op jit(solution)/shard_map/ppermute | solution.py:224
  4.8 2.8 %fusion.2.refs_5_.lam_in = f32[32,14,512]{2,1,0:T(8,128)} fusion(s32[14,32,512]{2,1,0:T(8,128)} %param.6, s32[14]{0:T(128)S(1)} %concatenate.3), kind=kLoop, calls=%fused_computation.3 | loop fusion | flops 688128 | bytes 1835064 | tf_op jit(solution)/shard_map/div | solution.py:229
  8.4 9.1 %states.2 = (bf16[512,2048]{1,0:T(8,128)(2,1)}, bf16[2048,512]{1,0:T(8,128)(2,1)}, bf16[16,128,128]{2,1,0:T(8,128)(2,1)}) custom-call(bf16[3,512,4096]{2,1,0:T(8,128)(2,1)} %q_in.3, bf16[3,512,4096]{2,1,0:T(8,128)(2,1)} %q_in.3, f32[3,8,4096]{2,1,0:T(8,128)} %pad_convert_fusion.k_rim.v_rim.refs_1_.q_rim, ...), custom_call_target="tpu_custom_call" | custom-call | flops 268435456 | bytes 8388608 | tf_op jit(solution)/shard_map/states/pallas_call | solution.py:255
  17.5 0.9 collective-permute-start.1
  18.4 9.0 %states.3 = (bf16[512,2048]{1,0:T(8,128)(2,1)}, bf16[2048,512]{1,0:T(8,128)(2,1)}, bf16[16,128,128]{2,1,0:T(8,128)(2,1)}) custom-call(bf16[3,512,4096]{2,1,0:T(8,128)(2,1)} %q_in.3, bf16[3,512,4096]{2,1,0:T(8,128)(2,1)} %q_in.3, f32[3,8,4096]{2,1,0:T(8,128)} %pad_convert_fusion.k_rim.v_rim.refs_1_.q_rim, ...), custom_call_target="tpu_custom_call" | custom-call | flops 268435456 | bytes 8388608 | tf_op jit(solution)/shard_map/states/pallas_call | solution.py:255
  28.0 6.5 %inside.4 = (bf16[512,2048]{1,0:T(8,128)(2,1)}, f32[2048,512]{1,0:T(8,128)}) custom-call(bf16[3,512,4096]{2,1,0:T(8,128)(2,1)} %q_in.3, f32[3,8,4096]{2,1,0:T(8,128)} %pad_convert_fusion.k_rim.v_rim.refs_1_.q_rim, f32[3,4,4096]{2,1,0:T(4,128)} %q_taps.3, bf16[512,2048]{1,0:T(8,128)(2,1)} %get-tuple-element.122.refs_3_.k_in, ...), custom_call_target="tpu_custom_call" | custom-call | flops 2147483648 | bytes 5242880 | tf_op jit(solution)/shard_map/inside/pallas_call | solution.py:299
  35.3 1.4 %collective-permute-start.4 = (bf16[8,128,128]{2,1,0:T(8,128)(2,1)S(1)}, bf16[8,128,128]{2,1,0:T(8,128)(2,1)S(1)}, u32[]{:S(2)}, u32[]{:S(2)}) collective-permute-start(bf16[8,128,128]{2,1,0:T(8,128)(2,1)S(1)} %collective-permute-done.2.rest_1_), channel_id=1, source_target_pairs={{1,0},{0,1},{3,2},{2,3},{5,4},{4,5},{7,6},{6,7},{9,8},{8,9},{11,10... | collective-permute-start | bytes 786440 | tf_op jit(solution)/shard_map/ppermute | solution.py:165
  37.6 6.5 %inside.5 = (bf16[512,2048]{1,0:T(8,128)(2,1)}, f32[2048,512]{1,0:T(8,128)}) custom-call(bf16[3,512,4096]{2,1,0:T(8,128)(2,1)} %q_in.3, f32[3,8,4096]{2,1,0:T(8,128)} %pad_convert_fusion.k_rim.v_rim.refs_1_.q_rim, f32[3,4,4096]{2,1,0:T(4,128)} %q_taps.3, ...), custom_call_target="tpu_custom_call", output_to_operand_aliasing={{0}: (6, {}), {1}: (7, {})} | custom-call | flops 2147483648 | bytes 5242880 | tf_op jit(solution)/shard_map/inside/pallas_call | solution.py:299
  44.5 1.2 %collective-permute-start.10 = (bf16[8,128,128]{2,1,0:T(8,128)(2,1)S(1)}, bf16[8,128,128]{2,1,0:T(8,128)(2,1)S(1)}, u32[]{:S(2)}, u32[]{:S(2)}) collective-permute-start(bf16[8,128,128]{2,1,0:T(8,128)(2,1)S(1)} %add_convert_fusion), channel_id=1, source_target_pairs={{4,0},{5,1},{6,2},{7,3},{0,4},{1,5},{2,6},{3,7},{12,8},{13,9},{14,... | collective-permute-start | bytes 786440 | tf_op jit(solution)/shard_map/ppermute | solution.py:165
  45.8 1.5 %collective-permute-start.7 = (bf16[8,128,128]{2,1,0:T(8,128)(2,1)S(1)}, bf16[8,128,128]{2,1,0:T(8,128)(2,1)S(1)}, u32[]{:S(2)}, u32[]{:S(2)}) collective-permute-start(bf16[8,128,128]{2,1,0:T(8,128)(2,1)S(1)} %collective-permute-done.5.rest_3_), channel_id=1, source_target_pairs={{1,0},{0,1},{3,2},{2,3},{5,4},{4,5},{7,6},{6,7},{9,8},{8,9},{11,10... | collective-permute-start | bytes 786440 | tf_op jit(solution)/shard_map/ppermute | solution.py:165
  47.3 1.3 %collective-permute-start.8 = (bf16[4,128,128]{2,1,0:T(8,128)(2,1)S(1)}, bf16[4,128,128]{2,1,0:T(8,128)(2,1)S(1)}, u32[]{:S(2)}, u32[]{:S(2)}) collective-permute-start(bf16[4,128,128]{2,1,0:T(8,128)(2,1)S(1)} %add_convert_fusion.5), channel_id=1, source_target_pairs={{0,8},{1,9},{2,10},{3,11},{4,12},{5,13},{6,14},{7,15},{16,24},{17,... | collective-permute-start | bytes 393224 | tf_op jit(solution)/shard_map/ppermute | solution.py:165
  48.6 6.5 %inside.6 = (bf16[512,2048]{1,0:T(8,128)(2,1)}, f32[2048,512]{1,0:T(8,128)}) custom-call(bf16[3,512,4096]{2,1,0:T(8,128)(2,1)} %q_in.3, f32[3,8,4096]{2,1,0:T(8,128)} %pad_convert_fusion.k_rim.v_rim.refs_1_.q_rim, f32[3,4,4096]{2,1,0:T(4,128)} %q_taps.3, bf16[512,2048]{1,0:T(8,128)(2,1)} %get-tuple-element.155.refs_3_.k_in, ...), custom_call_target="tpu_custom_call" | custom-call | flops 2147483648 | bytes 5242880 | tf_op jit(solution)/shard_map/inside/pallas_call | solution.py:299
  55.1 3.2 %collective-permute-done.8.rest_5_ = bf16[4,128,128]{2,1,0:T(8,128)(2,1)S(1)} collective-permute-done((bf16[4,128,128]{2,1,0:T(8,128)(2,1)S(1)}, bf16[4,128,128]{2,1,0:T(8,128)(2,1)S(1)}, u32[]{:S(2)}, u32[]{:S(2)}) %collective-permute-start.8) | collective-permute-done | bytes 131104 | tf_op jit(solution)/shard_map/ppermute | solution.py:165
  58.9 2.3 %collective-permute-start.11 = (bf16[4,128,128]{2,1,0:T(8,128)(2,1)S(1)}, bf16[4,128,128]{2,1,0:T(8,128)(2,1)S(1)}, u32[]{:S(2)}, u32[]{:S(2)}) collective-permute-start(bf16[4,128,128]{2,1,0:T(8,128)(2,1)S(1)} %collective-permute-done.8.rest_5_), channel_id=1, source_target_pairs={{10,8},{11,9},{8,10},{9,11},{14,12},{15,13},{12,14},{13,15},{26,24... | collective-permute-start | bytes 393224 | tf_op jit(solution)/shard_map/ppermute | solution.py:165
  61.2 2.2 %collective-permute-start.12 = (bf16[4,128,128]{2,1,0:T(8,128)(2,1)S(1)}, bf16[4,128,128]{2,1,0:T(8,128)(2,1)S(1)}, u32[]{:S(2)}, u32[]{:S(2)}) collective-permute-start(bf16[4,128,128]{2,1,0:T(8,128)(2,1)S(1)} %collective-permute-done.8.rest_5_), channel_id=1, source_target_pairs={{9,8},{8,9},{11,10},{10,11},{13,12},{12,13},{15,14},{14,15},{25,24... | collective-permute-start | bytes 393224 | tf_op jit(solution)/shard_map/ppermute | solution.py:165
  63.4 3.0 %collective-permute-start.13 = (bf16[4,128,128]{2,1,0:T(8,128)(2,1)S(1)}, bf16[4,128,128]{2,1,0:T(8,128)(2,1)S(1)}, u32[]{:S(2)}, u32[]{:S(2)}) collective-permute-start(bf16[4,128,128]{2,1,0:T(8,128)(2,1)S(1)} %collective-permute-done.8.rest_5_), channel_id=1, source_target_pairs={{11,8},{10,9},{9,10},{8,11},{15,12},{14,13},{13,14},{12,15},{27,24... | collective-permute-start | bytes 393224 | tf_op jit(solution)/shard_map/ppermute | solution.py:165
  66.5 1.5 %collective-permute-start.15 = (bf16[4,128,128]{2,1,0:T(8,128)(2,1)S(1)}, bf16[4,128,128]{2,1,0:T(8,128)(2,1)S(1)}, u32[]{:S(2)}, u32[]{:S(2)}) collective-permute-start(bf16[4,128,128]{2,1,0:T(8,128)(2,1)S(1)} %add_convert_fusion.4), channel_id=1, source_target_pairs={{0,8},{1,9},{2,10},{3,11},{4,12},{5,13},{6,14},{7,15},{16,24},{17,... | collective-permute-start | bytes 393224 | tf_op jit(solution)/shard_map/ppermute | solution.py:165
  68.0 6.4 %inside.7 = (bf16[512,2048]{1,0:T(8,128)(2,1)}, f32[2048,512]{1,0:T(8,128)}) custom-call(bf16[3,512,4096]{2,1,0:T(8,128)(2,1)} %q_in.3, f32[3,8,4096]{2,1,0:T(8,128)} %pad_convert_fusion.k_rim.v_rim.refs_1_.q_rim, f32[3,4,4096]{2,1,0:T(4,128)} %q_taps.3, ...), custom_call_target="tpu_custom_call", output_to_operand_aliasing={{0}: (6, {}), {1}: (7, {})} | custom-call | flops 2147483648 | bytes 5242880 | tf_op jit(solution)/shard_map/inside/pallas_call | solution.py:299
  74.5 2.7 %collective-permute-start.16 = (bf16[4,128,128]{2,1,0:T(8,128)(2,1)S(1)}, bf16[4,128,128]{2,1,0:T(8,128)(2,1)S(1)}, u32[]{:S(2)}, u32[]{:S(2)}) collective-permute-start(bf16[4,128,128]{2,1,0:T(8,128)(2,1)S(1)} %collective-permute-done.15.rest_5_), channel_id=1, source_target_pairs={{10,8},{11,9},{8,10},{9,11},{14,12},{15,13},{12,14},{13,15},{26,24... | collective-permute-start | bytes 393224 | tf_op jit(solution)/shard_map/ppermute | solution.py:165
  77.3 2.9 %collective-permute-start.17 = (bf16[4,128,128]{2,1,0:T(8,128)(2,1)S(1)}, bf16[4,128,128]{2,1,0:T(8,128)(2,1)S(1)}, u32[]{:S(2)}, u32[]{:S(2)}) collective-permute-start(bf16[4,128,128]{2,1,0:T(8,128)(2,1)S(1)} %collective-permute-done.15.rest_5_), channel_id=1, source_target_pairs={{9,8},{8,9},{11,10},{10,11},{13,12},{12,13},{15,14},{14,15},{25,24... | collective-permute-start | bytes 393224 | tf_op jit(solution)/shard_map/ppermute | solution.py:165
  80.2 2.5 %collective-permute-start.18 = (bf16[4,128,128]{2,1,0:T(8,128)(2,1)S(1)}, bf16[4,128,128]{2,1,0:T(8,128)(2,1)S(1)}, u32[]{:S(2)}, u32[]{:S(2)}) collective-permute-start(bf16[4,128,128]{2,1,0:T(8,128)(2,1)S(1)} %collective-permute-done.15.rest_5_), channel_id=1, source_target_pairs={{11,8},{10,9},{9,10},{8,11},{15,12},{14,13},{13,14},{12,15},{27,24... | collective-permute-start | bytes 393224 | tf_op jit(solution)/shard_map/ppermute | solution.py:165
  83.2 8.5 %mix.2.rest_9_ = bf16[512,4096]{1,0:T(8,128)(2,1)} custom-call(s32[4]{0:T(128)} %iota_xor_fusion.order, bf16[512,2048]{1,0:T(8,128)(2,1)} %get-tuple-element.195.q_in, f32[2048,512]{1,0:T(8,128)} %get-tuple-element.196.in_in, f32[32,14,512]{2,1,0:T(8,128)} %fusion.2.refs_5_.lam_in, f32[1,4096]{1,0:T(1,128)} %bitcast.3, bf16[16,128,128]{2,1,0:T(8,128)(2,1)} %copy-done.1, ...), custom_call_target="tpu_custom_call" | custom-call | flops 1073741824 | bytes 8388608 | tf_op jit(solution)/shard_map/mix/pallas_call | solution.py:318
  93.0 8.4 %mix.3 = bf16[512,4096]{1,0:T(8,128)(2,1)} custom-call(s32[4]{0:T(128)} %iota_xor_fusion.order, bf16[512,2048]{1,0:T(8,128)(2,1)} %get-tuple-element.179.q_in, f32[2048,512]{1,0:T(8,128)} %get-tuple-element.180.in_in, f32[32,14,512]{2,1,0:T(8,128)} %fusion.2.refs_5_.lam_in, f32[1,4096]{1,0:T(1,128)} %bitcast.4, ...), custom_call_target="tpu_custom_call", output_to_operand_aliasing={{}: (14, {})} | custom-call | flops 1073741824 | bytes 8388608 | tf_op jit(solution)/shard_map/mix/pallas_call | solution.py:318
  (73 shorter events, 6.1 us)
Async XLA Ops:
  1.0 6.6 %collective-permute-start = (bf16[3,3,4096]{2,1,0:T(4,128)(2,1)S(1)}, bf16[3,3,4096]{2,1,0:T(4,128)(2,1)S(1)}, u32[]{:S(2)}, u32[]{:S(2)}) collective-permute-start(bf16[3,3,4096]{2,1,0:T(4,128)(2,1)S(1)} %slice.3), channel_id=1, source_target_pairs={{0,1},{1,2},{2,3},{3,4},{4,5},{5,6},{6,7},{7,8},{8,9},{9,10},{10,1... | collective-permute-start | bytes 221192 | tf_op jit(solution)/shard_map/ppermute | solution.py:224
  17.5 9.9 %collective-permute-start.1 = (bf16[16,128,128]{2,1,0:T(8,128)(2,1)}, bf16[16,128,128]{2,1,0:T(8,128)(2,1)S(1)}, u32[]{:S(2)}, u32[]{:S(2)}) collective-permute-start(bf16[16,128,128]{2,1,0:T(8,128)(2,1)} %get-tuple-element.115), channel_id=1, source_target_pairs={{1,0},{0,1},{3,2},{2,3},{5,4},{4,5},{7,6},{6,7},{9,8},{8,9},{11,10... | collective-permute-start | bytes 1572872 | tf_op jit(solution)/shard_map/ppermute | solution.py:165
  27.5 7.6 %collective-permute-start.3 = (bf16[16,128,128]{2,1,0:T(8,128)(2,1)}, bf16[16,128,128]{2,1,0:T(8,128)(2,1)S(1)}, u32[]{:S(2)}, u32[]{:S(2)}) collective-permute-start(bf16[16,128,128]{2,1,0:T(8,128)(2,1)} %get-tuple-element.128), channel_id=1, source_target_pairs={{1,0},{0,1},{3,2},{2,3},{5,4},{4,5},{7,6},{6,7},{9,8},{8,9},{11,10... | collective-permute-start | bytes 1572872 | tf_op jit(solution)/shard_map/ppermute | solution.py:165
  27.6 7.5 %collective-permute-start.2 = (bf16[8,128,128]{2,1,0:T(8,128)(2,1)S(1)}, bf16[8,128,128]{2,1,0:T(8,128)(2,1)S(1)}, u32[]{:S(2)}, u32[]{:S(2)}) collective-permute-start(bf16[8,128,128]{2,1,0:T(8,128)(2,1)S(1)} %add_convert_fusion.3), channel_id=1, source_target_pairs={{2,0},{3,1},{0,2},{1,3},{6,4},{7,5},{4,6},{5,7},{10,8},{11,9},{8,1... | collective-permute-start | bytes 786440 | tf_op jit(solution)/shard_map/ppermute | solution.py:165
  35.3 8.8 %collective-permute-start.4 = (bf16[8,128,128]{2,1,0:T(8,128)(2,1)S(1)}, bf16[8,128,128]{2,1,0:T(8,128)(2,1)S(1)}, u32[]{:S(2)}, u32[]{:S(2)}) collective-permute-start(bf16[8,128,128]{2,1,0:T(8,128)(2,1)S(1)} %collective-permute-done.2.rest_1_), channel_id=1, source_target_pairs={{1,0},{0,1},{3,2},{2,3},{5,4},{4,5},{7,6},{6,7},{9,8},{8,9},{11,10... | collective-permute-start | bytes 786440 | tf_op jit(solution)/shard_map/ppermute | solution.py:165
  36.6 7.8 %collective-permute-start.5 = (bf16[8,128,128]{2,1,0:T(8,128)(2,1)S(1)}, bf16[8,128,128]{2,1,0:T(8,128)(2,1)S(1)}, u32[]{:S(2)}, u32[]{:S(2)}) collective-permute-start(bf16[8,128,128]{2,1,0:T(8,128)(2,1)S(1)} %get-tuple-element.142), channel_id=1, source_target_pairs={{4,0},{5,1},{6,2},{7,3},{0,4},{1,5},{2,6},{3,7},{12,8},{13,9},{14,... | collective-permute-start | bytes 786440 | tf_op jit(solution)/shard_map/ppermute | solution.py:165
  36.8 7.6 %collective-permute-start.6 = (bf16[8,128,128]{2,1,0:T(8,128)(2,1)S(1)}, bf16[8,128,128]{2,1,0:T(8,128)(2,1)S(1)}, u32[]{:S(2)}, u32[]{:S(2)}) collective-permute-start(bf16[8,128,128]{2,1,0:T(8,128)(2,1)S(1)} %get-tuple-element.144), channel_id=1, source_target_pairs={{2,0},{3,1},{0,2},{1,3},{6,4},{7,5},{4,6},{5,7},{10,8},{11,9},{8,1... | collective-permute-start | bytes 786440 | tf_op jit(solution)/shard_map/ppermute | solution.py:165
  44.5 13.7 %collective-permute-start.10 = (bf16[8,128,128]{2,1,0:T(8,128)(2,1)S(1)}, bf16[8,128,128]{2,1,0:T(8,128)(2,1)S(1)}, u32[]{:S(2)}, u32[]{:S(2)}) collective-permute-start(bf16[8,128,128]{2,1,0:T(8,128)(2,1)S(1)} %add_convert_fusion), channel_id=1, source_target_pairs={{4,0},{5,1},{6,2},{7,3},{0,4},{1,5},{2,6},{3,7},{12,8},{13,9},{14,... | collective-permute-start | bytes 786440 | tf_op jit(solution)/shard_map/ppermute | solution.py:165
  45.8 12.5 %collective-permute-start.7 = (bf16[8,128,128]{2,1,0:T(8,128)(2,1)S(1)}, bf16[8,128,128]{2,1,0:T(8,128)(2,1)S(1)}, u32[]{:S(2)}, u32[]{:S(2)}) collective-permute-start(bf16[8,128,128]{2,1,0:T(8,128)(2,1)S(1)} %collective-permute-done.5.rest_3_), channel_id=1, source_target_pairs={{1,0},{0,1},{3,2},{2,3},{5,4},{4,5},{7,6},{6,7},{9,8},{8,9},{11,10... | collective-permute-start | bytes 786440 | tf_op jit(solution)/shard_map/ppermute | solution.py:165
  47.3 11.0 %collective-permute-start.9 = (bf16[8,128,128]{2,1,0:T(8,128)(2,1)S(1)}, bf16[8,128,128]{2,1,0:T(8,128)(2,1)S(1)}, u32[]{:S(2)}, u32[]{:S(2)}) collective-permute-start(bf16[8,128,128]{2,1,0:T(8,128)(2,1)S(1)} %collective-permute-done.6.rest_1_), channel_id=1, source_target_pairs={{1,0},{0,1},{3,2},{2,3},{5,4},{4,5},{7,6},{6,7},{9,8},{8,9},{11,10... | collective-permute-start | bytes 786440 | tf_op jit(solution)/shard_map/ppermute | solution.py:165
  47.3 10.9 %collective-permute-start.8 = (bf16[4,128,128]{2,1,0:T(8,128)(2,1)S(1)}, bf16[4,128,128]{2,1,0:T(8,128)(2,1)S(1)}, u32[]{:S(2)}, u32[]{:S(2)}) collective-permute-start(bf16[4,128,128]{2,1,0:T(8,128)(2,1)S(1)} %add_convert_fusion.5), channel_id=1, source_target_pairs={{0,8},{1,9},{2,10},{3,11},{4,12},{5,13},{6,14},{7,15},{16,24},{17,... | collective-permute-start | bytes 393224 | tf_op jit(solution)/shard_map/ppermute | solution.py:165
  58.2 16.2 %copy-start.10 = (bf16[4,128,128]{2,1,0:T(8,128)(2,1)}, bf16[4,128,128]{2,1,0:T(8,128)(2,1)S(1)}, u32[]{:S(2)}) copy-start(bf16[4,128,128]{2,1,0:T(8,128)(2,1)S(1)} %collective-permute-done.8.rest_5_) | copy-start | bytes 393220
  58.2 16.2 %copy-start.4 = (bf16[8,128,128]{2,1,0:T(8,128)(2,1)}, bf16[8,128,128]{2,1,0:T(8,128)(2,1)S(1)}, u32[]{:S(2)}) copy-start(bf16[8,128,128]{2,1,0:T(8,128)(2,1)S(1)} %collective-permute-done.10.rest_3_) | copy-start | bytes 786436
  58.2 16.2 %copy-start.9 = (bf16[8,128,128]{2,1,0:T(8,128)(2,1)}, bf16[8,128,128]{2,1,0:T(8,128)(2,1)S(1)}, u32[]{:S(2)}) copy-start(bf16[8,128,128]{2,1,0:T(8,128)(2,1)S(1)} %collective-permute-done.7.rest_4_) | copy-start | bytes 786436
  58.3 16.2 %collective-permute-start.14 = (bf16[8,128,128]{2,1,0:T(8,128)(2,1)S(1)}, bf16[8,128,128]{2,1,0:T(8,128)(2,1)S(1)}, u32[]{:S(2)}, u32[]{:S(2)}) collective-permute-start(bf16[8,128,128]{2,1,0:T(8,128)(2,1)S(1)} %collective-permute-done.10.rest_3_), channel_id=1, source_target_pairs={{1,0},{0,1},{3,2},{2,3},{5,4},{4,5},{7,6},{6,7},{9,8},{8,9},{11,10... | collective-permute-start | bytes 786440 | tf_op jit(solution)/shard_map/ppermute | solution.py:165
  58.9 15.6 %collective-permute-start.11 = (bf16[4,128,128]{2,1,0:T(8,128)(2,1)S(1)}, bf16[4,128,128]{2,1,0:T(8,128)(2,1)S(1)}, u32[]{:S(2)}, u32[]{:S(2)}) collective-permute-start(bf16[4,128,128]{2,1,0:T(8,128)(2,1)S(1)} %collective-permute-done.8.rest_5_), channel_id=1, source_target_pairs={{10,8},{11,9},{8,10},{9,11},{14,12},{15,13},{12,14},{13,15},{26,24... | collective-permute-start | bytes 393224 | tf_op jit(solution)/shard_map/ppermute | solution.py:165
  61.2 13.3 %collective-permute-start.12 = (bf16[4,128,128]{2,1,0:T(8,128)(2,1)S(1)}, bf16[4,128,128]{2,1,0:T(8,128)(2,1)S(1)}, u32[]{:S(2)}, u32[]{:S(2)}) collective-permute-start(bf16[4,128,128]{2,1,0:T(8,128)(2,1)S(1)} %collective-permute-done.8.rest_5_), channel_id=1, source_target_pairs={{9,8},{8,9},{11,10},{10,11},{13,12},{12,13},{15,14},{14,15},{25,24... | collective-permute-start | bytes 393224 | tf_op jit(solution)/shard_map/ppermute | solution.py:165
  63.4 11.1 %collective-permute-start.13 = (bf16[4,128,128]{2,1,0:T(8,128)(2,1)S(1)}, bf16[4,128,128]{2,1,0:T(8,128)(2,1)S(1)}, u32[]{:S(2)}, u32[]{:S(2)}) collective-permute-start(bf16[4,128,128]{2,1,0:T(8,128)(2,1)S(1)} %collective-permute-done.8.rest_5_), channel_id=1, source_target_pairs={{11,8},{10,9},{9,10},{8,11},{15,12},{14,13},{13,14},{12,15},{27,24... | collective-permute-start | bytes 393224 | tf_op jit(solution)/shard_map/ppermute | solution.py:165
  66.5 8.0 %collective-permute-start.15 = (bf16[4,128,128]{2,1,0:T(8,128)(2,1)S(1)}, bf16[4,128,128]{2,1,0:T(8,128)(2,1)S(1)}, u32[]{:S(2)}, u32[]{:S(2)}) collective-permute-start(bf16[4,128,128]{2,1,0:T(8,128)(2,1)S(1)} %add_convert_fusion.4), channel_id=1, source_target_pairs={{0,8},{1,9},{2,10},{3,11},{4,12},{5,13},{6,14},{7,15},{16,24},{17,... | collective-permute-start | bytes 393224 | tf_op jit(solution)/shard_map/ppermute | solution.py:165
  74.5 17.1 %copy-start.11 = (bf16[4,128,128]{2,1,0:T(8,128)(2,1)}, bf16[4,128,128]{2,1,0:T(8,128)(2,1)S(1)}, u32[]{:S(2)}) copy-start(bf16[4,128,128]{2,1,0:T(8,128)(2,1)S(1)} %collective-permute-done.15.rest_5_) | copy-start | bytes 393220
  74.5 17.1 %copy-start.7 = (bf16[8,128,128]{2,1,0:T(8,128)(2,1)}, bf16[8,128,128]{2,1,0:T(8,128)(2,1)S(1)}, u32[]{:S(2)}) copy-start(bf16[8,128,128]{2,1,0:T(8,128)(2,1)S(1)} %collective-permute-done.14.rest_4_) | copy-start | bytes 786436
  74.5 17.1 %collective-permute-start.16 = (bf16[4,128,128]{2,1,0:T(8,128)(2,1)S(1)}, bf16[4,128,128]{2,1,0:T(8,128)(2,1)S(1)}, u32[]{:S(2)}, u32[]{:S(2)}) collective-permute-start(bf16[4,128,128]{2,1,0:T(8,128)(2,1)S(1)} %collective-permute-done.15.rest_5_), channel_id=1, source_target_pairs={{10,8},{11,9},{8,10},{9,11},{14,12},{15,13},{12,14},{13,15},{26,24... | collective-permute-start | bytes 393224 | tf_op jit(solution)/shard_map/ppermute | solution.py:165
  77.3 14.4 %collective-permute-start.17 = (bf16[4,128,128]{2,1,0:T(8,128)(2,1)S(1)}, bf16[4,128,128]{2,1,0:T(8,128)(2,1)S(1)}, u32[]{:S(2)}, u32[]{:S(2)}) collective-permute-start(bf16[4,128,128]{2,1,0:T(8,128)(2,1)S(1)} %collective-permute-done.15.rest_5_), channel_id=1, source_target_pairs={{9,8},{8,9},{11,10},{10,11},{13,12},{12,13},{15,14},{14,15},{25,24... | collective-permute-start | bytes 393224 | tf_op jit(solution)/shard_map/ppermute | solution.py:165
  80.2 11.5 %collective-permute-start.18 = (bf16[4,128,128]{2,1,0:T(8,128)(2,1)S(1)}, bf16[4,128,128]{2,1,0:T(8,128)(2,1)S(1)}, u32[]{:S(2)}, u32[]{:S(2)}) collective-permute-start(bf16[4,128,128]{2,1,0:T(8,128)(2,1)S(1)} %collective-permute-done.15.rest_5_), channel_id=1, source_target_pairs={{11,8},{10,9},{9,10},{8,11},{15,12},{14,13},{13,14},{12,15},{27,24... | collective-permute-start | bytes 393224 | tf_op jit(solution)/shard_map/ppermute | solution.py:165
  (15 other events, 117.7 us)

commit v5 on v4

--- a/solution.py
+++ b/solution.py
@@ -15,7 +15,7 @@
 def convolve(data_ref, rim_ref, taps_ref, held):
     rows = data_ref.shape[1]
     taps = taps_ref.shape[1]
-    held[0:PAD, :] = rim_ref[0]
+    held[PAD - taps + 1 : PAD, :] = rim_ref[0].astype(jnp.float32)
     held[PAD : PAD + rows, :] = data_ref[0].astype(jnp.float32)
     total = taps_ref[0, 0:1, :] * held[PAD - taps + 1 : PAD - taps + 1 + rows, :]
     for tap in range(1, taps):
@@ -137,7 +137,7 @@
         self.state, self.cut, self.got = None, 0, {}
 
     def depth(self, bit):
-        return min((bit + 1) // 2, self.deepest)
+        return min((bit + 1) // 2, self.deepest, 1)
 
     def operations(self, bit):
         return [(bit, offset) for offset in range(2 ** self.depth(bit))]
@@ -228,12 +228,11 @@
     scale = jnp.concatenate([jnp.ones((tok_bits + 1,), jnp.int32), on_bit])
     lam = (level_codes * scale[:, None, None]).transpose(1, 0, 2).astype(jnp.float32) / 8.0
     rim, lam = tie((rim, lam))
-    rim = jnp.pad(rim.astype(jnp.float32), ((0, 0), (PAD - taps + 1, 0), (0, 0)))
 
     def data(kind, base):
         return [
             pl.BlockSpec((1, rows, lanes), lambda g: (kind, 0, g + base)),
-            pl.BlockSpec((1, PAD, lanes), lambda g: (kind, 0, g + base)),
+            pl.BlockSpec((1, taps - 1, lanes), lambda g: (kind, 0, g + base)),
             pl.BlockSpec((1, taps, lanes), lambda g: (kind, 0, g + base)),
         ]
 

time: 102 us -> 97.8 us (0.959)
  starting transfers between devices: 29.1 us -> 18.6 us
  waiting for transfers between devices: 4.13 us -> 12.1 us
    ppermute x18 -> x14, starting transfers between devices: 25.4 us -> 14.9 us  [exchange(): lax.ppermute(value, 'ctx', [(to ^ away, to) for to in self.takers(bit)])]
    ppermute x18 -> x14, waiting for transfers between devices: 4.13 us -> 12.1 us  [exchange(): lax.ppermute(value, 'ctx', [(to ^ away, to) for to in self.takers(bit)])]
  transfers between devices with their start and end apart: 19 -> 15, of which waited for: 3 -> 4; matrix products, arithmetic and copies ran while one was open for 3% -> 3% of each run, Pallas kernels for 43% -> 44%
where the time goes in v5:
time: 97.8 us; the launch traced here: 97.3 us
  Pallas kernels  60.2 us (62%)
  starting transfers between devices  18.6 us (19%)
  waiting for transfers between devices  12.1 us (12%)
  other arithmetic  3.73 us (4%)
  local copies, waits for them, and re-layouts  2.44 us (2%)
    pallas_call x4, Pallas kernels, inside(): return list(call(projected, rim, conv_weight, keys, values_t, lam, *done))  25.8 us
    pallas_call x2, Pallas kernels, states(): pl.pallas_call(functools.partial(state_kernel, dim), grid=(steps,), in_sp...  18.2 us
    pallas_call x2, Pallas kernels, mix(): pl.pallas_call(kernel, grid_spec=pltpu.PrefetchScalarGridSpec(num_scalar_...  16.2 us
    ppermute x14, starting transfers between devices, exchange(): lax.ppermute(value, 'ctx', [(to ^ away, to) for to in self.takers(bit)])  14.9 us
    ppermute x14, waiting for transfers between devices, exchange(): lax.ppermute(value, 'ctx', [(to ^ away, to) for to in self.takers(bit)])  12.1 us
    ppermute x1, starting transfers between devices, on_device(): lax.ppermute(projected[:, rows - taps + 1:, :], 'ctx', [(c, c + 1) for c...  3.71 us
    div x1, other arithmetic, on_device(): (level_codes * scale[:, None, None]).transpose(1, 0, 2).astype(jnp.float32)  2.76 us
  transfers between devices with their start and end apart: 15, of which 4 were waited for; matrix products, arithmetic and copies ran while one was open for 3% of the time, Pallas kernels for 44%

profile of v5, /device:TPU:25, one launch (start us, length us, event | category | flops | bytes accessed | tf_op | source)
XLA Modules:
  0.0 97.3 jit_solution(16616182465841884799)
XLA Ops:
  0.0 1.0 %slice.3 = bf16[3,3,4096]{2,1,0:T(4,128)(2,1)S(1)} slice(bf16[3,512,4096]{2,1,0:T(8,128)(2,1)} %q_in.3), slice={[0:3], [509:512], [0:4096]} | slice | bytes 147456 | tf_op jit(solution)/shard_map/slice | solution.py:225
  1.0 3.7 %collective-permute-start = (bf16[3,3,4096]{2,1,0:T(4,128)(2,1)S(1)}, bf16[3,3,4096]{2,1,0:T(4,128)(2,1)S(1)}, u32[]{:S(2)}, u32[]{:S(2)}) collective-permute-start(bf16[3,3,4096]{2,1,0:T(4,128)(2,1)S(1)} %slice.3), channel_id=1, source_target_pairs={{0,1},{1,2},{2,3},{3,4},{4,5},{5,6},{6,7},{7,8},{8,9},{9,10},{10,1... | collective-permute-start | bytes 221192 | tf_op jit(solution)/shard_map/ppermute | solution.py:224
  4.8 2.8 %fusion.2.refs_5_.lam_in = f32[32,14,512]{2,1,0:T(8,128)} fusion(s32[14,32,512]{2,1,0:T(8,128)} %param.6, s32[14]{0:T(128)S(1)} %concatenate.3), kind=kLoop, calls=%fused_computation.3 | loop fusion | flops 688128 | bytes 1835064 | tf_op jit(solution)/shard_map/div | solution.py:229
  7.6 0.6 copy-done
  8.2 9.1 %states.2 = (bf16[512,2048]{1,0:T(8,128)(2,1)}, bf16[2048,512]{1,0:T(8,128)(2,1)}, bf16[16,128,128]{2,1,0:T(8,128)(2,1)}) custom-call(bf16[3,512,4096]{2,1,0:T(8,128)(2,1)} %q_in.3, bf16[3,512,4096]{2,1,0:T(8,128)(2,1)} %q_in.3, bf16[3,3,4096]{2,1,0:T(4,128)(2,1)} %copy-done, bf16[3,3,4096]{2,1,0:T(4,128)(2,1)} %copy-done, f32[3,4,4096]{2,1,0:T(4,128)} %q_taps.3, ...), custom_call_target="tpu_custom_call" | custom-call | flops 268435456 | bytes 8388608 | tf_op jit(solution)/shard_map/states/pallas_call | solution.py:254
  17.3 0.9 collective-permute-start.1
  18.3 9.1 %states.3 = (bf16[512,2048]{1,0:T(8,128)(2,1)}, bf16[2048,512]{1,0:T(8,128)(2,1)}, bf16[16,128,128]{2,1,0:T(8,128)(2,1)}) custom-call(bf16[3,512,4096]{2,1,0:T(8,128)(2,1)} %q_in.3, bf16[3,512,4096]{2,1,0:T(8,128)(2,1)} %q_in.3, bf16[3,3,4096]{2,1,0:T(4,128)(2,1)} %copy-done, bf16[3,3,4096]{2,1,0:T(4,128)(2,1)} %copy-done, f32[3,4,4096]{2,1,0:T(4,128)} %q_taps.3, ...), custom_call_target="tpu_custom_call" | custom-call | flops 268435456 | bytes 8388608 | tf_op jit(solution)/shard_map/states/pallas_call | solution.py:254
  27.9 6.5 %inside.4 = (bf16[512,2048]{1,0:T(8,128)(2,1)}, f32[2048,512]{1,0:T(8,128)}) custom-call(bf16[3,512,4096]{2,1,0:T(8,128)(2,1)} %q_in.3, bf16[3,3,4096]{2,1,0:T(4,128)(2,1)} %copy-done, f32[3,4,4096]{2,1,0:T(4,128)} %q_taps.3, bf16[512,2048]{1,0:T(8,128)(2,1)} %get-tuple-element.112.refs_3_.k_in, bf16[2048,512]{1,0:T(8,128)(2,1)} %get-tuple-element.113.refs_4_.vt_in, ...), custom_call_target="tpu_custom_call" | custom-call | flops 2147483648 | bytes 5242880 | tf_op jit(solution)/shard_map/inside/pallas_call | solution.py:298
  35.2 1.4 %collective-permute-start.4 = (bf16[8,128,128]{2,1,0:T(8,128)(2,1)S(1)}, bf16[8,128,128]{2,1,0:T(8,128)(2,1)S(1)}, u32[]{:S(2)}, u32[]{:S(2)}) collective-permute-start(bf16[8,128,128]{2,1,0:T(8,128)(2,1)S(1)} %collective-permute-done.2.rest_1_), channel_id=1, source_target_pairs={{1,0},{0,1},{3,2},{2,3},{5,4},{4,5},{7,6},{6,7},{9,8},{8,9},{11,10... | collective-permute-start | bytes 786440 | tf_op jit(solution)/shard_map/ppermute | solution.py:165
  36.7 0.7 collective-permute-start.6
  37.4 6.5 %inside.5 = (bf16[512,2048]{1,0:T(8,128)(2,1)}, f32[2048,512]{1,0:T(8,128)}) custom-call(bf16[3,512,4096]{2,1,0:T(8,128)(2,1)} %q_in.3, bf16[3,3,4096]{2,1,0:T(4,128)(2,1)} %copy-done, f32[3,4,4096]{2,1,0:T(4,128)} %q_taps.3, bf16[512,2048]{1,0:T(8,128)(2,1)} %get-tuple-element.112.refs_3_.k_in, ...), custom_call_target="tpu_custom_call", output_to_operand_aliasing={{0}: (6, {}), {1}: (7, {})} | custom-call | flops 2147483648 | bytes 5242880 | tf_op jit(solution)/shard_map/inside/pallas_call | solution.py:298
  44.5 1.2 %collective-permute-start.10 = (bf16[8,128,128]{2,1,0:T(8,128)(2,1)S(1)}, bf16[8,128,128]{2,1,0:T(8,128)(2,1)S(1)}, u32[]{:S(2)}, u32[]{:S(2)}) collective-permute-start(bf16[8,128,128]{2,1,0:T(8,128)(2,1)S(1)} %add_convert_fusion.1), channel_id=1, source_target_pairs={{4,0},{5,1},{6,2},{7,3},{0,4},{1,5},{2,6},{3,7},{12,8},{13,9},{14,... | collective-permute-start | bytes 786440 | tf_op jit(solution)/shard_map/ppermute | solution.py:165
  45.7 1.5 %collective-permute-start.7 = (bf16[8,128,128]{2,1,0:T(8,128)(2,1)S(1)}, bf16[8,128,128]{2,1,0:T(8,128)(2,1)S(1)}, u32[]{:S(2)}, u32[]{:S(2)}) collective-permute-start(bf16[8,128,128]{2,1,0:T(8,128)(2,1)S(1)} %collective-permute-done.5.rest_3_), channel_id=1, source_target_pairs={{1,0},{0,1},{3,2},{2,3},{5,4},{4,5},{7,6},{6,7},{9,8},{8,9},{11,10... | collective-permute-start | bytes 786440 | tf_op jit(solution)/shard_map/ppermute | solution.py:165
  47.2 1.3 %collective-permute-start.8 = (bf16[8,128,128]{2,1,0:T(8,128)(2,1)S(1)}, bf16[8,128,128]{2,1,0:T(8,128)(2,1)S(1)}, u32[]{:S(2)}, u32[]{:S(2)}) collective-permute-start(bf16[8,128,128]{2,1,0:T(8,128)(2,1)S(1)} %add_convert_fusion.2), channel_id=1, source_target_pairs={{0,8},{1,9},{2,10},{3,11},{4,12},{5,13},{6,14},{7,15},{16,24},{17,... | collective-permute-start | bytes 786440 | tf_op jit(solution)/shard_map/ppermute | solution.py:165
  48.6 6.4 %inside.6 = (bf16[512,2048]{1,0:T(8,128)(2,1)}, f32[2048,512]{1,0:T(8,128)}) custom-call(bf16[3,512,4096]{2,1,0:T(8,128)(2,1)} %q_in.3, bf16[3,3,4096]{2,1,0:T(4,128)(2,1)} %copy-done, f32[3,4,4096]{2,1,0:T(4,128)} %q_taps.3, bf16[512,2048]{1,0:T(8,128)(2,1)} %get-tuple-element.145.refs_3_.k_in, bf16[2048,512]{1,0:T(8,128)(2,1)} %get-tuple-element.146.refs_4_.vt_in, ...), custom_call_target="tpu_custom_call" | custom-call | flops 2147483648 | bytes 5242880 | tf_op jit(solution)/shard_map/inside/pallas_call | solution.py:298
  55.1 8.7 %collective-permute-done.8.rest_5_ = bf16[8,128,128]{2,1,0:T(8,128)(2,1)S(1)} collective-permute-done((bf16[8,128,128]{2,1,0:T(8,128)(2,1)S(1)}, bf16[8,128,128]{2,1,0:T(8,128)(2,1)S(1)}, u32[]{:S(2)}, u32[]{:S(2)}) %collective-permute-start.8) | collective-permute-done | bytes 262176 | tf_op jit(solution)/shard_map/ppermute | solution.py:165
  63.9 2.3 %collective-permute-start.11 = (bf16[8,128,128]{2,1,0:T(8,128)(2,1)S(1)}, bf16[8,128,128]{2,1,0:T(8,128)(2,1)S(1)}, u32[]{:S(2)}, u32[]{:S(2)}) collective-permute-start(bf16[8,128,128]{2,1,0:T(8,128)(2,1)S(1)} %collective-permute-done.8.rest_5_), channel_id=1, source_target_pairs={{9,8},{8,9},{11,10},{10,11},{13,12},{12,13},{15,14},{14,15},{25,24... | collective-permute-start | bytes 786440 | tf_op jit(solution)/shard_map/ppermute | solution.py:165
  66.4 1.5 %collective-permute-start.13 = (bf16[8,128,128]{2,1,0:T(8,128)(2,1)S(1)}, bf16[8,128,128]{2,1,0:T(8,128)(2,1)S(1)}, u32[]{:S(2)}, u32[]{:S(2)}) collective-permute-start(bf16[8,128,128]{2,1,0:T(8,128)(2,1)S(1)} %add_convert_fusion), channel_id=1, source_target_pairs={{0,8},{1,9},{2,10},{3,11},{4,12},{5,13},{6,14},{7,15},{16,24},{17,... | collective-permute-start | bytes 786440 | tf_op jit(solution)/shard_map/ppermute | solution.py:165
  67.9 6.4 %inside.7 = (bf16[512,2048]{1,0:T(8,128)(2,1)}, f32[2048,512]{1,0:T(8,128)}) custom-call(bf16[3,512,4096]{2,1,0:T(8,128)(2,1)} %q_in.3, bf16[3,3,4096]{2,1,0:T(4,128)(2,1)} %copy-done, f32[3,4,4096]{2,1,0:T(4,128)} %q_taps.3, bf16[512,2048]{1,0:T(8,128)(2,1)} %get-tuple-element.145.refs_3_.k_in, ...), custom_call_target="tpu_custom_call", output_to_operand_aliasing={{0}: (6, {}), {1}: (7, {})} | custom-call | flops 2147483648 | bytes 5242880 | tf_op jit(solution)/shard_map/inside/pallas_call | solution.py:298
  74.4 2.3 %collective-permute-done.13.rest_5_ = bf16[8,128,128]{2,1,0:T(8,128)(2,1)S(1)} collective-permute-done((bf16[8,128,128]{2,1,0:T(8,128)(2,1)S(1)}, bf16[8,128,128]{2,1,0:T(8,128)(2,1)S(1)}, u32[]{:S(2)}, u32[]{:S(2)}) %collective-permute-start.13) | collective-permute-done | bytes 262176 | tf_op jit(solution)/shard_map/ppermute | solution.py:165
  76.7 3.1 %collective-permute-start.14 = (bf16[8,128,128]{2,1,0:T(8,128)(2,1)S(1)}, bf16[8,128,128]{2,1,0:T(8,128)(2,1)S(1)}, u32[]{:S(2)}, u32[]{:S(2)}) collective-permute-start(bf16[8,128,128]{2,1,0:T(8,128)(2,1)S(1)} %collective-permute-done.13.rest_5_), channel_id=1, source_target_pairs={{9,8},{8,9},{11,10},{10,11},{13,12},{12,13},{15,14},{14,15},{25,24... | collective-permute-start | bytes 786440 | tf_op jit(solution)/shard_map/ppermute | solution.py:165
  80.4 8.1 %mix.2.rest_7_ = bf16[512,4096]{1,0:T(8,128)(2,1)} custom-call(s32[4]{0:T(128)} %iota_xor_fusion.order, bf16[512,2048]{1,0:T(8,128)(2,1)} %get-tuple-element.179.q_in, f32[2048,512]{1,0:T(8,128)} %get-tuple-element.180.in_in, f32[32,14,512]{2,1,0:T(8,128)} %fusion.2.refs_5_.lam_in, f32[1,4096]{1,0:T(1,128)} %bitcast.3, bf16[16,128,128]{2,1,0:T(8,128)(2,1)} %copy-done.2, ...), custom_call_target="tpu_custom_call" | custom-call | flops 1073741824 | bytes 8388608 | tf_op jit(solution)/shard_map/mix/pallas_call | solution.py:317
  88.5 0.7 copy-done.10
  89.2 8.1 %mix.3 = bf16[512,4096]{1,0:T(8,128)(2,1)} custom-call(s32[4]{0:T(128)} %iota_xor_fusion.order, bf16[512,2048]{1,0:T(8,128)(2,1)} %get-tuple-element.167.q_in, f32[2048,512]{1,0:T(8,128)} %get-tuple-element.168.in_in, f32[32,14,512]{2,1,0:T(8,128)} %fusion.2.refs_5_.lam_in, f32[1,4096]{1,0:T(1,128)} %bitcast.4, ...), custom_call_target="tpu_custom_call", output_to_operand_aliasing={{}: (12, {})} | custom-call | flops 1073741824 | bytes 8388608 | tf_op jit(solution)/shard_map/mix/pallas_call | solution.py:317
  (58 shorter events, 3.0 us)
Async XLA Ops:
  1.0 6.6 %collective-permute-start = (bf16[3,3,4096]{2,1,0:T(4,128)(2,1)S(1)}, bf16[3,3,4096]{2,1,0:T(4,128)(2,1)S(1)}, u32[]{:S(2)}, u32[]{:S(2)}) collective-permute-start(bf16[3,3,4096]{2,1,0:T(4,128)(2,1)S(1)} %slice.3), channel_id=1, source_target_pairs={{0,1},{1,2},{2,3},{3,4},{4,5},{5,6},{6,7},{7,8},{8,9},{9,10},{10,1... | collective-permute-start | bytes 221192 | tf_op jit(solution)/shard_map/ppermute | solution.py:224
  17.3 10.0 %collective-permute-start.1 = (bf16[16,128,128]{2,1,0:T(8,128)(2,1)}, bf16[16,128,128]{2,1,0:T(8,128)(2,1)S(1)}, u32[]{:S(2)}, u32[]{:S(2)}) collective-permute-start(bf16[16,128,128]{2,1,0:T(8,128)(2,1)} %get-tuple-element.105), channel_id=1, source_target_pairs={{1,0},{0,1},{3,2},{2,3},{5,4},{4,5},{7,6},{6,7},{9,8},{8,9},{11,10... | collective-permute-start | bytes 1572872 | tf_op jit(solution)/shard_map/ppermute | solution.py:165
  27.4 7.6 %collective-permute-start.3 = (bf16[16,128,128]{2,1,0:T(8,128)(2,1)}, bf16[16,128,128]{2,1,0:T(8,128)(2,1)S(1)}, u32[]{:S(2)}, u32[]{:S(2)}) collective-permute-start(bf16[16,128,128]{2,1,0:T(8,128)(2,1)} %get-tuple-element.118), channel_id=1, source_target_pairs={{1,0},{0,1},{3,2},{2,3},{5,4},{4,5},{7,6},{6,7},{9,8},{8,9},{11,10... | collective-permute-start | bytes 1572872 | tf_op jit(solution)/shard_map/ppermute | solution.py:165
  27.5 7.5 %collective-permute-start.2 = (bf16[8,128,128]{2,1,0:T(8,128)(2,1)S(1)}, bf16[8,128,128]{2,1,0:T(8,128)(2,1)S(1)}, u32[]{:S(2)}, u32[]{:S(2)}) collective-permute-start(bf16[8,128,128]{2,1,0:T(8,128)(2,1)S(1)} %add_convert_fusion.5), channel_id=1, source_target_pairs={{2,0},{3,1},{0,2},{1,3},{6,4},{7,5},{4,6},{5,7},{10,8},{11,9},{8,1... | collective-permute-start | bytes 786440 | tf_op jit(solution)/shard_map/ppermute | solution.py:165
  35.2 8.8 %collective-permute-start.4 = (bf16[8,128,128]{2,1,0:T(8,128)(2,1)S(1)}, bf16[8,128,128]{2,1,0:T(8,128)(2,1)S(1)}, u32[]{:S(2)}, u32[]{:S(2)}) collective-permute-start(bf16[8,128,128]{2,1,0:T(8,128)(2,1)S(1)} %collective-permute-done.2.rest_1_), channel_id=1, source_target_pairs={{1,0},{0,1},{3,2},{2,3},{5,4},{4,5},{7,6},{6,7},{9,8},{8,9},{11,10... | collective-permute-start | bytes 786440 | tf_op jit(solution)/shard_map/ppermute | solution.py:165
  36.5 7.8 %collective-permute-start.5 = (bf16[8,128,128]{2,1,0:T(8,128)(2,1)S(1)}, bf16[8,128,128]{2,1,0:T(8,128)(2,1)S(1)}, u32[]{:S(2)}, u32[]{:S(2)}) collective-permute-start(bf16[8,128,128]{2,1,0:T(8,128)(2,1)S(1)} %get-tuple-element.132), channel_id=1, source_target_pairs={{4,0},{5,1},{6,2},{7,3},{0,4},{1,5},{2,6},{3,7},{12,8},{13,9},{14,... | collective-permute-start | bytes 786440 | tf_op jit(solution)/shard_map/ppermute | solution.py:165
  36.7 7.6 %collective-permute-start.6 = (bf16[8,128,128]{2,1,0:T(8,128)(2,1)S(1)}, bf16[8,128,128]{2,1,0:T(8,128)(2,1)S(1)}, u32[]{:S(2)}, u32[]{:S(2)}) collective-permute-start(bf16[8,128,128]{2,1,0:T(8,128)(2,1)S(1)} %get-tuple-element.134), channel_id=1, source_target_pairs={{2,0},{3,1},{0,2},{1,3},{6,4},{7,5},{4,6},{5,7},{10,8},{11,9},{8,1... | collective-permute-start | bytes 786440 | tf_op jit(solution)/shard_map/ppermute | solution.py:165
  43.9 11.1 %copy-start.11 = (bf16[8,128,128]{2,1,0:T(8,128)(2,1)}, bf16[8,128,128]{2,1,0:T(8,128)(2,1)S(1)}, u32[]{:S(2)}) copy-start(bf16[8,128,128]{2,1,0:T(8,128)(2,1)S(1)} %collective-permute-done.4.rest_2_) | copy-start | bytes 786436
  44.3 10.7 %copy-start.5 = (bf16[8,128,128]{2,1,0:T(8,128)(2,1)}, bf16[8,128,128]{2,1,0:T(8,128)(2,1)S(1)}, u32[]{:S(2)}) copy-start(bf16[8,128,128]{2,1,0:T(8,128)(2,1)S(1)} %collective-permute-done.5.rest_3_) | copy-start | bytes 786436
  44.3 10.7 %copy-start.3 = (bf16[8,128,128]{2,1,0:T(8,128)(2,1)}, bf16[8,128,128]{2,1,0:T(8,128)(2,1)S(1)}, u32[]{:S(2)}) copy-start(bf16[8,128,128]{2,1,0:T(8,128)(2,1)S(1)} %collective-permute-done.6.rest_1_) | copy-start | bytes 786436
  44.5 10.6 %collective-permute-start.10 = (bf16[8,128,128]{2,1,0:T(8,128)(2,1)S(1)}, bf16[8,128,128]{2,1,0:T(8,128)(2,1)S(1)}, u32[]{:S(2)}, u32[]{:S(2)}) collective-permute-start(bf16[8,128,128]{2,1,0:T(8,128)(2,1)S(1)} %add_convert_fusion.1), channel_id=1, source_target_pairs={{4,0},{5,1},{6,2},{7,3},{0,4},{1,5},{2,6},{3,7},{12,8},{13,9},{14,... | collective-permute-start | bytes 786440 | tf_op jit(solution)/shard_map/ppermute | solution.py:165
  45.7 9.3 %collective-permute-start.7 = (bf16[8,128,128]{2,1,0:T(8,128)(2,1)S(1)}, bf16[8,128,128]{2,1,0:T(8,128)(2,1)S(1)}, u32[]{:S(2)}, u32[]{:S(2)}) collective-permute-start(bf16[8,128,128]{2,1,0:T(8,128)(2,1)S(1)} %collective-permute-done.5.rest_3_), channel_id=1, source_target_pairs={{1,0},{0,1},{3,2},{2,3},{5,4},{4,5},{7,6},{6,7},{9,8},{8,9},{11,10... | collective-permute-start | bytes 786440 | tf_op jit(solution)/shard_map/ppermute | solution.py:165
  47.2 16.6 %collective-permute-start.8 = (bf16[8,128,128]{2,1,0:T(8,128)(2,1)S(1)}, bf16[8,128,128]{2,1,0:T(8,128)(2,1)S(1)}, u32[]{:S(2)}, u32[]{:S(2)}) collective-permute-start(bf16[8,128,128]{2,1,0:T(8,128)(2,1)S(1)} %add_convert_fusion.2), channel_id=1, source_target_pairs={{0,8},{1,9},{2,10},{3,11},{4,12},{5,13},{6,14},{7,15},{16,24},{17,... | collective-permute-start | bytes 786440 | tf_op jit(solution)/shard_map/ppermute | solution.py:165
  48.5 15.3 %collective-permute-start.9 = (bf16[8,128,128]{2,1,0:T(8,128)(2,1)S(1)}, bf16[8,128,128]{2,1,0:T(8,128)(2,1)S(1)}, u32[]{:S(2)}, u32[]{:S(2)}) collective-permute-start(bf16[8,128,128]{2,1,0:T(8,128)(2,1)S(1)} %collective-permute-done.6.rest_1_), channel_id=1, source_target_pairs={{1,0},{0,1},{3,2},{2,3},{5,4},{4,5},{7,6},{6,7},{9,8},{8,9},{11,10... | collective-permute-start | bytes 786440 | tf_op jit(solution)/shard_map/ppermute | solution.py:165
  55.1 19.3 %copy-start.4 = (bf16[8,128,128]{2,1,0:T(8,128)(2,1)}, bf16[8,128,128]{2,1,0:T(8,128)(2,1)S(1)}, u32[]{:S(2)}) copy-start(bf16[8,128,128]{2,1,0:T(8,128)(2,1)S(1)} %collective-permute-done.10.rest_3_) | copy-start | bytes 786436
  55.1 19.2 %copy-start.12 = (bf16[8,128,128]{2,1,0:T(8,128)(2,1)}, bf16[8,128,128]{2,1,0:T(8,128)(2,1)S(1)}, u32[]{:S(2)}) copy-start(bf16[8,128,128]{2,1,0:T(8,128)(2,1)S(1)} %collective-permute-done.7.rest_4_) | copy-start | bytes 786436
  63.8 10.5 %copy-start.13 = (bf16[8,128,128]{2,1,0:T(8,128)(2,1)}, bf16[8,128,128]{2,1,0:T(8,128)(2,1)S(1)}, u32[]{:S(2)}) copy-start(bf16[8,128,128]{2,1,0:T(8,128)(2,1)S(1)} %collective-permute-done.8.rest_5_) | copy-start | bytes 786436
  63.8 10.5 %copy-start.7 = (bf16[8,128,128]{2,1,0:T(8,128)(2,1)}, bf16[8,128,128]{2,1,0:T(8,128)(2,1)S(1)}, u32[]{:S(2)}) copy-start(bf16[8,128,128]{2,1,0:T(8,128)(2,1)S(1)} %collective-permute-done.9.rest_2_) | copy-start | bytes 786436
  63.9 10.4 %collective-permute-start.11 = (bf16[8,128,128]{2,1,0:T(8,128)(2,1)S(1)}, bf16[8,128,128]{2,1,0:T(8,128)(2,1)S(1)}, u32[]{:S(2)}, u32[]{:S(2)}) collective-permute-start(bf16[8,128,128]{2,1,0:T(8,128)(2,1)S(1)} %collective-permute-done.8.rest_5_), channel_id=1, source_target_pairs={{9,8},{8,9},{11,10},{10,11},{13,12},{12,13},{15,14},{14,15},{25,24... | collective-permute-start | bytes 786440 | tf_op jit(solution)/shard_map/ppermute | solution.py:165
  66.3 8.1 %collective-permute-start.12 = (bf16[8,128,128]{2,1,0:T(8,128)(2,1)S(1)}, bf16[8,128,128]{2,1,0:T(8,128)(2,1)S(1)}, u32[]{:S(2)}, u32[]{:S(2)}) collective-permute-start(bf16[8,128,128]{2,1,0:T(8,128)(2,1)S(1)} %collective-permute-done.10.rest_3_), channel_id=1, source_target_pairs={{1,0},{0,1},{3,2},{2,3},{5,4},{4,5},{7,6},{6,7},{9,8},{8,9},{11,10... | collective-permute-start | bytes 786440 | tf_op jit(solution)/shard_map/ppermute | solution.py:165
  66.4 10.3 %collective-permute-start.13 = (bf16[8,128,128]{2,1,0:T(8,128)(2,1)S(1)}, bf16[8,128,128]{2,1,0:T(8,128)(2,1)S(1)}, u32[]{:S(2)}, u32[]{:S(2)}) collective-permute-start(bf16[8,128,128]{2,1,0:T(8,128)(2,1)S(1)} %add_convert_fusion), channel_id=1, source_target_pairs={{0,8},{1,9},{2,10},{3,11},{4,12},{5,13},{6,14},{7,15},{16,24},{17,... | collective-permute-start | bytes 786440 | tf_op jit(solution)/shard_map/ppermute | solution.py:165
  74.4 14.1 %copy-start.8 = (bf16[8,128,128]{2,1,0:T(8,128)(2,1)}, bf16[8,128,128]{2,1,0:T(8,128)(2,1)S(1)}, u32[]{:S(2)}) copy-start(bf16[8,128,128]{2,1,0:T(8,128)(2,1)S(1)} %collective-permute-done.12.rest_4_) | copy-start | bytes 786436
  76.7 11.8 %copy-start.9 = (bf16[8,128,128]{2,1,0:T(8,128)(2,1)}, bf16[8,128,128]{2,1,0:T(8,128)(2,1)S(1)}, u32[]{:S(2)}) copy-start(bf16[8,128,128]{2,1,0:T(8,128)(2,1)S(1)} %collective-permute-done.13.rest_5_) | copy-start | bytes 786436
  76.7 11.8 %collective-permute-start.14 = (bf16[8,128,128]{2,1,0:T(8,128)(2,1)S(1)}, bf16[8,128,128]{2,1,0:T(8,128)(2,1)S(1)}, u32[]{:S(2)}, u32[]{:S(2)}) collective-permute-start(bf16[8,128,128]{2,1,0:T(8,128)(2,1)S(1)} %collective-permute-done.13.rest_5_), channel_id=1, source_target_pairs={{9,8},{8,9},{11,10},{10,11},{13,12},{12,13},{15,14},{14,15},{25,24... | collective-permute-start | bytes 786440 | tf_op jit(solution)/shard_map/ppermute | solution.py:165
  (8 other events, 48.5 us)

commit v6 on v5

--- a/solution.py
+++ b/solution.py
@@ -12,15 +12,27 @@
 NT = (((1,), (1,)), ((), ()))
 
 
-def convolve(data_ref, rim_ref, taps_ref, held):
+def convolve(data_ref, rim_ref, taps_ref, scratch):
+    held, older = scratch.at[0], scratch.at[1]
     rows = data_ref.shape[1]
     taps = taps_ref.shape[1]
     held[PAD - taps + 1 : PAD, :] = rim_ref[0].astype(jnp.float32)
     held[PAD : PAD + rows, :] = data_ref[0].astype(jnp.float32)
-    total = taps_ref[0, 0:1, :] * held[PAD - taps + 1 : PAD - taps + 1 + rows, :]
-    for tap in range(1, taps):
-        first = PAD - taps + 1 + tap
-        total = total + taps_ref[0, tap : tap + 1, :] * held[first : first + rows, :]
+    weight = [taps_ref[0, tap : tap + 1, :] for tap in range(taps)]
+    last = slice(PAD, PAD + rows)
+    before = held[PAD - 1 : PAD - 1 + rows, :]
+    if taps == 4:
+        older[PAD - 2 : PAD, :] = (
+            weight[1] * held[PAD - 2 : PAD, :] + weight[0] * held[PAD - 3 : PAD - 1, :]
+        )
+        older[last, :] = weight[1] * held[last, :] + weight[0] * before
+        total = older[PAD - 2 : PAD - 2 + rows, :]
+        total = total + weight[2] * before + weight[3] * held[last, :]
+    else:
+        total = weight[0] * held[PAD - taps + 1 : PAD - taps + 1 + rows, :]
+        for tap in range(1, taps):
+            first = PAD - taps + 1 + tap
+            total = total + weight[tap] * held[first : first + rows, :]
     return total.astype(jnp.bfloat16)
 
 
@@ -245,7 +257,7 @@
     def per_head(size, base=0):
         return pl.BlockSpec((group,) + size, lambda g: (g + base, 0, 0))
 
-    held = pltpu.VMEM((PAD + rows, lanes), jnp.float32)
+    held = pltpu.VMEM((2, PAD + rows, lanes), jnp.float32)
     limit = pltpu.CompilerParams(vmem_limit_bytes=56 * 2**20)
     half_width = width // halves
 

time: 97.8 us -> 96.1 us (0.983)
  Pallas kernels: 60.2 us -> 58 us
    pallas_call x2, Pallas kernels: 18.2 us -> 16.5 us  [states(): pl.pallas_call(functools.partial(state_kernel, dim), grid=(steps,), in_sp...]
  transfers between devices with their start and end apart: 15 -> 15, of which waited for: 4 -> 4; matrix products, arithmetic and copies ran while one was open for 3% -> 4% of each run, Pallas kernels for 44% -> 44%
where the time goes in v6:
time: 96.1 us; the launch traced here: 95.6 us
  Pallas kernels  58 us (60%)
  starting transfers between devices  18.4 us (19%)
  waiting for transfers between devices  12.8 us (13%)
  other arithmetic  3.73 us (4%)
  local copies, waits for them, and re-layouts  2.44 us (3%)
    pallas_call x4, Pallas kernels, inside(): return list(call(projected, rim, conv_weight, keys, values_t, lam, *done))  25.3 us
    pallas_call x2, Pallas kernels, states(): pl.pallas_call(functools.partial(state_kernel, dim), grid=(steps,), in_sp...  16.5 us
    pallas_call x2, Pallas kernels, mix(): pl.pallas_call(kernel, grid_spec=pltpu.PrefetchScalarGridSpec(num_scalar_...  16.2 us
    ppermute x14, starting transfers between devices, exchange(): lax.ppermute(value, 'ctx', [(to ^ away, to) for to in self.takers(bit)])  14.7 us
    ppermute x14, waiting for transfers between devices, exchange(): lax.ppermute(value, 'ctx', [(to ^ away, to) for to in self.takers(bit)])  12.8 us
    ppermute x1, starting transfers between devices, on_device(): lax.ppermute(projected[:, rows - taps + 1:, :], 'ctx', [(c, c + 1) for c...  3.71 us
    div x1, other arithmetic, on_device(): (level_codes * scale[:, None, None]).transpose(1, 0, 2).astype(jnp.float32)  2.76 us
  transfers between devices with their start and end apart: 15, of which 4 were waited for; matrix products, arithmetic and copies ran while one was open for 4% of the time, Pallas kernels for 44%

profile of v6, /device:TPU:25, one launch (start us, length us, event | category | flops | bytes accessed | tf_op | source)
XLA Modules:
  0.0 95.6 jit_solution(3538409984759971767)
XLA Ops:
  0.0 1.0 %slice.3 = bf16[3,3,4096]{2,1,0:T(4,128)(2,1)S(1)} slice(bf16[3,512,4096]{2,1,0:T(8,128)(2,1)} %q_in.3), slice={[0:3], [509:512], [0:4096]} | slice | bytes 147456 | tf_op jit(solution)/shard_map/slice | solution.py:237
  1.0 3.7 %collective-permute-start = (bf16[3,3,4096]{2,1,0:T(4,128)(2,1)S(1)}, bf16[3,3,4096]{2,1,0:T(4,128)(2,1)S(1)}, u32[]{:S(2)}, u32[]{:S(2)}) collective-permute-start(bf16[3,3,4096]{2,1,0:T(4,128)(2,1)S(1)} %slice.3), channel_id=1, source_target_pairs={{0,1},{1,2},{2,3},{3,4},{4,5},{5,6},{6,7},{7,8},{8,9},{9,10},{10,1... | collective-permute-start | bytes 221192 | tf_op jit(solution)/shard_map/ppermute | solution.py:236
  4.8 2.8 %fusion.2.refs_5_.lam_in = f32[32,14,512]{2,1,0:T(8,128)} fusion(s32[14,32,512]{2,1,0:T(8,128)} %param.6, s32[14]{0:T(128)S(1)} %concatenate.3), kind=kLoop, calls=%fused_computation.3 | loop fusion | flops 688128 | bytes 1835064 | tf_op jit(solution)/shard_map/div | solution.py:241
  8.2 8.3 %states.2 = (bf16[512,2048]{1,0:T(8,128)(2,1)}, bf16[2048,512]{1,0:T(8,128)(2,1)}, bf16[16,128,128]{2,1,0:T(8,128)(2,1)}) custom-call(bf16[3,512,4096]{2,1,0:T(8,128)(2,1)} %q_in.3, bf16[3,512,4096]{2,1,0:T(8,128)(2,1)} %q_in.3, bf16[3,3,4096]{2,1,0:T(4,128)(2,1)} %copy-done, bf16[3,3,4096]{2,1,0:T(4,128)(2,1)} %copy-done, f32[3,4,4096]{2,1,0:T(4,128)} %q_taps.3, ...), custom_call_target="tpu_custom_call" | custom-call | flops 268435456 | bytes 8388608 | tf_op jit(solution)/shard_map/states/pallas_call | solution.py:266
  16.5 0.9 collective-permute-start.1
  17.4 8.2 %states.3 = (bf16[512,2048]{1,0:T(8,128)(2,1)}, bf16[2048,512]{1,0:T(8,128)(2,1)}, bf16[16,128,128]{2,1,0:T(8,128)(2,1)}) custom-call(bf16[3,512,4096]{2,1,0:T(8,128)(2,1)} %q_in.3, bf16[3,512,4096]{2,1,0:T(8,128)(2,1)} %q_in.3, bf16[3,3,4096]{2,1,0:T(4,128)(2,1)} %copy-done, bf16[3,3,4096]{2,1,0:T(4,128)(2,1)} %copy-done, f32[3,4,4096]{2,1,0:T(4,128)} %q_taps.3, ...), custom_call_target="tpu_custom_call" | custom-call | flops 268435456 | bytes 8388608 | tf_op jit(solution)/shard_map/states/pallas_call | solution.py:266
  26.2 6.3 %inside.4 = (bf16[512,2048]{1,0:T(8,128)(2,1)}, f32[2048,512]{1,0:T(8,128)}) custom-call(bf16[3,512,4096]{2,1,0:T(8,128)(2,1)} %q_in.3, bf16[3,3,4096]{2,1,0:T(4,128)(2,1)} %copy-done, f32[3,4,4096]{2,1,0:T(4,128)} %q_taps.3, bf16[512,2048]{1,0:T(8,128)(2,1)} %get-tuple-element.112.refs_3_.k_in, bf16[2048,512]{1,0:T(8,128)(2,1)} %get-tuple-element.113.refs_4_.vt_in, ...), custom_call_target="tpu_custom_call" | custom-call | flops 2147483648 | bytes 5242880 | tf_op jit(solution)/shard_map/inside/pallas_call | solution.py:310
  32.6 0.7 collective-permute-done.2.rest_1_
  33.5 1.4 %collective-permute-start.4 = (bf16[8,128,128]{2,1,0:T(8,128)(2,1)S(1)}, bf16[8,128,128]{2,1,0:T(8,128)(2,1)S(1)}, u32[]{:S(2)}, u32[]{:S(2)}) collective-permute-start(bf16[8,128,128]{2,1,0:T(8,128)(2,1)S(1)} %collective-permute-done.2.rest_1_), channel_id=1, source_target_pairs={{1,0},{0,1},{3,2},{2,3},{5,4},{4,5},{7,6},{6,7},{9,8},{8,9},{11,10... | collective-permute-start | bytes 786440 | tf_op jit(solution)/shard_map/ppermute | solution.py:177
  35.0 0.7 collective-permute-start.6
  35.7 6.3 %inside.5 = (bf16[512,2048]{1,0:T(8,128)(2,1)}, f32[2048,512]{1,0:T(8,128)}) custom-call(bf16[3,512,4096]{2,1,0:T(8,128)(2,1)} %q_in.3, bf16[3,3,4096]{2,1,0:T(4,128)(2,1)} %copy-done, f32[3,4,4096]{2,1,0:T(4,128)} %q_taps.3, bf16[512,2048]{1,0:T(8,128)(2,1)} %get-tuple-element.112.refs_3_.k_in, ...), custom_call_target="tpu_custom_call", output_to_operand_aliasing={{0}: (6, {}), {1}: (7, {})} | custom-call | flops 2147483648 | bytes 5242880 | tf_op jit(solution)/shard_map/inside/pallas_call | solution.py:310
  42.8 1.2 %collective-permute-start.10 = (bf16[8,128,128]{2,1,0:T(8,128)(2,1)S(1)}, bf16[8,128,128]{2,1,0:T(8,128)(2,1)S(1)}, u32[]{:S(2)}, u32[]{:S(2)}) collective-permute-start(bf16[8,128,128]{2,1,0:T(8,128)(2,1)S(1)} %add_convert_fusion.1), channel_id=1, source_target_pairs={{4,0},{5,1},{6,2},{7,3},{0,4},{1,5},{2,6},{3,7},{12,8},{13,9},{14,... | collective-permute-start | bytes 786440 | tf_op jit(solution)/shard_map/ppermute | solution.py:177
  44.0 1.5 %collective-permute-start.7 = (bf16[8,128,128]{2,1,0:T(8,128)(2,1)S(1)}, bf16[8,128,128]{2,1,0:T(8,128)(2,1)S(1)}, u32[]{:S(2)}, u32[]{:S(2)}) collective-permute-start(bf16[8,128,128]{2,1,0:T(8,128)(2,1)S(1)} %collective-permute-done.5.rest_3_), channel_id=1, source_target_pairs={{1,0},{0,1},{3,2},{2,3},{5,4},{4,5},{7,6},{6,7},{9,8},{8,9},{11,10... | collective-permute-start | bytes 786440 | tf_op jit(solution)/shard_map/ppermute | solution.py:177
  45.5 1.3 %collective-permute-start.8 = (bf16[8,128,128]{2,1,0:T(8,128)(2,1)S(1)}, bf16[8,128,128]{2,1,0:T(8,128)(2,1)S(1)}, u32[]{:S(2)}, u32[]{:S(2)}) collective-permute-start(bf16[8,128,128]{2,1,0:T(8,128)(2,1)S(1)} %add_convert_fusion.2), channel_id=1, source_target_pairs={{0,8},{1,9},{2,10},{3,11},{4,12},{5,13},{6,14},{7,15},{16,24},{17,... | collective-permute-start | bytes 786440 | tf_op jit(solution)/shard_map/ppermute | solution.py:177
  46.9 6.3 %inside.6 = (bf16[512,2048]{1,0:T(8,128)(2,1)}, f32[2048,512]{1,0:T(8,128)}) custom-call(bf16[3,512,4096]{2,1,0:T(8,128)(2,1)} %q_in.3, bf16[3,3,4096]{2,1,0:T(4,128)(2,1)} %copy-done, f32[3,4,4096]{2,1,0:T(4,128)} %q_taps.3, bf16[512,2048]{1,0:T(8,128)(2,1)} %get-tuple-element.145.refs_3_.k_in, bf16[2048,512]{1,0:T(8,128)(2,1)} %get-tuple-element.146.refs_4_.vt_in, ...), custom_call_target="tpu_custom_call" | custom-call | flops 2147483648 | bytes 5242880 | tf_op jit(solution)/shard_map/inside/pallas_call | solution.py:310
  53.3 8.9 %collective-permute-done.8.rest_5_ = bf16[8,128,128]{2,1,0:T(8,128)(2,1)S(1)} collective-permute-done((bf16[8,128,128]{2,1,0:T(8,128)(2,1)S(1)}, bf16[8,128,128]{2,1,0:T(8,128)(2,1)S(1)}, u32[]{:S(2)}, u32[]{:S(2)}) %collective-permute-start.8) | collective-permute-done | bytes 262176 | tf_op jit(solution)/shard_map/ppermute | solution.py:177
  62.2 2.3 %collective-permute-start.11 = (bf16[8,128,128]{2,1,0:T(8,128)(2,1)S(1)}, bf16[8,128,128]{2,1,0:T(8,128)(2,1)S(1)}, u32[]{:S(2)}, u32[]{:S(2)}) collective-permute-start(bf16[8,128,128]{2,1,0:T(8,128)(2,1)S(1)} %collective-permute-done.8.rest_5_), channel_id=1, source_target_pairs={{9,8},{8,9},{11,10},{10,11},{13,12},{12,13},{15,14},{14,15},{25,24... | collective-permute-start | bytes 786440 | tf_op jit(solution)/shard_map/ppermute | solution.py:177
  64.7 1.3 %collective-permute-start.13 = (bf16[8,128,128]{2,1,0:T(8,128)(2,1)S(1)}, bf16[8,128,128]{2,1,0:T(8,128)(2,1)S(1)}, u32[]{:S(2)}, u32[]{:S(2)}) collective-permute-start(bf16[8,128,128]{2,1,0:T(8,128)(2,1)S(1)} %add_convert_fusion), channel_id=1, source_target_pairs={{0,8},{1,9},{2,10},{3,11},{4,12},{5,13},{6,14},{7,15},{16,24},{17,... | collective-permute-start | bytes 786440 | tf_op jit(solution)/shard_map/ppermute | solution.py:177
  66.0 6.3 %inside.7 = (bf16[512,2048]{1,0:T(8,128)(2,1)}, f32[2048,512]{1,0:T(8,128)}) custom-call(bf16[3,512,4096]{2,1,0:T(8,128)(2,1)} %q_in.3, bf16[3,3,4096]{2,1,0:T(4,128)(2,1)} %copy-done, f32[3,4,4096]{2,1,0:T(4,128)} %q_taps.3, bf16[512,2048]{1,0:T(8,128)(2,1)} %get-tuple-element.145.refs_3_.k_in, ...), custom_call_target="tpu_custom_call", output_to_operand_aliasing={{0}: (6, {}), {1}: (7, {})} | custom-call | flops 2147483648 | bytes 5242880 | tf_op jit(solution)/shard_map/inside/pallas_call | solution.py:310
  72.4 2.6 %collective-permute-done.13.rest_5_ = bf16[8,128,128]{2,1,0:T(8,128)(2,1)S(1)} collective-permute-done((bf16[8,128,128]{2,1,0:T(8,128)(2,1)S(1)}, bf16[8,128,128]{2,1,0:T(8,128)(2,1)S(1)}, u32[]{:S(2)}, u32[]{:S(2)}) %collective-permute-start.13) | collective-permute-done | bytes 262176 | tf_op jit(solution)/shard_map/ppermute | solution.py:177
  75.0 3.1 %collective-permute-start.14 = (bf16[8,128,128]{2,1,0:T(8,128)(2,1)S(1)}, bf16[8,128,128]{2,1,0:T(8,128)(2,1)S(1)}, u32[]{:S(2)}, u32[]{:S(2)}) collective-permute-start(bf16[8,128,128]{2,1,0:T(8,128)(2,1)S(1)} %collective-permute-done.13.rest_5_), channel_id=1, source_target_pairs={{9,8},{8,9},{11,10},{10,11},{13,12},{12,13},{15,14},{14,15},{25,24... | collective-permute-start | bytes 786440 | tf_op jit(solution)/shard_map/ppermute | solution.py:177
  78.7 8.1 %mix.2.rest_7_ = bf16[512,4096]{1,0:T(8,128)(2,1)} custom-call(s32[4]{0:T(128)} %iota_xor_fusion.order, bf16[512,2048]{1,0:T(8,128)(2,1)} %get-tuple-element.179.q_in, f32[2048,512]{1,0:T(8,128)} %get-tuple-element.180.in_in, f32[32,14,512]{2,1,0:T(8,128)} %fusion.2.refs_5_.lam_in, f32[1,4096]{1,0:T(1,128)} %bitcast.3, bf16[16,128,128]{2,1,0:T(8,128)(2,1)} %copy-done.2, ...), custom_call_target="tpu_custom_call" | custom-call | flops 1073741824 | bytes 8388608 | tf_op jit(solution)/shard_map/mix/pallas_call | solution.py:329
  86.8 0.7 copy-done.10
  87.5 8.1 %mix.3 = bf16[512,4096]{1,0:T(8,128)(2,1)} custom-call(s32[4]{0:T(128)} %iota_xor_fusion.order, bf16[512,2048]{1,0:T(8,128)(2,1)} %get-tuple-element.167.q_in, f32[2048,512]{1,0:T(8,128)} %get-tuple-element.168.in_in, f32[32,14,512]{2,1,0:T(8,128)} %fusion.2.refs_5_.lam_in, f32[1,4096]{1,0:T(1,128)} %bitcast.4, ...), custom_call_target="tpu_custom_call", output_to_operand_aliasing={{}: (12, {})} | custom-call | flops 1073741824 | bytes 8388608 | tf_op jit(solution)/shard_map/mix/pallas_call | solution.py:329
  (58 shorter events, 3.1 us)
Async XLA Ops:
  1.0 6.6 %collective-permute-start = (bf16[3,3,4096]{2,1,0:T(4,128)(2,1)S(1)}, bf16[3,3,4096]{2,1,0:T(4,128)(2,1)S(1)}, u32[]{:S(2)}, u32[]{:S(2)}) collective-permute-start(bf16[3,3,4096]{2,1,0:T(4,128)(2,1)S(1)} %slice.3), channel_id=1, source_target_pairs={{0,1},{1,2},{2,3},{3,4},{4,5},{5,6},{6,7},{7,8},{8,9},{9,10},{10,1... | collective-permute-start | bytes 221192 | tf_op jit(solution)/shard_map/ppermute | solution.py:236
  16.5 9.2 %collective-permute-start.1 = (bf16[16,128,128]{2,1,0:T(8,128)(2,1)}, bf16[16,128,128]{2,1,0:T(8,128)(2,1)S(1)}, u32[]{:S(2)}, u32[]{:S(2)}) collective-permute-start(bf16[16,128,128]{2,1,0:T(8,128)(2,1)} %get-tuple-element.105), channel_id=1, source_target_pairs={{1,0},{0,1},{3,2},{2,3},{5,4},{4,5},{7,6},{6,7},{9,8},{8,9},{11,10... | collective-permute-start | bytes 1572872 | tf_op jit(solution)/shard_map/ppermute | solution.py:177
  25.7 7.6 %collective-permute-start.3 = (bf16[16,128,128]{2,1,0:T(8,128)(2,1)}, bf16[16,128,128]{2,1,0:T(8,128)(2,1)S(1)}, u32[]{:S(2)}, u32[]{:S(2)}) collective-permute-start(bf16[16,128,128]{2,1,0:T(8,128)(2,1)} %get-tuple-element.118), channel_id=1, source_target_pairs={{1,0},{0,1},{3,2},{2,3},{5,4},{4,5},{7,6},{6,7},{9,8},{8,9},{11,10... | collective-permute-start | bytes 1572872 | tf_op jit(solution)/shard_map/ppermute | solution.py:177
  25.8 7.5 %collective-permute-start.2 = (bf16[8,128,128]{2,1,0:T(8,128)(2,1)S(1)}, bf16[8,128,128]{2,1,0:T(8,128)(2,1)S(1)}, u32[]{:S(2)}, u32[]{:S(2)}) collective-permute-start(bf16[8,128,128]{2,1,0:T(8,128)(2,1)S(1)} %add_convert_fusion.5), channel_id=1, source_target_pairs={{2,0},{3,1},{0,2},{1,3},{6,4},{7,5},{4,6},{5,7},{10,8},{11,9},{8,1... | collective-permute-start | bytes 786440 | tf_op jit(solution)/shard_map/ppermute | solution.py:177
  33.5 8.6 %collective-permute-start.4 = (bf16[8,128,128]{2,1,0:T(8,128)(2,1)S(1)}, bf16[8,128,128]{2,1,0:T(8,128)(2,1)S(1)}, u32[]{:S(2)}, u32[]{:S(2)}) collective-permute-start(bf16[8,128,128]{2,1,0:T(8,128)(2,1)S(1)} %collective-permute-done.2.rest_1_), channel_id=1, source_target_pairs={{1,0},{0,1},{3,2},{2,3},{5,4},{4,5},{7,6},{6,7},{9,8},{8,9},{11,10... | collective-permute-start | bytes 786440 | tf_op jit(solution)/shard_map/ppermute | solution.py:177
  34.8 7.8 %collective-permute-start.5 = (bf16[8,128,128]{2,1,0:T(8,128)(2,1)S(1)}, bf16[8,128,128]{2,1,0:T(8,128)(2,1)S(1)}, u32[]{:S(2)}, u32[]{:S(2)}) collective-permute-start(bf16[8,128,128]{2,1,0:T(8,128)(2,1)S(1)} %get-tuple-element.132), channel_id=1, source_target_pairs={{4,0},{5,1},{6,2},{7,3},{0,4},{1,5},{2,6},{3,7},{12,8},{13,9},{14,... | collective-permute-start | bytes 786440 | tf_op jit(solution)/shard_map/ppermute | solution.py:177
  35.0 7.6 %collective-permute-start.6 = (bf16[8,128,128]{2,1,0:T(8,128)(2,1)S(1)}, bf16[8,128,128]{2,1,0:T(8,128)(2,1)S(1)}, u32[]{:S(2)}, u32[]{:S(2)}) collective-permute-start(bf16[8,128,128]{2,1,0:T(8,128)(2,1)S(1)} %get-tuple-element.134), channel_id=1, source_target_pairs={{2,0},{3,1},{0,2},{1,3},{6,4},{7,5},{4,6},{5,7},{10,8},{11,9},{8,1... | collective-permute-start | bytes 786440 | tf_op jit(solution)/shard_map/ppermute | solution.py:177
  42.1 11.1 %copy-start.11 = (bf16[8,128,128]{2,1,0:T(8,128)(2,1)}, bf16[8,128,128]{2,1,0:T(8,128)(2,1)S(1)}, u32[]{:S(2)}) copy-start(bf16[8,128,128]{2,1,0:T(8,128)(2,1)S(1)} %collective-permute-done.4.rest_2_) | copy-start | bytes 786436
  42.6 10.6 %copy-start.5 = (bf16[8,128,128]{2,1,0:T(8,128)(2,1)}, bf16[8,128,128]{2,1,0:T(8,128)(2,1)S(1)}, u32[]{:S(2)}) copy-start(bf16[8,128,128]{2,1,0:T(8,128)(2,1)S(1)} %collective-permute-done.5.rest_3_) | copy-start | bytes 786436
  42.6 10.6 %copy-start.3 = (bf16[8,128,128]{2,1,0:T(8,128)(2,1)}, bf16[8,128,128]{2,1,0:T(8,128)(2,1)S(1)}, u32[]{:S(2)}) copy-start(bf16[8,128,128]{2,1,0:T(8,128)(2,1)S(1)} %collective-permute-done.6.rest_1_) | copy-start | bytes 786436
  42.8 10.4 %collective-permute-start.10 = (bf16[8,128,128]{2,1,0:T(8,128)(2,1)S(1)}, bf16[8,128,128]{2,1,0:T(8,128)(2,1)S(1)}, u32[]{:S(2)}, u32[]{:S(2)}) collective-permute-start(bf16[8,128,128]{2,1,0:T(8,128)(2,1)S(1)} %add_convert_fusion.1), channel_id=1, source_target_pairs={{4,0},{5,1},{6,2},{7,3},{0,4},{1,5},{2,6},{3,7},{12,8},{13,9},{14,... | collective-permute-start | bytes 786440 | tf_op jit(solution)/shard_map/ppermute | solution.py:177
  44.0 9.2 %collective-permute-start.7 = (bf16[8,128,128]{2,1,0:T(8,128)(2,1)S(1)}, bf16[8,128,128]{2,1,0:T(8,128)(2,1)S(1)}, u32[]{:S(2)}, u32[]{:S(2)}) collective-permute-start(bf16[8,128,128]{2,1,0:T(8,128)(2,1)S(1)} %collective-permute-done.5.rest_3_), channel_id=1, source_target_pairs={{1,0},{0,1},{3,2},{2,3},{5,4},{4,5},{7,6},{6,7},{9,8},{8,9},{11,10... | collective-permute-start | bytes 786440 | tf_op jit(solution)/shard_map/ppermute | solution.py:177
  45.5 16.6 %collective-permute-start.8 = (bf16[8,128,128]{2,1,0:T(8,128)(2,1)S(1)}, bf16[8,128,128]{2,1,0:T(8,128)(2,1)S(1)}, u32[]{:S(2)}, u32[]{:S(2)}) collective-permute-start(bf16[8,128,128]{2,1,0:T(8,128)(2,1)S(1)} %add_convert_fusion.2), channel_id=1, source_target_pairs={{0,8},{1,9},{2,10},{3,11},{4,12},{5,13},{6,14},{7,15},{16,24},{17,... | collective-permute-start | bytes 786440 | tf_op jit(solution)/shard_map/ppermute | solution.py:177
  46.8 15.3 %collective-permute-start.9 = (bf16[8,128,128]{2,1,0:T(8,128)(2,1)S(1)}, bf16[8,128,128]{2,1,0:T(8,128)(2,1)S(1)}, u32[]{:S(2)}, u32[]{:S(2)}) collective-permute-start(bf16[8,128,128]{2,1,0:T(8,128)(2,1)S(1)} %collective-permute-done.6.rest_1_), channel_id=1, source_target_pairs={{1,0},{0,1},{3,2},{2,3},{5,4},{4,5},{7,6},{6,7},{9,8},{8,9},{11,10... | collective-permute-start | bytes 786440 | tf_op jit(solution)/shard_map/ppermute | solution.py:177
  53.2 19.1 %copy-start.4 = (bf16[8,128,128]{2,1,0:T(8,128)(2,1)}, bf16[8,128,128]{2,1,0:T(8,128)(2,1)S(1)}, u32[]{:S(2)}) copy-start(bf16[8,128,128]{2,1,0:T(8,128)(2,1)S(1)} %collective-permute-done.10.rest_3_) | copy-start | bytes 786436
  53.2 19.1 %copy-start.12 = (bf16[8,128,128]{2,1,0:T(8,128)(2,1)}, bf16[8,128,128]{2,1,0:T(8,128)(2,1)S(1)}, u32[]{:S(2)}) copy-start(bf16[8,128,128]{2,1,0:T(8,128)(2,1)S(1)} %collective-permute-done.7.rest_4_) | copy-start | bytes 786436
  62.1 10.2 %copy-start.13 = (bf16[8,128,128]{2,1,0:T(8,128)(2,1)}, bf16[8,128,128]{2,1,0:T(8,128)(2,1)S(1)}, u32[]{:S(2)}) copy-start(bf16[8,128,128]{2,1,0:T(8,128)(2,1)S(1)} %collective-permute-done.8.rest_5_) | copy-start | bytes 786436
  62.1 10.2 %copy-start.7 = (bf16[8,128,128]{2,1,0:T(8,128)(2,1)}, bf16[8,128,128]{2,1,0:T(8,128)(2,1)S(1)}, u32[]{:S(2)}) copy-start(bf16[8,128,128]{2,1,0:T(8,128)(2,1)S(1)} %collective-permute-done.9.rest_2_) | copy-start | bytes 786436
  62.2 10.1 %collective-permute-start.11 = (bf16[8,128,128]{2,1,0:T(8,128)(2,1)S(1)}, bf16[8,128,128]{2,1,0:T(8,128)(2,1)S(1)}, u32[]{:S(2)}, u32[]{:S(2)}) collective-permute-start(bf16[8,128,128]{2,1,0:T(8,128)(2,1)S(1)} %collective-permute-done.8.rest_5_), channel_id=1, source_target_pairs={{9,8},{8,9},{11,10},{10,11},{13,12},{12,13},{15,14},{14,15},{25,24... | collective-permute-start | bytes 786440 | tf_op jit(solution)/shard_map/ppermute | solution.py:177
  64.6 7.8 %collective-permute-start.12 = (bf16[8,128,128]{2,1,0:T(8,128)(2,1)S(1)}, bf16[8,128,128]{2,1,0:T(8,128)(2,1)S(1)}, u32[]{:S(2)}, u32[]{:S(2)}) collective-permute-start(bf16[8,128,128]{2,1,0:T(8,128)(2,1)S(1)} %collective-permute-done.10.rest_3_), channel_id=1, source_target_pairs={{1,0},{0,1},{3,2},{2,3},{5,4},{4,5},{7,6},{6,7},{9,8},{8,9},{11,10... | collective-permute-start | bytes 786440 | tf_op jit(solution)/shard_map/ppermute | solution.py:177
  64.7 10.3 %collective-permute-start.13 = (bf16[8,128,128]{2,1,0:T(8,128)(2,1)S(1)}, bf16[8,128,128]{2,1,0:T(8,128)(2,1)S(1)}, u32[]{:S(2)}, u32[]{:S(2)}) collective-permute-start(bf16[8,128,128]{2,1,0:T(8,128)(2,1)S(1)} %add_convert_fusion), channel_id=1, source_target_pairs={{0,8},{1,9},{2,10},{3,11},{4,12},{5,13},{6,14},{7,15},{16,24},{17,... | collective-permute-start | bytes 786440 | tf_op jit(solution)/shard_map/ppermute | solution.py:177
  72.4 14.4 %copy-start.8 = (bf16[8,128,128]{2,1,0:T(8,128)(2,1)}, bf16[8,128,128]{2,1,0:T(8,128)(2,1)S(1)}, u32[]{:S(2)}) copy-start(bf16[8,128,128]{2,1,0:T(8,128)(2,1)S(1)} %collective-permute-done.12.rest_4_) | copy-start | bytes 786436
  75.0 11.8 %copy-start.9 = (bf16[8,128,128]{2,1,0:T(8,128)(2,1)}, bf16[8,128,128]{2,1,0:T(8,128)(2,1)S(1)}, u32[]{:S(2)}) copy-start(bf16[8,128,128]{2,1,0:T(8,128)(2,1)S(1)} %collective-permute-done.13.rest_5_) | copy-start | bytes 786436
  75.0 11.8 %collective-permute-start.14 = (bf16[8,128,128]{2,1,0:T(8,128)(2,1)S(1)}, bf16[8,128,128]{2,1,0:T(8,128)(2,1)S(1)}, u32[]{:S(2)}, u32[]{:S(2)}) collective-permute-start(bf16[8,128,128]{2,1,0:T(8,128)(2,1)S(1)} %collective-permute-done.13.rest_5_), channel_id=1, source_target_pairs={{9,8},{8,9},{11,10},{10,11},{13,12},{12,13},{15,14},{14,15},{25,24... | collective-permute-start | bytes 786440 | tf_op jit(solution)/shard_map/ppermute | solution.py:177
  (8 other events, 47.5 us)
